TPU v7x, 32 devices: a whole 2x2x4 slice. The times are simulated.
32 devices in a mesh: wide: 8 (over z, x), narrow: 4 (over y, core).
Axes of the slice: x: 2, y: 2, z: 4, core: 2. Of those that a mesh axis runs over, the one named last changes fastest.
Arguments:
- tokens: bfloat16 [20480, 1024], P(('wide', 'narrow')), may hold values from -6 to 6
- cotangent: bfloat16 [20480, 1024], P(('wide', 'narrow')), may hold values from -6 to 6
- flags: int32 [8], P('wide'), may hold values from 0 to 1
- norm_gain: bfloat16 [1024], replicated, may hold values from 0.5 to 1.5
- query_weight: bfloat16 [1024, 512], P(None, 'narrow'), may hold values from -0.1875 to 0.1875
- key_weight: bfloat16 [1024, 512], P(None, 'narrow'), may hold values from -0.1875 to 0.1875
- value_weight: bfloat16 [1024, 1024], P(None, 'narrow'), may hold values from -0.1875 to 0.1875
- swish_weight: bfloat16 [1024, 1024], P(None, 'narrow'), may hold values from -0.1875 to 0.1875
- rank_down: bfloat16 [1024, 16], replicated, may hold values from -0.1875 to 0.1875
- rank_up: bfloat16 [16, 512], replicated, may hold values from -0.375 to 0.375
- decay_bias: bfloat16 [512], replicated, may hold values from 0 to 10
- group_gain: bfloat16 [256], replicated, may hold values from 0.5 to 1.5
- output_weight: bfloat16 [1024, 1024], P('narrow'), may hold values from -0.1875 to 0.1875
- mlp_gain: bfloat16 [1024], replicated, may hold values from 0.5 to 1.5
- mlp_gate: bfloat16 [1024, 2816], P(None, 'narrow'), may hold values from -0.1875 to 0.1875
- mlp_up: bfloat16 [1024, 2816], P(None, 'narrow'), may hold values from -0.1875 to 0.1875
- mlp_down: bfloat16 [2816, 1024], P('narrow'), may hold values from -0.109375 to 0.109375
Outputs:
- result: bfloat16 [20480, 1024], P(('wide', 'narrow'))
- input_grad: float32 [20480, 1024], P(('wide', 'narrow'))
- norm_gain_grad: float32 [1024], replicated
- query_grad: float32 [1024, 512], P('wide', 'narrow')
- key_grad: float32 [1024, 512], P('wide', 'narrow')
- value_grad: float32 [1024, 1024], P('wide', 'narrow')
- swish_grad: float32 [1024, 1024], P('wide', 'narrow')
- rank_down_grad: float32 [1024, 16], replicated
- rank_up_grad: float32 [16, 512], replicated
- decay_bias_grad: float32 [512], replicated
- group_gain_grad: float32 [256], replicated
- output_grad: float32 [1024, 1024], P('narrow', 'wide')
- mlp_gain_grad: float32 [1024], replicated
- mlp_gate_grad: float32 [1024, 2816], P('wide', 'narrow')
- mlp_up_grad: float32 [1024, 2816], P('wide', 'narrow')
- mlp_down_grad: float32 [2816, 1024], P('narrow', 'wide')
All inputs are finite; a program needn't handle non-finite values.
Results may differ from a plain program's by a relative error of at most 0.03.
Values may be sent and summed in bfloat16 or wider, within the bound.
A program may use at most 192 MiB of HBM per device.

v0:
```python
import itertools

import jax
import jax.numpy as jnp
from jax import lax
from jax.experimental import pallas as pl
from jax.experimental.pallas import tpu as pltpu
from jax.sharding import PartitionSpec as P

NORM_EPS = 1e-06
GROUP_EPS = 1e-05
GATE_NORM = 16.0
HIGHEST_PREC = lax.Precision.HIGHEST
MESH = pl.DeviceIdType.MESH
CHUNK = 128
HALF = CHUNK // 2
BLOCK = 256
F32 = jnp.float32
BF16 = jnp.bfloat16


def dot(a, b):
    return lax.dot_general(a, b, (((1,), (0,)), ((), ())), preferred_element_type=F32)


def dot_nt(a, b):
    return lax.dot_general(a, b, (((1,), (1,)), ((), ())), preferred_element_type=F32)


def dot_tn(a, b):
    return lax.dot_general(a, b, (((0,), (0,)), ((), ())), preferred_element_type=F32)


def exact(a, b, dims):
    return lax.dot_general(
        a, b, (dims, ((), ())), precision=HIGHEST_PREC, preferred_element_type=F32
    )


def sds(shape, dtype):
    return jax.ShapeDtypeStruct(shape, dtype)


def params(mib=48):
    return pltpu.CompilerParams(vmem_limit_bytes=mib << 20)


def cost(flops, nbytes, trans=0):
    return pl.CostEstimate(flops=int(flops), bytes_accessed=int(nbytes), transcendentals=int(trans))


def whole(shape):
    return pl.BlockSpec(shape, lambda i: (0,) * len(shape), pipeline_mode=pl.Buffered(1))


def rows_spec(rows, cols):
    return pl.BlockSpec((rows, cols), lambda i: (i, 0))


def triangle(lower):
    r = lax.broadcasted_iota(jnp.int32, (CHUNK, CHUNK), 0)
    c = lax.broadcasted_iota(jnp.int32, (CHUNK, CHUNK), 1)
    return r >= c if lower else r <= c


def forward_head_kernel(
    x_ref, w_ref, rd_ref, ru_ref, bias_ref,
    q_ref, k_ref, v_ref, s_ref, cum_ref, dpre_ref, rank_ref, base_ref, reach_ref, sin_ref, off_ref,
    state_ref, mult_ref,
    st, off,
):
    i = pl.program_id(0)
    dk = q_ref.shape[1]
    dv = v_ref.shape[1]

    @pl.when(i == 0)
    def _():
        st[...] = jnp.zeros_like(st)
        off[...] = jnp.zeros_like(off)

    x = x_ref[...]
    proj = dot(x, w_ref[...])
    rank = dot(x, rd_ref[...])
    dpre = exact(rank, ru_ref[...], ((1,), (0,))) + bias_ref[...]
    dlog = jax.nn.log_sigmoid(dpre) * (1.0 / GATE_NORM)
    k_low = proj[:, :dk].astype(BF16)
    v_low = proj[:, dk : dk + dv].astype(BF16)
    q_low = proj[:, dk + dv : 2 * dk + dv].astype(BF16)
    q_ref[...] = q_low
    k_ref[...] = k_low
    v_ref[...] = v_low
    s_ref[...] = proj[:, 2 * dk + dv :]
    rank_ref[...] = rank
    dpre_ref[...] = dpre
    mask = triangle(True)
    ones = mask.astype(F32)
    scale = dk**-0.5
    for j in range(BLOCK // CHUNK):
        rows = slice(j * CHUNK, (j + 1) * CHUNK)
        cum = exact(ones, dlog[rows], ((1,), (0,)))
        mid = cum[HALF - 1 : HALF]
        end = cum[CHUNK - 1 :]
        qf = q_low[rows].astype(F32) * scale
        kf = k_low[rows].astype(F32)
        v = v_low[rows]
        qd = (qf * jnp.exp(cum - mid)).astype(BF16)
        kd = (kf * jnp.exp(mid - cum)).astype(BF16)
        qi = (qf * jnp.exp(cum)).astype(BF16)
        ke = (kf * jnp.exp(end - cum)).astype(BF16)
        scores = jnp.where(mask, dot_nt(qd, kd), 0.0).astype(BF16)
        state = st[...]
        state_low = state.astype(BF16)
        offset = off[...]
        base_ref[rows, :] = dot(scores, v) + dot_nt(qi, state_low)
        reach_ref[rows, :] = (qf * jnp.exp(cum + offset)).astype(BF16)
        cum_ref[rows, :] = cum
        sin_ref[j] = state_low
        off_ref[j] = offset
        st[...] = state * jnp.exp(end) + dot_tn(v, ke)
        off[...] = offset + end
    state_ref[...] = st[...]
    mult_ref[...] = jnp.exp(off[...])


def forward_head(x, w, rank_down, rank_cols, bias_cols, dk, dv):
    n, d = x.shape
    rank = rank_down.shape[1]
    per = BLOCK // CHUNK
    return pl.pallas_call(
        forward_head_kernel,
        name="forward_head",
        grid=(n // BLOCK,),
        in_specs=[
            rows_spec(BLOCK, d), whole(w.shape), whole(rank_down.shape), whole(rank_cols.shape), whole(bias_cols.shape),
        ],
        out_specs=[
            rows_spec(BLOCK, dk), rows_spec(BLOCK, dk), rows_spec(BLOCK, dv), rows_spec(BLOCK, dv),
            rows_spec(BLOCK, dk), rows_spec(BLOCK, dk), rows_spec(BLOCK, rank), rows_spec(BLOCK, dv), rows_spec(BLOCK, dk),
            pl.BlockSpec((per, dv, dk), lambda i: (i, 0, 0)), pl.BlockSpec((per, 1, dk), lambda i: (i, 0, 0)),
            whole((dv, dk)), whole((1, dk)),
        ],
        out_shape=[
            sds((n, dk), BF16), sds((n, dk), BF16), sds((n, dv), BF16), sds((n, dv), F32),
            sds((n, dk), F32), sds((n, dk), F32), sds((n, rank), F32), sds((n, dv), F32), sds((n, dk), BF16),
            sds((n // CHUNK, dv, dk), BF16), sds((n // CHUNK, 1, dk), F32),
            sds((dv, dk), F32), sds((1, dk), F32),
        ],
        scratch_shapes=[pltpu.VMEM((dv, dk), F32), pltpu.VMEM((1, dk), F32)],
        compiler_params=params(),
        cost_estimate=cost(2 * n * d * (2 * dk + 2 * dv) * 1.5, n * d * 2 + n * 4000, n * dk * 6),
    )(x, w, rank_down, rank_cols, bias_cols)


def gate_out_kernel(b0, b1, r0, r1, s0, s1, e0, e1, gain_ref, w0, w1, m0, m1, g0, g1, out_ref):
    total = None
    gain = gain_ref[...]
    for b, r, s, e, w, m, g in ((b0, r0, s0, e0, w0, m0, g0), (b1, r1, s1, e1, w1, m1, g1)):
        mixed = b[...] + dot_nt(r[...], e[...])
        inv = lax.rsqrt(jnp.mean(mixed * mixed, axis=-1, keepdims=True) + GROUP_EPS)
        sw = s[...]
        gated = (mixed * inv * gain * (sw * jax.nn.sigmoid(sw))).astype(BF16)
        m[...] = mixed
        g[...] = gated
        part = dot(gated, w[...])
        total = part if total is None else total + part
    out_ref[...] = total.astype(BF16)


def gate_out(bases, reaches, swishes, enters, gain, weights):
    n, dv = bases[0].shape
    dk = reaches[0].shape[1]
    d = weights[0].shape[1]
    row = rows_spec(BLOCK, dv)
    return pl.pallas_call(
        gate_out_kernel,
        name="gate_out",
        grid=(n // BLOCK,),
        in_specs=[row, row, rows_spec(BLOCK, dk), rows_spec(BLOCK, dk), row, row]
        + [whole((dv, dk))] * 2 + [whole((1, dv))] + [whole((dv, d))] * 2,
        out_specs=[row, row, row, row, rows_spec(BLOCK, d)],
        out_shape=[sds((n, dv), F32)] * 2 + [sds((n, dv), BF16)] * 2 + [sds((n, d), BF16)],
        compiler_params=params(),
        cost_estimate=cost(2 * n * dv * (d + dk) * 2, n * (dv * 28 + d * 2), n * dv * 2),
    )(*bases, *reaches, *swishes, *enters, gain, *weights)


def tile_of(step):
    return jnp.where((step == 5) | (step == 6), 11 - step, step)


def mlp_phase_kernel(
    mid_h, c0_h, c1_h, c2_h, c3_h, wg_h, wu_h, wd_h, gain_ref,
    gmid_h, gm_h, part_ref, gg_h, gu_h, gd_h, near_h, far_h,
    mid, xs, cs, wg, wu, wd, hs, ggs, gus, gn, rc, rd, ac, ry, dn, dnr, gr_st, gmb,
    load_sem, send_sem, recv_sem, gr_sem, out_sem,
):
    tile = xs.shape[1]
    rows = 2 * tile
    d = xs.shape[2]
    ff = hs.shape[2]
    wide, place = lax.axis_index("wide"), lax.axis_index("narrow")
    core = place % 2
    by_core = (wide, place + 1 - 2 * core)
    by_row = (wide, (place + 2) % 4)

    loads = [pltpu.make_async_copy(mid_h, mid, load_sem.at[0])]
    for i, (src, dst) in enumerate(((wg_h, wg), (wu_h, wu), (wd_h, wd))):
        loads.append(pltpu.make_async_copy(src, dst, load_sem.at[1 + i]))
    for i, src in enumerate((c0_h, c1_h, c2_h, c3_h)):
        for j in range(2):
            loads.append(
                pltpu.make_async_copy(src.at[pl.ds(j * tile, tile)], cs.at[2 * i + j], load_sem.at[4 + 2 * i + j])
            )
    for load in loads:
        load.start()

    barrier = pltpu.get_barrier_semaphore()
    for other in (by_core, by_row):
        pl.semaphore_signal(barrier, 1, device_id=other, device_id_type=MESH)
    pl.semaphore_wait(barrier, 2)

    def remote(src, dst, index, target):
        return pltpu.make_async_remote_copy(
            src, dst, send_sem.at[index], recv_sem.at[index], device_id=target, device_id_type=MESH
        )

    x_row = [remote(xs.at[j], xs.at[4 + j], j, by_row) for j in range(2)]
    x_core = [remote(xs.at[j], xs.at[2 + j], 2 + j, by_core) for j in range(2)]
    x_both = [remote(xs.at[4 + j], xs.at[6 + j], 4 + j, by_core) for j in range(2)]
    g_near = [remote(gn.at[2 + j], rc.at[j], 6 + j, by_core) for j in range(2)]
    g_far = [remote(gn.at[6 + j], rd.at[j], 8 + j, by_core) for j in range(2)]
    g_row = [remote(ac.at[j], ry.at[j], 10 + j, by_row) for j in range(2)]
    d_in = [remote(dn.at[(2, 3, 6, 7)[j]], dnr.at[j], 14 + j, by_core) for j in range(4)]
    gain = gain_ref[...]

    loads[0].wait()
    for j in range(2):
        m = mid[pl.ds(j * tile, tile), :]
        inv = lax.rsqrt(jnp.mean(m * m, axis=-1, keepdims=True) + NORM_EPS)
        xs[j] = (m * inv * gain).astype(BF16)
        x_row[j].start()
        x_core[j].start()
    for load in loads[1:]:
        load.wait()

    def step(s, _):
        t = tile_of(s)

        @pl.when(s == 2)
        def _():
            x_core[0].wait_recv()

        @pl.when(s == 3)
        def _():
            x_core[1].wait_recv()

        for j in range(2):

            @pl.when(s == 4 + 2 * j)
            def _():
                x_row[j].wait_recv()
                x_both[j].start()

            @pl.when(s == 5 + 2 * j)
            def _():
                x_both[j].wait_recv()

        x = xs[t]
        gate = dot_nt(x, wg[...])
        up = dot_nt(x, wu[...])
        gh = dot_nt(cs[t], wd[...])
        sig = jax.nn.sigmoid(gate)
        act = gate * sig
        hidden = (act * up).astype(BF16)
        g_up = (gh * act).astype(BF16)
        g_gate = (gh * up * sig * (1.0 + gate * (1.0 - sig))).astype(BF16)
        hs[t] = hidden
        ggs[t] = g_gate
        gus[t] = g_up
        gn[t] = (dot(g_gate, wg[...]) + dot(g_up, wu[...])).astype(BF16)

        for j in range(2):

            @pl.when(s == 2 + j)
            def _():
                g_near[j].start()

            @pl.when(s == 5 + 2 * j)
            def _():
                g_far[j].start()

        dn[t] = dot(hidden, wd[...]).astype(BF16)

        for j in range(2):

            @pl.when(s == 5 + 2 * j)
            def _():
                g_far[j].wait_recv()
                ac[j] = (gn[4 + j].astype(F32) + rd[j].astype(F32)).astype(BF16)
                g_row[j].start()

        return 0

    lax.fori_loop(0, 8, step, 0)
    for copy in d_in:
        copy.start()

    blk = gr_st.shape[2]
    count = d // blk

    def gr_copies(slot, j):
        at = pl.ds(pl.multiple_of(j * blk, blk), blk)
        return [
            pltpu.make_async_copy(gr_st.at[slot, i], dst.at[at], gr_sem.at[slot, i])
            for i, dst in enumerate((gg_h, gu_h, gd_h))
        ]

    def weights(j, _):
        slot = j % 2
        cols = pl.ds(pl.multiple_of(j * blk, blk), blk)

        @pl.when(j >= 2)
        def _():
            for copy in gr_copies(slot, j - 2):
                copy.wait()

        for i, lefts, rights in ((0, xs, ggs), (1, xs, gus), (2, cs, hs)):
            acc = dot_tn(lefts[0, :, cols], rights[0])
            for t in range(1, 8):
                acc = acc + dot_tn(lefts[t, :, cols], rights[t])
            gr_st[slot, i] = acc.astype(BF16)
        for copy in gr_copies(slot, j):
            copy.start()
        return 0

    lax.fori_loop(0, count, weights, 0)
    for j in (count - 2, count - 1):
        for copy in gr_copies(j % 2, j):
            copy.wait()
    sums = []
    for j in range(2):
        d_in[j].wait_recv()
        d_in[2 + j].wait_recv()
        for at, extra, out in ((j, j, near_h), (4 + j, 2 + j, far_h)):
            dn[at] = (dn[at].astype(F32) + dnr[extra].astype(F32)).astype(BF16)
            sums.append(pltpu.make_async_copy(dn.at[at], out.at[pl.ds(j * tile, tile)], out_sem.at[3 + len(sums)]))
            sums[-1].start()

    part = jnp.zeros((1, d), F32)
    gm_out = []
    for j in range(2):
        at = pl.ds(j * tile, tile)
        g_near[j].wait_recv()
        g_row[j].wait_recv()
        grad = gn[j].astype(F32) + rc[j].astype(F32) + ry[j].astype(F32)
        m = mid[at, :]
        inv = lax.rsqrt(jnp.mean(m * m, axis=-1, keepdims=True) + NORM_EPS)
        unit = m * inv
        weighted = grad * gain
        part = part + jnp.sum(grad * unit, axis=0, keepdims=True)
        gmid = cs[j].astype(F32) + inv * (weighted - unit * jnp.mean(weighted * unit, axis=-1, keepdims=True))
        mid[at, :] = gmid
        gmb[j] = gmid.astype(BF16)
        there = gm_h.at[pl.ds(pl.multiple_of(core * rows + j * tile, tile), tile)]
        copies = [
            pltpu.make_async_copy(gmb.at[j], there, out_sem.at[1 + j]),
            remote(gmb.at[j], there, 12 + j, by_core),
        ]
        for copy in copies:
            copy.start()
        gm_out += copies
    part_ref[...] = part
    last = pltpu.make_async_copy(mid, gmid_h, out_sem.at[0])
    last.start()
    for copy in gm_out:
        copy.wait()
    last.wait()
    for copy in sums:
        copy.wait()
    for group in (d_in, x_row, x_core, x_both, g_near, g_far, g_row):
        for copy in group:
            copy.wait_send()


def mlp_phase(middle, cots, wg_t, wu_t, wd, gain):
    rows, d = middle.shape
    ff = wd.shape[0]
    tile = rows // 2
    blk = 128
    hbm = pl.BlockSpec(memory_space=pltpu.HBM)
    vmem = pl.BlockSpec(memory_space=pltpu.VMEM)
    dma = pltpu.SemaphoreType.DMA
    return pl.pallas_call(
        mlp_phase_kernel,
        name="mlp_phase",
        in_specs=[hbm] * 8 + [vmem],
        out_specs=[hbm, hbm, vmem] + [hbm] * 5,
        out_shape=[sds((rows, d), F32), sds((2 * rows, d), BF16), sds((1, d), F32)]
        + [sds((d, ff), BF16)] * 3 + [sds((rows, d), BF16)] * 2,
        scratch_shapes=[
            pltpu.VMEM((rows, d), F32), pltpu.VMEM((8, tile, d), BF16), pltpu.VMEM((8, tile, d), BF16),
            pltpu.VMEM((ff, d), BF16), pltpu.VMEM((ff, d), BF16), pltpu.VMEM((ff, d), BF16),
            pltpu.VMEM((8, tile, ff), BF16), pltpu.VMEM((8, tile, ff), BF16), pltpu.VMEM((8, tile, ff), BF16),
            pltpu.VMEM((8, tile, d), BF16), pltpu.VMEM((2, tile, d), BF16), pltpu.VMEM((2, tile, d), BF16),
            pltpu.VMEM((2, tile, d), BF16), pltpu.VMEM((2, tile, d), BF16),
            pltpu.VMEM((8, tile, d), BF16), pltpu.VMEM((4, tile, d), BF16),
            pltpu.VMEM((2, 3, blk, ff), BF16), pltpu.VMEM((2, tile, d), BF16),
            dma((12,)), dma((18,)), dma((18,)), dma((2, 3)), dma((7,)),
        ],
        compiler_params=pltpu.CompilerParams(collective_id=1, has_side_effects=True, vmem_limit_bytes=62 << 20),
        cost_estimate=cost(18 * 4 * rows * d * ff, 60e6, 4 * rows * ff),
    )(middle, *cots, wg_t, wu_t, wd, gain)


class Wires:
    def __init__(self, send_sem, recv_sem):
        self.send_sem, self.recv_sem, self.used, self.all = send_sem, recv_sem, 0, []

    def copy(self, src, dst, target):
        made = pltpu.make_async_remote_copy(
            src,
            dst,
            self.send_sem.at[self.used],
            self.recv_sem.at[self.used],
            device_id=target,
            device_id_type=MESH,
        )
        self.used += 1
        self.all.append(made)
        return made

    def drain(self):
        for made in self.all:
            made.wait_send()


class Places:
    def __init__(self, wide_count):
        self.wide, self.place = lax.axis_index("wide"), lax.axis_index("narrow")
        self.core = self.place % 2
        self.second = self.place // 2
        self.by_core = (self.wide, self.place + 1 - 2 * self.core)
        self.by_row = (self.wide, (self.place + 2) % 4)
        self.bits = []
        bit = 1
        while bit < wide_count:
            self.bits.append(bit)
            bit *= 2

    def has(self, bit):
        return (self.wide // bit) % 2

    def across(self, bit):
        return (self.wide + bit - 2 * bit * self.has(bit), self.place)

    def meet(self):
        barrier = pltpu.get_barrier_semaphore()
        others = [self.by_core, self.by_row] + [self.across(bit) for bit in self.bits]
        for other in others:
            pl.semaphore_signal(barrier, 1, device_id=other, device_id_type=MESH)
        pl.semaphore_wait(barrier, len(others))


class Scan:
    def __init__(self, where, wires, tot_s, tot_m, pre_s, pre_m, out, into, backward):
        self.tot_s, self.tot_m, self.pre_s, self.pre_m = tot_s, tot_m, pre_s, pre_m
        self.out, self.into = out, into
        self.steps = []
        for i, bit in enumerate([0] + where.bits):
            target = where.across(bit) if bit else where.by_row
            is_set = where.has(bit) if bit else where.second
            later = (1 - is_set if backward else is_set) > 0
            self.steps.append((wires.copy(out.at[i], into.at[i], target), later, bit == 0))
        pre_s[...] = jnp.zeros_like(pre_s)
        pre_m[...] = jnp.ones_like(pre_m)

    def begin(self, i=0):
        self.at = i
        dv = self.tot_s.shape[1]
        for h in range(2):
            self.out[i, h, :dv, :] = self.tot_s[h].astype(BF16)
            self.out[i, h, dv:, :] = jnp.broadcast_to(self.tot_m[h], (16, self.tot_m.shape[2])).astype(BF16)
        self.steps[i][0].start()

    def advance(self):
        self.finish(self.at)
        if self.at + 1 < len(self.steps):
            self.begin(self.at + 1)
            return True
        return False

    def finish(self, i):
        copy, later, swapped = self.steps[i]
        copy.wait_recv()
        dv = self.tot_s.shape[1]
        for h in range(2):
            g = 1 - h if swapped else h
            oth_s = self.into[i, g, :dv, :].astype(F32)
            oth_m = self.into[i, g, dv : dv + 1, :].astype(F32)
            pre_s, pre_m, tot_s, tot_m = self.pre_s[h], self.pre_m[h], self.tot_s[h], self.tot_m[h]
            self.pre_s[h] = jnp.where(later, oth_s * pre_m + pre_s, pre_s)
            self.pre_m[h] = jnp.where(later, oth_m * pre_m, pre_m)
            self.tot_s[h] = jnp.where(later, oth_s * tot_m + tot_s, tot_s * oth_m + oth_s)
            self.tot_m[h] = tot_m * oth_m


class Scatter:
    def __init__(self, where, wires, source, keep, order, recvs):
        self.recvs, self.steps = recvs, []
        left = sorted(where.bits, reverse=True)
        held, first = source, keep
        for bit, recv in zip(order, recvs):
            dim = left.index(bit)
            mine = where.has(bit)
            other = held.at[(slice(None),) * dim + (1 - mine,)]
            self.steps.append((wires.copy(other, recv, where.across(bit)), first if first is not None else held, dim, mine, first is not None))
            left.pop(dim)
            held, first = recv, None

    def begin(self, i=0):
        self.at = i
        self.steps[i][0].start()

    def advance(self):
        if self.at + 1 < len(self.steps):
            self.finish(self.at)
            self.begin(self.at + 1)

    def result(self):
        while self.at + 1 < len(self.steps):
            self.advance()
        return self.finish(self.at)

    def finish(self, i):
        copy, held, dim, mine, picked = self.steps[i]
        copy.wait_recv()
        recv = self.recvs[i]
        last = i == len(self.steps) - 1
        for at in itertools.product(range(2), repeat=len(recv.shape) - 2):
            source = at if picked else at[:dim] + (mine,) + at[dim:]
            total = recv[at].astype(F32) + held[source].astype(F32)
            if last:
                return total
            recv[at] = total.astype(BF16)
        return None


class Everywhere:
    def __init__(self, where, wires, values, recvs):
        self.values, self.recvs = values, recvs
        targets = [where.by_core, where.by_row] + [where.across(bit) for bit in where.bits]
        self.steps = [wires.copy(values.at[i], recvs.at[i], target) for i, target in enumerate(targets)]

    def begin(self, i=0):
        self.at = i
        self.steps[i].start()

    def advance(self):
        if self.at + 1 < len(self.steps):
            self.finish(self.at)
            self.begin(self.at + 1)

    def result(self):
        while self.at + 1 < len(self.steps):
            self.advance()
        self.finish(self.at)
        return self.values[len(self.steps)]

    def finish(self, i):
        self.steps[i].wait_recv()
        self.values[i + 1] = self.values[i] + self.recvs[i]


def bit_index(w, bits):
    return tuple((w // bit) % 2 for bit in sorted(bits, reverse=True))


def back_phase_kernel(
    bits,
    gm_h, mx_h, s_h, r_h, gt_h, rows_h, q_h, k_h, v_h, cum_h, dpre_h, rank_h, sin_h, w_h, wo_h, g_h, gmid_h, tok_h,
    off_ref, enter_ref, mult_ref, ru_ref, rd_ref, ggain_ref, ngain_ref, mpart_ref, restart_ref,
    in_h, gate_o, up_o, down_o, wout_o, k_o, v_o, q_o, s_o, rdown_o, rup_o, bias_o, mgain_o, group_o, ngain_o,
    gm, mx, sw, reach, gated, rows, q, k, v, cum, dpre, rank, sin, w, wo, keep, mrecv, gmid, tok,
    gx, al, grank, ds, lb_m, pre_s, pre_m, sc_out, sc_in, osv, osy, osr, kv, kvy, kvr, tb, tr, sm, smr, ng, ngr,
    load_sem, send_sem, recv_sem, out_sem,
):
    count, d = rows.shape
    half = count // 2
    dk, dv = q.shape[2], v.shape[2]
    where = Places(2 ** len(bits))
    wires = Wires(send_sem, recv_sem)
    loads = []

    def load(src, dst):
        copy = pltpu.make_async_copy(src, dst, load_sem.at[len(loads)])
        loads.append(copy)
        copy.start()
        return copy

    orders = (bits, bits[1:] + bits[:1], bits)
    first = [load(gm_h, gm)]
    for h in range(2):
        first += [load(wo_h[h], wo.at[h]), load(mx_h[h], mx.at[h]), load(s_h[h], sw.at[h]), load(r_h[h], reach.at[h])]
    second = [load(gt_h[h], gated.at[h]) for h in range(2)] + [load(rows_h, rows)]
    third = []
    for i in range(3):
        left = sorted(bits, reverse=True)
        dim = left.index(orders[i][0])
        third.append(load(g_h[i].at[(slice(None),) * dim + (where.has(orders[i][0]),)], keep[i]))
    fourth = [load(rank_h, rank)]
    for h in range(2):
        for src, dst in ((q_h, q), (k_h, k), (v_h, v), (cum_h, cum), (dpre_h, dpre), (sin_h, sin), (w_h, w)):
            fourth.append(load(src[h], dst.at[h]))
    fifth = [load(gmid_h, gmid), load(tok_h, tok)]

    where.meet()
    mlp = [Scatter(where, wires, g_h[i], keep[i], orders[i], mrecv[i]) for i in range(3)]
    scan = Scan(where, wires, ds, lb_m, pre_s, pre_m, sc_out, sc_in, True)
    os_y = wires.copy(osv.at[1], osy, where.by_row)
    os_s = Scatter(where, wires, osv.at[0], None, bits[1:] + bits[:1], osr)
    kv_y = wires.copy(kv.at[1], kvy, where.by_row)
    kv_s = Scatter(where, wires, kv.at[0], None, bits, kvr)
    tots = [wires.copy(tb.at[j], tr.at[j], where.by_core) for j in range(2)]
    every = Everywhere(where, wires, sm, smr)
    every_n = Everywhere(where, wires, ng, ngr)
    n_bits = len(bits)
    for part in mlp:
        part.begin()

    blk = half // 2
    gain = ggain_ref[...]
    ds[...] = jnp.zeros_like(ds)
    sm[0] = jnp.zeros_like(sm[0])
    ng[0] = jnp.zeros_like(ng[0])
    for copy in first:
        copy.wait()

    def gate_step(i, part):
        at = pl.ds(pl.multiple_of(i * blk, blk), blk)
        g = gm[at, :]
        for h in range(2):
            grad = dot_nt(g, wo[h])
            mixed = mx[h, at, :]
            inv = lax.rsqrt(jnp.mean(mixed * mixed, axis=-1, keepdims=True) + GROUP_EPS)
            unit = mixed * inv
            s = sw[h, at, :]
            sig = jax.nn.sigmoid(s)
            al[h, at, 2 * dk + dv :] = (grad * unit * gain * (sig * (1.0 + s * (1.0 - sig)))).astype(BF16)
            dn = grad * (s * sig)
            part = part + jnp.sum(dn * unit, axis=0, keepdims=True)
            weighted = dn * gain
            gmix = (inv * (weighted - unit * jnp.mean(weighted * unit, axis=-1, keepdims=True))).astype(BF16)
            gx[h, at, :] = gmix
            ds[h] += dot_tn(gmix, reach[h, at, :])
        return part

    group_part = lax.fori_loop(0, 4, gate_step, jnp.zeros((1, dv), F32))
    for h in range(2):
        ds[h] = ds[h] * restart_ref[...]
        lb_m[h] = mult_ref[h]
    scan.begin()

    size = 256
    per = size // osv.shape[-2]

    def put(ref, h, j, lanes, value):
        rows_each = ref.shape[-2]
        for p in range(per):
            ref[(h,) + bit_index(j * per + p, bits) + (slice(None), lanes)] = value[p * rows_each : (p + 1) * rows_each]

    def out_step(j, _):
        cols = pl.ds(pl.multiple_of(j * size, size), size)
        for h in (1, 0):
            put(osv, h, j, slice(0, dv), dot_tn(gm[:, cols], gated[h]).astype(BF16))
        return 0

    def swish_step(j, _):
        cols = pl.ds(pl.multiple_of(j * size, size), size)
        for h in (1, 0):
            put(osv, h, j, slice(dv, 2 * dv), dot_tn(rows[:, cols], al[h, :, 2 * dk + dv :]).astype(BF16))
        return 0

    for copy in second:
        copy.wait()
    lax.fori_loop(0, d // size, out_step, 0)
    scan.advance()
    lax.fori_loop(0, d // size, swish_step, 0)
    os_y.start()
    for copy in third:
        copy.wait()
    while scan.advance():
        if scan.at == n_bits:
            mlp[1].advance()
            mlp[0].advance()
    for copy in fourth:
        copy.wait()

    ds[...] = pre_s[...]
    chunks = count // CHUNK
    mask = triangle(True)
    ones = triangle(False).astype(F32)
    scale = dk**-0.5
    rk = rank.shape[1]

    def back_step(step, carry):
        c = chunks - 1 - step
        at = pl.ds(pl.multiple_of(c * CHUNK, CHUNK), CHUNK)
        grs, new = None, []
        for h in range(2):
            ch = cum[h, at, :]
            mid = ch[HALF - 1 : HALF]
            end = ch[CHUNK - 1 :]
            e_qd, e_kd, e_qi, e_ke = jnp.exp(ch - mid), jnp.exp(mid - ch), jnp.exp(ch), jnp.exp(end - ch)
            e_end = jnp.exp(end)
            qf = q[h, at, :].astype(F32) * scale
            kf = k[h, at, :].astype(F32)
            vc = v[h, at, :]
            qd = (qf * e_qd).astype(BF16)
            kd = (kf * e_kd).astype(BF16)
            qi = (qf * e_qi).astype(BF16)
            ke = (kf * e_ke).astype(BF16)
            go = gx[h, at, :]
            state = sin[h, c].astype(F32) + enter_ref[h] * jnp.exp(off_ref[h, c])
            state_low = state.astype(BF16)
            dstate = ds[h]
            dstate_low = dstate.astype(BF16)
            scores = jnp.where(mask, dot_nt(qd, kd), 0.0).astype(BF16)
            dscores = jnp.where(mask, dot_nt(go, vc), 0.0).astype(BF16)
            d_v = dot_tn(scores, go) + dot_nt(ke, dstate_low)
            d_qd = dot(dscores, kd)
            d_qi = dot(go, state_low)
            d_kd = dot_tn(dscores, qd)
            d_ke = dot(vc, dstate_low)
            d_q = scale * (d_qd * e_qd + d_qi * e_qi)
            d_k = d_kd * e_kd + d_ke * e_ke
            tail = ke.astype(F32) * d_ke
            d_cum = qd.astype(F32) * d_qd + qi.astype(F32) * d_qi - kd.astype(F32) * d_kd - tail
            d_end = jnp.sum(tail, axis=0, keepdims=True) + e_end * jnp.sum(dstate * state, axis=0, keepdims=True)
            grad_decay = exact(ones, d_cum, ((1,), (0,))) + d_end
            g_pre = grad_decay * jax.nn.sigmoid(-dpre[h, at, :]) * (1.0 / GATE_NORM)
            al[h, at, :dk] = d_k.astype(BF16)
            al[h, at, dk : dk + dv] = d_v.astype(BF16)
            al[h, at, dk + dv : 2 * dk + dv] = d_q.astype(BF16)
            gr = exact(g_pre, ru_ref[h], ((1,), (1,)))
            grs = gr if grs is None else grs + gr
            new.append(carry[2 * h] + exact(rank[at, :], g_pre, ((0,), (0,))))
            new.append(carry[2 * h + 1] + jnp.sum(g_pre, axis=0, keepdims=True))
            ds[h] = dstate * e_end + dot_tn(go, qi)
        grank[at, :] = grs.astype(BF16)
        return tuple(new)

    zero = (jnp.zeros((rk, dk), F32), jnp.zeros((1, dk), F32))
    rup0, gb0, rup1, gb1 = lax.fori_loop(0, chunks, back_step, zero + zero)
    for i in (1, 0, 2):
        mlp[i].advance()

    def kvq_step(h):
        def step(j, _):
            cols = pl.ds(pl.multiple_of(j * size, size), size)
            put(kv, h, j, slice(None), dot_tn(rows[:, cols], al[h, :, : 2 * dk + dv]).astype(BF16))
            return 0

        lax.fori_loop(0, d // size, step, 0)

    kvq_step(1)
    kv_y.start()

    def add_row(ref, extra):
        for at in itertools.product(range(2), repeat=n_bits):
            ref[(0,) + at] = (ref[(0,) + at].astype(F32) + extra[at].astype(F32)).astype(BF16)

    os_y.wait_recv()
    add_row(osv, osy)
    os_s.begin()

    def total_step(i, _):
        b = jnp.where(i < 2, 2 - 2 * where.core + i, 2 * where.core + i - 2)
        at = pl.ds(pl.multiple_of(b * blk, blk), blk)
        total = dot_nt(al[0, at, :], w[0]) + dot_nt(al[1, at, :], w[1]) + dot_nt(grank[at, :], rd_ref[...])
        for j in range(2):

            @pl.when(i == j)
            def _():
                tb[j] = total.astype(BF16)
                tots[j].start()

            @pl.when(i == 2 + j)
            def _():
                tb[2 + j] = total.astype(BF16)

        return 0

    lax.fori_loop(0, 4, total_step, 0)

    sm[0, 0:rk, :] = dot_tn(grank[...], rows[...])
    at0 = pl.ds(pl.multiple_of(where.place * dk, dk), dk)
    at1 = pl.ds(pl.multiple_of(((where.place + 2) % 4) * dk, dk), dk)
    sm[0, rk : 2 * rk, at0] = rup0
    sm[0, rk : 2 * rk, at1] = rup1
    sm[0, 2 * rk : 2 * rk + 1, at0] = gb0
    sm[0, 2 * rk : 2 * rk + 1, at1] = gb1
    sm[0, 2 * rk + 1 : 2 * rk + 2, :] = mpart_ref[...]
    sm[0, 2 * rk + 2 : 2 * rk + 3, :dv] = group_part
    every.begin()
    kvq_step(0)
    every.advance()

    for copy in fifth:
        copy.wait()
    ngain = ngain_ref[...]
    part = jnp.zeros((1, d), F32)
    for j in range(2):
        at = pl.ds(j * blk, blk)
        tots[j].wait_recv()
        grad = tb[2 + j].astype(F32) + tr[j].astype(F32)
        x = tok[at, :].astype(F32)
        inv = lax.rsqrt(jnp.mean(x * x, axis=-1, keepdims=True) + NORM_EPS)
        unit = x * inv
        weighted = grad * ngain
        part = part + jnp.sum(grad * unit, axis=0, keepdims=True)
        gmid[at, :] = gmid[at, :] + inv * (weighted - unit * jnp.mean(weighted * unit, axis=-1, keepdims=True))
    done = pltpu.make_async_copy(gmid, in_h, out_sem.at[0])
    done.start()
    ng[0, 0:1, :] = part
    every_n.begin()

    outs = (gate_o, up_o, down_o)
    kv_y.wait_recv()
    add_row(kv, kvy)
    kv_s.begin()
    for i in (1, 0):
        outs[i][...] = jnp.transpose(mlp[i].result())
    mlp[2].advance()
    every.advance()
    every_n.advance()
    for _ in range(n_bits - 1):
        os_s.advance()
        every_n.advance()
        kv_s.advance()
        every.advance()
    outs[2][...] = jnp.transpose(mlp[2].result())
    total = os_s.result()
    wout_o[...] = jnp.transpose(total[:, :dv])
    s_o[...] = total[:, dv:]
    every_n.advance()
    total = kv_s.result()
    k_o[...] = total[:, :dk]
    v_o[...] = total[:, dk : dk + dv]
    q_o[...] = total[:, dk + dv :]
    small = every.result()
    rdown_o[...] = small[:rk]
    rup_o[...] = small[rk : 2 * rk, : rup_o.shape[1]]
    bias_o[...] = small[2 * rk : 2 * rk + 1, : bias_o.shape[1]]
    mgain_o[...] = small[2 * rk + 1 : 2 * rk + 2]
    group_o[...] = small[2 * rk + 2 : 2 * rk + 3, :dv]
    ngain_o[...] = every_n.result()[:1]
    done.wait()
    wires.drain()


def back_phase(
    gm, mx, s, reach, gated, rows, q, k, v, cum, dpre, rank, sin, w, wo, grads, gmid, tokens,
    off, enter, mult, ru, rd, ggain, ngain, mpart, restart,
):
    bits = wide_bits()
    count, d = rows.shape
    half = count // 2
    dk, dv, rk = q[0].shape[1], v[0].shape[1], rank.shape[1]
    ff = grads[0].shape[-1]
    each = d // 2 ** len(bits)
    n_bits, chunks = len(bits), count // CHUNK
    hbm = pl.BlockSpec(memory_space=pltpu.HBM)
    vmem = pl.BlockSpec(memory_space=pltpu.VMEM)
    dma = pltpu.SemaphoreType.DMA
    v_ = pltpu.VMEM

    def shape(lead, cols):
        return (2,) * lead + (each, cols)

    def falls(cols):
        return [v_(shape(n_bits - 1 - i, cols), BF16) for i in range(n_bits)]

    pair, three = [hbm] * 2, [hbm] * 3
    kvq = 2 * dk + dv
    small = 2 * rk + 8
    scratch = [
        v_((count, d), BF16), v_((2, count, dv), F32), v_((2, count, dv), F32), v_((2, count, dk), BF16),
        v_((2, count, dv), BF16), v_((count, d), BF16), v_((2, count, dk), BF16), v_((2, count, dk), BF16),
        v_((2, count, dv), BF16), v_((2, count, dk), F32), v_((2, count, dk), F32), v_((count, rk), F32),
        v_((2, chunks, dv, dk), BF16), v_((2, d, kvq + dv), BF16), v_((2, dv, d), BF16),
        [v_(shape(n_bits - 1, ff), BF16)] * 3, [falls(ff)] * 3, v_((half, d), F32), v_((half, d), BF16),
        v_((2, count, dv), BF16), v_((2, count, kvq + dv), BF16), v_((count, rk), BF16),
        v_((2, dv, dk), F32), v_((2, 1, dk), F32), v_((2, dv, dk), F32), v_((2, 1, dk), F32),
        v_((n_bits + 1, 2, dv + 16, dk), BF16), v_((n_bits + 1, 2, dv + 16, dk), BF16),
        v_((2,) + shape(n_bits, 2 * dv), BF16), v_(shape(n_bits, 2 * dv), BF16), falls(2 * dv),
        v_((2,) + shape(n_bits, kvq), BF16), v_(shape(n_bits, kvq), BF16), falls(kvq),
        v_((4, half // 2, d), BF16), v_((2, half // 2, d), BF16),
        v_((n_bits + 3, small, d), F32), v_((n_bits + 2, small, d), F32),
        v_((n_bits + 3, 8, d), F32), v_((n_bits + 2, 8, d), F32),
        dma((48,)), dma((64,)), dma((64,)), dma((1,)),
    ]
    out_shape = [
        sds((half, d), F32), sds((ff, each), F32), sds((ff, each), F32), sds((ff, each), F32), sds((dv, each), F32),
        sds((each, dk), F32), sds((each, dv), F32), sds((each, dk), F32), sds((each, dv), F32),
        sds((rk, d), F32), sds((rk, 4 * dk), F32), sds((1, 4 * dk), F32), sds((1, d), F32), sds((1, dv), F32), sds((1, d), F32),
    ]
    operands = (
        gm, mx, s, reach, gated, rows, q, k, v, cum, dpre, rank, sin, w, wo, grads, gmid, tokens,
        off, enter, mult, ru, rd, ggain, ngain, mpart, restart,
    )
    flat, tree = jax.tree.flatten(operands)
    n_vmem = len(jax.tree.leaves(operands[18:]))
    flat_scratch, scratch_tree = jax.tree.flatten(scratch, is_leaf=lambda x: not isinstance(x, list))
    n_in, n_out = len(flat), len(out_shape)

    def kernel(*refs):
        ins = jax.tree.unflatten(tree, refs[:n_in])
        rest = jax.tree.unflatten(scratch_tree, refs[n_in + n_out :])
        back_phase_kernel(bits, *ins, *refs[n_in : n_in + n_out], *rest)

    return pl.pallas_call(
        kernel,
        name="back_phase",
        in_specs=[hbm] * (n_in - n_vmem) + [vmem] * n_vmem,
        out_specs=[hbm] + [vmem] * (n_out - 1),
        out_shape=out_shape,
        scratch_shapes=flat_scratch,
        compiler_params=pltpu.CompilerParams(collective_id=2, has_side_effects=True, vmem_limit_bytes=62 << 20),
        cost_estimate=cost(40e9, 60e6, 1e6),
    )(*flat)


def hop(value, axis, bit):
    return lax.ppermute(value, axis, [(i, i ^ bit) for i in range(lax.axis_size(axis))])


def wide_bits():
    count, bits, bit = lax.axis_size("wide"), [], 1
    while bit < count:
        bits.append(bit)
        bit *= 2
    return bits


def scan_states(mult, state, backward):
    place = {"narrow": lax.axis_index("narrow"), "wide": lax.axis_index("wide")}
    heads, dv, dk = state.shape
    pre_m, pre_s = jnp.ones_like(mult), jnp.zeros_like(state)
    tot_m, tot_s = mult, state
    for axis, bit in [("narrow", 2)] + [("wide", b) for b in wide_bits()]:
        packed = jnp.concatenate(
            [tot_s, jnp.broadcast_to(tot_m, (heads, 16, dk))], axis=1
        ).astype(BF16)
        other = hop(packed, axis, bit).astype(F32)
        if axis == "narrow":
            other = other[::-1]
        oth_s, oth_m = other[:, :dv], other[:, dv : dv + 1]
        is_set = (place[axis] & bit) != 0
        mine_later = jnp.logical_not(is_set) if backward else is_set
        new_s = oth_s * pre_m + pre_s
        new_m = oth_m * pre_m
        sum_later = oth_s * tot_m + tot_s
        sum_first = tot_s * oth_m + oth_s
        pre_s = jnp.where(mine_later, new_s, pre_s)
        pre_m = jnp.where(mine_later, new_m, pre_m)
        tot_s = jnp.where(mine_later, sum_later, sum_first)
        tot_m = tot_m * oth_m
    return pre_s


def shards(
    tokens, cotangent, flags, norm_gain, query_weight, key_weight, value_weight, swish_weight, rank_down, rank_up,
    decay_bias, group_gain, output_weight, mlp_gain, mlp_gate, mlp_up, mlp_down,
):
    own_rows = tokens.shape[0]
    place = lax.axis_index("narrow")
    core = place & 1
    second = (place & 2) != 0
    wide_odd = (lax.axis_index("wide") & 1) != 0
    dk = query_weight.shape[1]
    dv = value_weight.shape[1]
    d = tokens.shape[1]

    def in_order(mine, other):
        return jnp.where(
            core == 0, jnp.concatenate([mine, other]), jnp.concatenate([other, mine])
        )

    def from_row_partner(value):
        half = value.shape[0] // 2
        piece = lax.dynamic_slice_in_dim(value, jnp.where(wide_odd, half, 0), half, 0)
        first = hop(piece, "narrow", 2)
        relayed = hop(first, "wide", 1)
        return jnp.where(
            wide_odd, jnp.concatenate([relayed, first]), jnp.concatenate([first, relayed])
        )

    def head_cols(index):
        ru = lax.dynamic_slice_in_dim(rank_up, index * dk, dk, 1).astype(F32)
        bias = lax.dynamic_slice_in_dim(decay_bias, index * dk, dk, 0).astype(F32)
        return ru, bias.reshape(1, dk)

    restart = 1.0 - flags[0].astype(F32)
    restart = jnp.where(second, 1.0, restart)
    norm_gain_f = norm_gain.astype(F32)
    mlp_gain_f = mlp_gain.astype(F32)
    gain_row = group_gain.astype(F32).reshape(1, dv)

    inputs = tokens.astype(F32)
    inv_one = lax.rsqrt(jnp.mean(inputs * inputs, axis=-1, keepdims=True) + NORM_EPS)
    normed = (inputs * inv_one * norm_gain_f).astype(BF16)
    normed_two = hop(normed, "narrow", 1)
    rows_all = in_order(normed, normed_two)

    w_own = jnp.concatenate([key_weight, value_weight, query_weight, swish_weight], axis=1)
    w_other = from_row_partner(w_own)
    out_other = from_row_partner(output_weight)
    cot_late, w_other, out_other = lax.optimization_barrier((cotangent, w_other, out_other))
    cot_y = hop(cot_late, "narrow", 2)
    cot_c = hop(cotangent, "narrow", 1)
    cot_d = hop(cot_y, "narrow", 1)

    ru_own, bias_own = head_cols(place)
    ru_oth, bias_oth = head_cols(place ^ 2)
    weights_out = (output_weight, out_other)
    one = forward_head(rows_all, w_own, rank_down, ru_own, bias_own, dk, dv)
    two = forward_head(rows_all, w_other, rank_down, ru_oth, bias_oth, dk, dv)
    (q, k, v, s, cum, dpre, rank_pre, base, reach, sin, off, state, mult) = zip(one, two)
    rank_pre = rank_pre[0]
    mults = restart * jnp.stack(mult)
    enter = restart * scan_states(mults, jnp.stack(state), False)
    enter_low = enter.astype(BF16)
    mixed0, mixed1, gated0, gated1, term = gate_out(
        base, reach, s, (enter_low[0], enter_low[1]), gain_row, weights_out
    )
    own_term = lax.dynamic_slice_in_dim(term, core * own_rows, own_rows, 0)
    send_term = lax.dynamic_slice_in_dim(term, (1 - core) * own_rows, own_rows, 0)
    middle = inputs + (own_term.astype(F32) + hop(send_term, "narrow", 1).astype(F32))
    grad_middle, gm_all, mlp_gain_part, gate_g, up_g, down_g, near, far = mlp_phase(
        middle, (cotangent, cot_c, cot_y, cot_d), mlp_gate.T, mlp_up.T, mlp_down, mlp_gain_f.reshape(1, d)
    )
    result = (middle + (near.astype(F32) + hop(far, "narrow", 2).astype(F32))).astype(BF16)
    bits = wide_bits()
    split = (2,) * len(bits) + (d // 2 ** len(bits), -1)
    input_grad, gate_t, up_t, down_t, out_t, k_g, v_g, q_g, s_g, rdown_t, rup_g, bias_g, mgain_g, group_g, ngain = back_phase(
        gm_all, (mixed0, mixed1), s, reach, (gated0, gated1), rows_all, q, k, v, cum, dpre, rank_pre, sin,
        (w_own, w_other), weights_out, tuple(g.reshape(split) for g in (gate_g, up_g, down_g)), grad_middle, tokens,
        jnp.stack(off), enter, mults, jnp.stack([ru_own, ru_oth]), rank_down, gain_row, norm_gain_f.reshape(1, d),
        mlp_gain_part, jnp.full((1, dk), restart, F32),
    )
    return (
        result,
        input_grad,
        ngain[0],
        q_g,
        k_g,
        v_g,
        s_g,
        rdown_t.T,
        rup_g,
        bias_g[0],
        group_g[0],
        out_t,
        mgain_g[0],
        gate_t.T,
        up_t.T,
        down_t,
    )


def solution(mesh):
    rows, cols = P(("wide", "narrow"), None), P(None, "narrow")
    both = P("wide", "narrow")
    in_specs = (
        rows, rows, P("wide"), P(), cols, cols, cols, cols, P(), P(), P(), P(), P("narrow", None), P(), cols, cols,
        P("narrow", None),
    )
    out_specs = (
        rows, rows, P(), both, both, both, both, P(), P(), P(), P(), P("narrow", "wide"), P(), both, both,
        P("narrow", "wide"),
    )
    return jax.shard_map(shards, mesh=mesh, in_specs=in_specs, out_specs=out_specs, check_vma=False)
```

profile of v0, /device:TPU:0, one launch (start us, length us, event | category | flops | bytes accessed | tf_op | source)
XLA Modules:
  0.0 356.5 jit_solution(3087600563552910335)
XLA Ops:
  0.7 0.8 convert_element_type.56
  1.4 1.6 fusion
  4.1 0.8 constant_dynamic-update-slice_fusion.3
  4.8 0.9 constant_dynamic-update-slice_fusion.2
  5.7 0.8 constant_dynamic-update-slice_fusion.1
  6.5 0.9 constant_dynamic-update-slice_fusion.w_ref.refs_23_
  7.4 1.2 constant_dynamic-slice_fusion.2
  8.6 3.0 collective-permute-start.1
  11.7 23.3 %collective-permute-done.3 = bf16[128,1024]{1,0:T(8,128)(2,1)S(1)} collective-permute-done((bf16[128,1024]{1,0:T(8,128)(2,1)S(1)}, bf16[128,1024]{1,0:T(8,128)(2,1)S(1)}, u32[]{:S(2)}, u32[]{:S(2)}) %collective-permute-start.3) | collective-permute-done | bytes 262176 | tf_op jit(solution)/shard_map/ppermute | solution.py:934
  35.0 1.7 collective-permute-start.4
  38.1 6.3 %collective-permute-done.4 = bf16[128,1024]{1,0:T(8,128)(2,1)} collective-permute-done((bf16[128,1024]{1,0:T(8,128)(2,1)S(1)}, bf16[128,1024]{1,0:T(8,128)(2,1)}, u32[]{:S(2)}, u32[]{:S(2)}) %collective-permute-start.4) | collective-permute-done | bytes 262176 | tf_op jit(solution)/shard_map/ppermute | solution.py:934
  44.4 1.4 maximum_select_fusion.2.w1.refs_26_
  45.8 3.7 %maximum_select_fusion.x_ref.refs_9_ = bf16[1280,1024]{1,0:T(8,128)(2,1)} fusion(bf16[640,1024]{1,0:T(8,128)(2,1)} %collective-permute-done, bf16[640,1024]{1,0:T(8,128)(2,1)S(1)} %fusion.2, pred[]{:T(512)S(6)} %eq.3), kind=kLoop, calls=%fused_computation.6 | loop fusion | flops 11796480 | bytes 5242881 | tf_op jit(solution)/shard_map/jit(_where)/select_n | solution.py:985
  49.5 12.8 %forward_head.2 = (bf16[1280,128]{1,0:T(8,128)(2,1)S(1)}, bf16[1280,128]{1,0:T(8,128)(2,1)S(1)}, bf16[1280,256]{1,0:T(8,128)(2,1)S(1)}, f32[1280,256]{1,0:T(8,12...) custom-call(bf16[1280,1024]{1,0:T(8,128)(2,1)} %maximum_select_fusio, ...), custom_call_target="tpu_custom_call" | custom-call | flops 3019898880 | bytes 7741440 | tf_op jit(solution)/shard_map/forward_head/pallas_call | solution.py:129
  62.3 0.8 copy-done.14
  63.1 0.8 copy-done.15
  64.0 0.9 copy-done.16
  64.8 0.7 copy-done.21
  65.6 0.7 copy-done.22
  66.3 4.2 %maximum_select_fusion.1.w_ref.refs_24_ = bf16[1024,768]{1,0:T(8,128)(2,1)} fusion(bf16[512,768]{1,0:T(8,128)(2,1)} %collective-permute-done.1, bf16[512,768]{1,0:T(8,128)(2,1)S(1)} %collective-permute-done.2, pred[]{:T(512)S(6)} %ne.14), kind=kLoop, calls=%fused_computation.8 | loop fusion | flops 7077888 | bytes 3145729 | tf_op jit(solution)/shard_map/jit(_where)/select_n | solution.py:994
  70.6 12.9 %forward_head.3 = (bf16[1280,128]{1,0:T(8,128)(2,1)S(1)}, bf16[1280,128]{1,0:T(8,128)(2,1)S(1)}, bf16[1280,256]{1,0:T(8,128)(2,1)S(1)}, f32[1280,256]{1,0:T(8,12...) custom-call(bf16[1280,1024]{1,0:T(8,128)(2,1)} %maximum_select_fusio, ...), custom_call_target="tpu_custom_call" | custom-call | flops 3019898880 | bytes 7741440 | tf_op jit(solution)/shard_map/forward_head/pallas_call | solution.py:129
  83.4 1.1 copy-done.2
  84.5 0.8 copy-done.17
  85.3 0.8 copy-done.18
  86.2 0.9 copy-done.19
  87.1 0.9 copy-done.20
  87.9 0.7 copy-done.23
  88.7 0.7 copy-done.24
  89.5 1.9 collective-permute-start.5
  91.3 3.3 collective-permute-done.5
  95.3 1.8 collective-permute-start.6
  97.1 3.3 collective-permute-done.6
  100.6 1.9 collective-permute-start.7
  102.4 1.6 collective-permute-start.11
  104.0 1.7 collective-permute-done.7
  105.9 3.3 collective-permute-start.8
  109.3 3.0 collective-permute-done.8
  112.3 0.8 fusion.8
  113.2 6.8 %gate_out.1 = (f32[1280,256]{1,0:T(8,128)S(1)}, f32[1280,256]{1,0:T(8,128)S(1)}, bf16[1280,256]{1,0:T(8,128)(2,1)S(1)}, bf16[1280,256]{1,0:T(8,128)(2,1)S(1)}, bf16[1280,1024]{1,0:T(8,128)(2,1)}) custom-call(f32[1280,256]{1,0:T(8,128)} %get-tuple-element.72.b0, f32[1280,256]{1,0:T(8,128)} %get-tuple-element.74.b1, ...), custom_call_target="tpu_custom_call" | custom-call | flops 1509949440 | bytes 11796480 | tf_op jit(solution)/shard_map/gate_out/pallas_call | solution.py:174
  120.0 1.1 copy-done.8
  121.1 1.1 copy-done.9
  122.2 0.9 copy-done.10
  123.1 2.7 constant_dynamic-slice_fusion
  126.3 1.1 collective-permute-done.11.c2_h
  127.4 0.6 reshape.132
  128.0 0.6 pad_maximum_fusion.5.refs_35_
  128.6 0.6 pad_maximum_fusion.6.refs_32_
  129.3 4.0 %convert_add_fusion.mid_h = f32[640,1024]{1,0:T(8,128)} fusion(bf16[640,1024]{1,0:T(8,128)(2,1)S(1)} %copy-done.26, bf16[640,1024]{1,0:T(8,128)(2,1)} %collective-permute-done.9, bf16[1280,1024]{1,0:T(8,128)(2,1)} %get-tuple-element.84, s32[]{:T(128)S(6)} %select_n.137), kind=kLoop, calls=%fused_computation | loop fusion | flops 3276800 | bytes 6553604 | tf_op jit(solution)/shard_map/add | solution.py:1038
  133.2 71.7 %mlp_phase.1 = (f32[640,1024]{1,0:T(8,128)}, bf16[1280,1024]{1,0:T(8,128)(2,1)}, f32[1,1024]{1,0:T(1,128)}, bf16[1024,704]{1,0:T(8,128)(2,1)}, bf16[1024,704]{1,...) custom-call(f32[640,1024]{1,0:T(8,128)} %convert_add_fusion.mid_h, ...), custom_call_target="tpu_custom_call" | custom-call | flops 33218887680 | bytes 60000000 | tf_op jit(solution)/shard_map/mlp_phase/pallas_call | solution.py:393
  204.9 1.0 collective-permute-start.13
  206.5 135.3 %back_phase.1 = (f32[640,1024]{1,0:T(8,128)}, f32[704,128]{1,0:T(8,128)}, f32[704,128]{1,0:T(8,128)}, f32[704,128]{1,0:T(8,128)}, f32[256,128]{1,0:T(8,128)}, /*...) custom-call(bf16[1280,1024]{1,0:T(8,128)(2,1)} %get-tuple-element.88, ...), custom_call_target="tpu_custom_call" | custom-call | flops 40000000000 | bytes 60000000 | tf_op jit(solution)/shard_map/back_phase/pallas_call | solution.py:921
  341.8 4.0 %add_convert_fusion = bf16[640,1024]{1,0:T(8,128)(2,1)} fusion(f32[640,1024]{1,0:T(8,128)} %convert_add_fusion.mid_h, bf16[640,1024]{1,0:T(8,128)(2,1)} %collective-permute-done.13, bf16[640,1024]{1,0:T(8,128)(2,1)S(1)} %copy-done.28), kind=kLoop, calls=%fused_computation.7 | loop fusion | flops 3276800 | bytes 6553600 | tf_op jit(solution)/shard_map/convert_element_type | solution.py:1042
  345.9 1.5 copy.61
  347.4 0.6 copy.62
  348.0 0.6 copy.63
  348.7 0.6 copy.64
  349.3 0.7 copy.65
  349.9 0.7 copy.66
  350.6 0.6 copy.67
  351.2 0.6 copy.68
  353.0 0.7 copy.71
  354.3 0.7 copy.73
  355.0 0.7 copy.74
  355.7 0.7 copy.75
  (144 shorter events, 5.6 us)
Async XLA Ops:
  0.6 2.5 copy-start.25
  1.4 2.1 copy-start.45
  3.1 1.0 copy-start.34
  3.1 1.7 copy-start.29
  3.1 2.6 copy-start.35
  3.5 2.9 copy-start.30
  3.5 42.2 %collective-permute-start = (bf16[640,1024]{1,0:T(8,128)(2,1)S(1)}, bf16[640,1024]{1,0:T(8,128)(2,1)}, u32[]{:S(2)}, u32[]{:S(2)}) collective-permute-start(bf16[640,1024]{1,0:T(8,128)(2,1)S(1)} %fusion.2), channel_id=1, source_target_pairs={{0,1},{1,0},{2,3},{3,2},{4,5},{5,4},{6,7},{7,6},{8,9},{9,8},{10,11... | collective-permute-start | bytes 3932168 | tf_op jit(solution)/shard_map/ppermute | solution.py:934
  5.7 5.9 %copy-start.3 = (bf16[256,1024]{1,0:T(8,128)(2,1)S(1)}, bf16[256,1024]{1,0:T(8,128)(2,1)}, u32[]{:S(2)}) copy-start(bf16[256,1024]{1,0:T(8,128)(2,1)} %refs_25_.1) | copy-start | bytes 1572868
  6.5 30.3 %copy-start.43 = (bf16[1024,16]{0,1:T(8,128)(2,1)S(1)}, bf16[1024,16]{0,1:T(8,128)(2,1)}, u32[]{:S(2)}) copy-start(bf16[1024,16]{0,1:T(8,128)(2,1)} %param.25) | copy-start | bytes 98308
  6.5 31.1 %copy-start.51 = (bf16[512]{0:T(512)(128)(2,1)S(1)}, bf16[512]{0:T(512)(128)(2,1)}, u32[]{:S(2)}) copy-start(bf16[512]{0:T(512)(128)(2,1)} %param.27) | copy-start | bytes 3076
  6.5 31.2 %copy-start.48 = (bf16[16,512]{1,0:T(8,128)(2,1)S(1)}, bf16[16,512]{1,0:T(8,128)(2,1)}, u32[]{:S(2)}) copy-start(bf16[16,512]{1,0:T(8,128)(2,1)} %param.26) | copy-start | bytes 49156
  8.6 29.1 %collective-permute-start.1 = (bf16[512,768]{1,0:T(8,128)(2,1)S(1)}, bf16[512,768]{1,0:T(8,128)(2,1)}, u32[]{:S(2)}, u32[]{:S(2)}) collective-permute-start(bf16[512,768]{1,0:T(8,128)(2,1)S(1)} %constant_dynamic-slice_fusion.2), channel_id=1, source_target_pairs={{0,2},{1,3},{2,0},{3,1},{4,6},{5,7},{6,4},{7,5},{8,10},{9,11},{10,... | collective-permute-start | bytes 2359304 | tf_op jit(solution)/shard_map/ppermute | solution.py:934
  11.6 23.4 %collective-permute-start.3 = (bf16[128,1024]{1,0:T(8,128)(2,1)S(1)}, bf16[128,1024]{1,0:T(8,128)(2,1)S(1)}, u32[]{:S(2)}, u32[]{:S(2)}) collective-permute-start(bf16[128,1024]{1,0:T(8,128)(2,1)S(1)} %constant_dynamic-slice_fusion.1), channel_id=1, source_target_pairs={{0,2},{1,3},{2,0},{3,1},{4,6},{5,7},{6,4},{7,5},{8,10},{9,11},{10,... | collective-permute-start | bytes 786440 | tf_op jit(solution)/shard_map/ppermute | solution.py:934
  35.0 3.1 copy-start.36
  35.0 9.3 %collective-permute-start.4 = (bf16[128,1024]{1,0:T(8,128)(2,1)S(1)}, bf16[128,1024]{1,0:T(8,128)(2,1)}, u32[]{:S(2)}, u32[]{:S(2)}) collective-permute-start(bf16[128,1024]{1,0:T(8,128)(2,1)S(1)} %collective-permute-done.3), channel_id=1, source_target_pairs={{0,4},{4,0},{8,12},{12,8},{16,20},{20,16},{24,28},{28,24},{1,5},{5... | collective-permute-start | bytes 786440 | tf_op jit(solution)/shard_map/ppermute | solution.py:934
  36.9 33.7 %copy-start.6 = (bf16[1024,16]{1,0:T(8,128)(2,1)}, bf16[1024,16]{1,0:T(8,128)(2,1)S(1)}, u32[]{:S(2)}) copy-start(bf16[1024,16]{1,0:T(8,128)(2,1)S(1)} %copy.36.rd_ref.refs_36_) | copy-start | bytes 98308
  37.7 28.6 %collective-permute-start.2 = (bf16[512,768]{1,0:T(8,128)(2,1)}, bf16[512,768]{1,0:T(8,128)(2,1)S(1)}, u32[]{:S(2)}, u32[]{:S(2)}) collective-permute-start(bf16[512,768]{1,0:T(8,128)(2,1)} %collective-permute-done.1), channel_id=1, source_target_pairs={{0,4},{4,0},{8,12},{12,8},{16,20},{20,16},{24,28},{28,24},{1,5},{5... | collective-permute-start | bytes 2359304 | tf_op jit(solution)/shard_map/ppermute | solution.py:934
  45.8 67.4 %copy-start = (bf16[256,1024]{1,0:T(8,128)(2,1)}, bf16[256,1024]{1,0:T(8,128)(2,1)S(1)}, u32[]{:S(2)}) copy-start(bf16[256,1024]{1,0:T(8,128)(2,1)S(1)} %maximum_select_fusion.2.w1.refs_26_) | copy-start | bytes 1572868
  62.3 0.8 copy-start.14
  63.1 0.8 copy-start.15
  64.0 0.9 copy-start.16
  66.3 4.3 %copy-start.1 = (f32[1280,256]{1,0:T(8,128)}, f32[1280,256]{1,0:T(8,128)S(1)}, u32[]{:S(2)}) copy-start(f32[1280,256]{1,0:T(8,128)S(1)} %get-tuple-element.77.s0.refs_3_) | copy-start | bytes 3932164
  66.3 4.3 %copy-start.12 = (bf16[1280,256]{1,0:T(8,128)(2,1)}, bf16[1280,256]{1,0:T(8,128)(2,1)S(1)}, u32[]{:S(2)}) copy-start(bf16[1280,256]{1,0:T(8,128)(2,1)S(1)} %get-tuple-element.97.refs_14_) | copy-start | bytes 1966084
  66.3 4.3 %copy-start.13 = (f32[1280,128]{1,0:T(8,128)}, f32[1280,128]{1,0:T(8,128)S(1)}, u32[]{:S(2)}) copy-start(f32[1280,128]{1,0:T(8,128)S(1)} %get-tuple-element.99.refs_16_) | copy-start | bytes 1966084
  66.3 46.9 %copy-start.4 = (bf16[1280,128]{1,0:T(8,128)(2,1)}, bf16[1280,128]{1,0:T(8,128)(2,1)S(1)}, u32[]{:S(2)}) copy-start(bf16[1280,128]{1,0:T(8,128)(2,1)S(1)} %get-tuple-element.75.r0.refs_5_) | copy-start | bytes 983044
  83.4 1.1 copy-start.2
  84.5 0.9 copy-start.17
  85.3 0.8 copy-start.18
  86.2 0.9 copy-start.19
  87.1 0.9 copy-start.20
  89.4 23.8 %copy-start.5 = (bf16[1280,128]{1,0:T(8,128)(2,1)}, bf16[1280,128]{1,0:T(8,128)(2,1)S(1)}, u32[]{:S(2)}) copy-start(bf16[1280,128]{1,0:T(8,128)(2,1)S(1)} %get-tuple-element.76.r1.refs_6_) | copy-start | bytes 983044
  89.5 5.1 %collective-permute-start.5 = (bf16[2,272,128]{2,1,0:T(8,128)(2,1)S(1)}, bf16[2,272,128]{2,1,0:T(8,128)(2,1)S(1)}, u32[]{:S(2)}, u32[]{:S(2)}) collective-permute-start(bf16[2,272,128]{2,1,0:T(8,128)(2,1)S(1)} %pad_maximum_fusion.1), channel_id=1, source_target_pairs={{0,2},{1,3},{2,0},{3,1},{4,6},{5,7},{6,4},{7,5},{8,10},{9,11},{10,... | collective-permute-start | bytes 417800 | tf_op jit(solution)/shard_map/ppermute | solution.py:934
  95.3 14.0 %copy-start.53 = (bf16[256]{0:T(256)(128)(2,1)S(1)}, bf16[256]{0:T(256)(128)(2,1)}, u32[]{:S(2)}) copy-start(bf16[256]{0:T(256)(128)(2,1)} %param.28) | copy-start | bytes 1540
  95.3 5.1 %collective-permute-start.6 = (bf16[2,272,128]{2,1,0:T(8,128)(2,1)S(1)}, bf16[2,272,128]{2,1,0:T(8,128)(2,1)S(1)}, u32[]{:S(2)}, u32[]{:S(2)}) collective-permute-start(bf16[2,272,128]{2,1,0:T(8,128)(2,1)S(1)} %pad_maximum_fusion.2), channel_id=1, source_target_pairs={{0,4},{4,0},{8,12},{12,8},{16,20},{20,16},{24,28},{28,24},{1,5},{5... | collective-permute-start | bytes 417800 | tf_op jit(solution)/shard_map/ppermute | solution.py:934
  100.6 5.2 %collective-permute-start.7 = (bf16[2,272,128]{2,1,0:T(8,128)(2,1)S(1)}, bf16[2,272,128]{2,1,0:T(8,128)(2,1)S(1)}, u32[]{:S(2)}, u32[]{:S(2)}) collective-permute-start(bf16[2,272,128]{2,1,0:T(8,128)(2,1)S(1)} %pad_maximum_fusion.3), channel_id=1, source_target_pairs={{0,8},{4,12},{8,0},{12,4},{16,24},{20,28},{24,16},{28,20},{1,9},{5... | collective-permute-start | bytes 417800 | tf_op jit(solution)/shard_map/ppermute | solution.py:934
  102.4 25.0 %collective-permute-start.11 = (bf16[640,1024]{1,0:T(8,128)(2,1)}, bf16[640,1024]{1,0:T(8,128)(2,1)}, u32[]{:S(2)}, u32[]{:S(2)}) collective-permute-start(bf16[640,1024]{1,0:T(8,128)(2,1)} %c0_h.1), channel_id=1, source_target_pairs={{0,2},{1,3},{2,0},{3,1},{4,6},{5,7},{6,4},{7,5},{8,10},{9,11},{10,... | collective-permute-start | bytes 3932168 | tf_op jit(solution)/shard_map/ppermute | solution.py:934
  105.9 6.4 %collective-permute-start.8 = (bf16[2,272,128]{2,1,0:T(8,128)(2,1)S(1)}, bf16[2,272,128]{2,1,0:T(8,128)(2,1)S(1)}, u32[]{:S(2)}, u32[]{:S(2)}) collective-permute-start(bf16[2,272,128]{2,1,0:T(8,128)(2,1)S(1)} %pad_maximum_fusion.4), channel_id=1, source_target_pairs={{0,16},{4,20},{8,24},{12,28},{16,0},{20,4},{24,8},{28,12},{1,17},{... | collective-permute-start | bytes 417800 | tf_op jit(solution)/shard_map/ppermute | solution.py:934
  109.3 10.7 %copy-start.7 = (f32[256]{0:T(256)}, f32[256]{0:T(256)S(1)}, u32[]{:S(2)}) copy-start(f32[256]{0:T(256)S(1)} %reshape.130) | copy-start | bytes 3076
  120.0 1.1 copy-start.8
  121.1 1.1 copy-start.9
  122.2 0.9 copy-start.10
  123.0 10.2 %copy-start.11 = (bf16[1280,256]{1,0:T(8,128)(2,1)}, bf16[1280,256]{1,0:T(8,128)(2,1)S(1)}, u32[]{:S(2)}) copy-start(bf16[1280,256]{1,0:T(8,128)(2,1)S(1)} %get-tuple-element.92.refs_8_) | copy-start | bytes 1966084
  123.0 4.4 %copy-start.49 = (bf16[1024]{0:T(1024)(128)(2,1)S(1)}, bf16[1024]{0:T(1024)(128)(2,1)}, u32[]{:S(2)}) copy-start(bf16[1024]{0:T(1024)(128)(2,1)} %param.30) | copy-start | bytes 6148
  123.0 6.2 %copy-start.26 = (bf16[640,1024]{1,0:T(8,128)(2,1)S(1)}, bf16[640,1024]{1,0:T(8,128)(2,1)}, u32[]{:S(2)}) copy-start(bf16[640,1024]{1,0:T(8,128)(2,1)} %refs_31_.1) | copy-start | bytes 3932164
  125.8 3.5 collective-permute-start.9
  125.8 7.5 %collective-permute-start.10 = (bf16[640,1024]{1,0:T(8,128)(2,1)}, bf16[640,1024]{1,0:T(8,128)(2,1)}, u32[]{:S(2)}, u32[]{:S(2)}) collective-permute-start(bf16[640,1024]{1,0:T(8,128)(2,1)} %c0_h.1), channel_id=1, source_target_pairs={{0,1},{1,0},{2,3},{3,2},{4,5},{5,4},{6,7},{7,6},{8,9},{9,8},{10,11... | collective-permute-start | bytes 3932168 | tf_op jit(solution)/shard_map/ppermute | solution.py:934
  127.4 5.8 %collective-permute-start.12 = (bf16[640,1024]{1,0:T(8,128)(2,1)}, bf16[640,1024]{1,0:T(8,128)(2,1)}, u32[]{:S(2)}, u32[]{:S(2)}) collective-permute-start(bf16[640,1024]{1,0:T(8,128)(2,1)} %collective-permute-done.11.c2_h), channel_id=1, source_target_pairs={{0,1},{1,0},{2,3},{3,2},{4,5},{5,4},{6,7},{7,6},{8,9},{9,8},{10,11... | collective-permute-start | bytes 3932168 | tf_op jit(solution)/shard_map/ppermute | solution.py:934
  204.9 136.9 %collective-permute-start.13 = (bf16[640,1024]{1,0:T(8,128)(2,1)}, bf16[640,1024]{1,0:T(8,128)(2,1)}, u32[]{:S(2)}, u32[]{:S(2)}) collective-permute-start(bf16[640,1024]{1,0:T(8,128)(2,1)} %get-tuple-element.87), channel_id=1, source_target_pairs={{0,2},{1,3},{2,0},{3,1},{4,6},{5,7},{6,4},{7,5},{8,10},{9,11},{10,... | collective-permute-start | bytes 3932168 | tf_op jit(solution)/shard_map/ppermute | solution.py:934
  206.5 135.4 %copy-start.28 = (bf16[640,1024]{1,0:T(8,128)(2,1)S(1)}, bf16[640,1024]{1,0:T(8,128)(2,1)}, u32[]{:S(2)}) copy-start(bf16[640,1024]{1,0:T(8,128)(2,1)} %get-tuple-element.86) | copy-start | bytes 3932164
  341.8 4.0 %copy-start.27 = (f32[640,1024]{1,0:T(8,128)S(1)}, f32[640,1024]{1,0:T(8,128)}, u32[]{:S(2)}) copy-start(f32[640,1024]{1,0:T(8,128)} %get-tuple-element.165) | copy-start | bytes 7864324
  345.8 1.6 copy-start.47
  345.8 2.2 copy-start.42
  345.8 2.8 copy-start.41
  345.8 3.5 copy-start.39
  345.8 4.1 %copy-start.38 = (f32[128,256]{1,0:T(8,128)S(1)}, f32[128,256]{1,0:T(8,128)}, u32[]{:S(2)}) copy-start(f32[128,256]{1,0:T(8,128)} %get-tuple-element.170) | copy-start | bytes 393220
  345.9 4.8 %copy-start.40 = (f32[16,1024]{1,0:T(8,128)S(1)}, f32[16,1024]{1,0:T(8,128)}, u32[]{:S(2)}) copy-start(f32[16,1024]{1,0:T(8,128)} %get-tuple-element.119) | copy-start | bytes 196612
  345.9 5.4 %copy-start.44 = (f32[16,512]{1,0:T(8,128)S(1)}, f32[16,512]{1,0:T(8,128)}, u32[]{:S(2)}) copy-start(f32[16,512]{1,0:T(8,128)} %get-tuple-element.172) | copy-start | bytes 98308
  345.9 6.0 %copy-start.50 = (f32[1,512]{1,0:T(1,128)S(1)}, f32[1,512]{1,0:T(1,128)}, u32[]{:S(2)}) copy-start(f32[1,512]{1,0:T(1,128)} %get-tuple-element.121) | copy-start | bytes 6148
  345.9 6.6 %copy-start.52 = (f32[1,256]{1,0:T(1,128)S(1)}, f32[1,256]{1,0:T(1,128)}, u32[]{:S(2)}) copy-start(f32[1,256]{1,0:T(1,128)} %get-tuple-element.122) | copy-start | bytes 3076
  345.9 7.1 %copy-start.37 = (f32[256,128]{1,0:T(8,128)S(1)}, f32[256,128]{1,0:T(8,128)}, u32[]{:S(2)}) copy-start(f32[256,128]{1,0:T(8,128)} %get-tuple-element.175) | copy-start | bytes 393220
  345.9 7.8 %copy-start.46 = (f32[1,1024]{1,0:T(1,128)S(1)}, f32[1,1024]{1,0:T(1,128)}, u32[]{:S(2)}) copy-start(f32[1,1024]{1,0:T(1,128)} %get-tuple-element.124) | copy-start | bytes 12292
  345.9 8.3 %copy-start.33 = (f32[704,128]{1,0:T(8,128)S(1)}, f32[704,128]{1,0:T(8,128)}, u32[]{:S(2)}) copy-start(f32[704,128]{1,0:T(8,128)} %get-tuple-element.125) | copy-start | bytes 1081348
  347.4 7.6 %copy-start.32 = (f32[704,128]{1,0:T(8,128)S(1)}, f32[704,128]{1,0:T(8,128)}, u32[]{:S(2)}) copy-start(f32[704,128]{1,0:T(8,128)} %get-tuple-element.126) | copy-start | bytes 1081348
  347.4 8.3 %copy-start.31 = (f32[704,128]{1,0:T(8,128)S(1)}, f32[704,128]{1,0:T(8,128)}, u32[]{:S(2)}) copy-start(f32[704,128]{1,0:T(8,128)} %get-tuple-element.179) | copy-start | bytes 1081348
  (4 other events, 2.9 us)
where the time goes:
time: 360 us; the launch traced here: 356 us
  Pallas kernels  240 us (67%)
  waiting for transfers between devices  42 us (12%)
  local copies, waits for them, and re-layouts  31.6 us (9%)
  other arithmetic  23.7 us (7%)
  starting transfers between devices  17.7 us (5%)
    pallas_call x1, Pallas kernels, back_phase(): pl.pallas_call(kernel, name='back_phase', in_specs=[hbm] * (n_in - n_vmem...  135 us
    pallas_call x1, Pallas kernels, mlp_phase(): pl.pallas_call(mlp_phase_kernel, name='mlp_phase', in_specs=[hbm] * 8 + [...  71.7 us
    ppermute x14, waiting for transfers between devices, hop(): lax.ppermute(value, axis, [(i, i ^ bit) for i in range(lax.axis_size(axis...  42 us
    unnamed x128, local copies, waits for them, and re-layouts  26.2 us
    pallas_call x2, Pallas kernels, forward_head(): pl.pallas_call(forward_head_kernel, name='forward_head', grid=(n // BLOCK...  25.7 us
    ppermute x14, starting transfers between devices, hop(): lax.ppermute(value, axis, [(i, i ^ bit) for i in range(lax.axis_size(axis...  17.7 us
  transfers between devices with their start and end apart: 14, of which 7 were waited for; matrix products, arithmetic and copies ran while one was open for 6% of the time, Pallas kernels for 43%

commit v1 on v0

--- a/solution.py
+++ b/solution.py
@@ -1,3 +1,4 @@
+import functools
 import itertools
 
 import jax
@@ -63,125 +64,475 @@
     return r >= c if lower else r <= c
 
 
-def forward_head_kernel(
-    x_ref, w_ref, rd_ref, ru_ref, bias_ref,
-    q_ref, k_ref, v_ref, s_ref, cum_ref, dpre_ref, rank_ref, base_ref, reach_ref, sin_ref, off_ref,
-    state_ref, mult_ref,
-    st, off,
+class Wires:
+    def __init__(self, send_sem, recv_sem):
+        self.send_sem, self.recv_sem, self.used, self.all = send_sem, recv_sem, 0, []
+
+    def copy(self, src, dst, target):
+        made = pltpu.make_async_remote_copy(
+            src,
+            dst,
+            self.send_sem.at[self.used],
+            self.recv_sem.at[self.used],
+            device_id=target,
+            device_id_type=MESH,
+        )
+        self.used += 1
+        self.all.append(made)
+        return made
+
+    def drain(self):
+        for made in self.all:
+            made.wait_send()
+
+
+class Places:
+    def __init__(self, wide_count):
+        self.wide, self.place = lax.axis_index("wide"), lax.axis_index("narrow")
+        self.core = self.place % 2
+        self.second = self.place // 2
+        self.by_core = (self.wide, self.place + 1 - 2 * self.core)
+        self.by_row = (self.wide, (self.place + 2) % 4)
+        self.bits = []
+        bit = 1
+        while bit < wide_count:
+            self.bits.append(bit)
+            bit *= 2
+
+    def has(self, bit):
+        return (self.wide // bit) % 2
+
+    def across(self, bit):
+        return (self.wide + bit - 2 * bit * self.has(bit), self.place)
+
+    def meet(self):
+        barrier = pltpu.get_barrier_semaphore()
+        others = [self.by_core, self.by_row] + [self.across(bit) for bit in self.bits]
+        for other in others:
+            pl.semaphore_signal(barrier, 1, device_id=other, device_id_type=MESH)
+        pl.semaphore_wait(barrier, len(others))
+
+
+class Scan:
+    def __init__(self, where, wires, tot_s, tot_m, pre_s, pre_m, out, into, backward):
+        self.tot_s, self.tot_m, self.pre_s, self.pre_m = tot_s, tot_m, pre_s, pre_m
+        self.out, self.into = out, into
+        self.steps = []
+        for i, bit in enumerate([0] + where.bits):
+            target = where.across(bit) if bit else where.by_row
+            is_set = where.has(bit) if bit else where.second
+            later = (1 - is_set if backward else is_set) > 0
+            self.steps.append((wires.copy(out.at[i], into.at[i], target), later, bit == 0))
+        pre_s[...] = jnp.zeros_like(pre_s)
+        pre_m[...] = jnp.ones_like(pre_m)
+
+    def begin(self, i=0):
+        self.at = i
+        dv = self.tot_s.shape[1]
+        for h in range(2):
+            self.out[i, h, :dv, :] = self.tot_s[h].astype(BF16)
+            self.out[i, h, dv:, :] = jnp.broadcast_to(self.tot_m[h], (16, self.tot_m.shape[2])).astype(BF16)
+        self.steps[i][0].start()
+
+    def advance(self):
+        self.finish(self.at)
+        if self.at + 1 < len(self.steps):
+            self.begin(self.at + 1)
+            return True
+        return False
+
+    def finish(self, i):
+        copy, later, swapped = self.steps[i]
+        copy.wait_recv()
+        dv = self.tot_s.shape[1]
+        for h in range(2):
+            g = 1 - h if swapped else h
+            oth_s = self.into[i, g, :dv, :].astype(F32)
+            oth_m = self.into[i, g, dv : dv + 1, :].astype(F32)
+            pre_s, pre_m, tot_s, tot_m = self.pre_s[h], self.pre_m[h], self.tot_s[h], self.tot_m[h]
+            self.pre_s[h] = jnp.where(later, oth_s * pre_m + pre_s, pre_s)
+            self.pre_m[h] = jnp.where(later, oth_m * pre_m, pre_m)
+            self.tot_s[h] = jnp.where(later, oth_s * tot_m + tot_s, tot_s * oth_m + oth_s)
+            self.tot_m[h] = tot_m * oth_m
+
+
+class Scatter:
+    def __init__(self, where, wires, source, keep, order, recvs):
+        self.recvs, self.steps = recvs, []
+        left = sorted(where.bits, reverse=True)
+        held, first = source, keep
+        for bit, recv in zip(order, recvs):
+            dim = left.index(bit)
+            mine = where.has(bit)
+            other = held.at[(slice(None),) * dim + (1 - mine,)]
+            self.steps.append((wires.copy(other, recv, where.across(bit)), first if first is not None else held, dim, mine, first is not None))
+            left.pop(dim)
+            held, first = recv, None
+
+    def begin(self, i=0):
+        self.at = i
+        self.steps[i][0].start()
+
+    def advance(self):
+        if self.at + 1 < len(self.steps):
+            self.finish(self.at)
+            self.begin(self.at + 1)
+
+    def result(self):
+        while self.at + 1 < len(self.steps):
+            self.advance()
+        return self.finish(self.at)
+
+    def finish(self, i):
+        copy, held, dim, mine, picked = self.steps[i]
+        copy.wait_recv()
+        recv = self.recvs[i]
+        last = i == len(self.steps) - 1
+        for at in itertools.product(range(2), repeat=len(recv.shape) - 2):
+            source = at if picked else at[:dim] + (mine,) + at[dim:]
+            total = recv[at].astype(F32) + held[source].astype(F32)
+            if last:
+                return total
+            recv[at] = total.astype(BF16)
+        return None
+
+
+class Everywhere:
+    def __init__(self, where, wires, values, recvs):
+        self.values, self.recvs = values, recvs
+        targets = [where.by_core, where.by_row] + [where.across(bit) for bit in where.bits]
+        self.steps = [wires.copy(values.at[i], recvs.at[i], target) for i, target in enumerate(targets)]
+
+    def begin(self, i=0):
+        self.at = i
+        self.steps[i].start()
+
+    def advance(self):
+        if self.at + 1 < len(self.steps):
+            self.finish(self.at)
+            self.begin(self.at + 1)
+
+    def result(self):
+        while self.at + 1 < len(self.steps):
+            self.advance()
+        self.finish(self.at)
+        return self.values[len(self.steps)]
+
+    def finish(self, i):
+        self.steps[i].wait_recv()
+        self.values[i + 1] = self.values[i] + self.recvs[i]
+
+
+def bit_index(w, bits):
+    return tuple((w // bit) % 2 for bit in sorted(bits, reverse=True))
+
+
+def front_phase_kernel(
+    bits,
+    tok_h, cot_h, kw_h, vw_h, qw_h, sw_h, wo_h, rd_ref, ru_ref, bias_ref, ggain_ref, ngain_ref, restart_ref,
+    mid_h, rows_h, q_h, k_h, v_h, s_h, cum_h, dpre_h, rank_h, reach_h, sin_h, mx_h, gated_h, w_h, wo2_h, c1_h, c2_h, c3_h,
+    off_o, enter_o, mult_o,
+    tok, rows, w, wo, q, k, v, sw, cum, dpre, rank, reach, sin, mx, gated, tb, tr, mid, st, off,
+    tot_s, tot_m, pre_s, pre_m, sc_out, sc_in,
+    load_sem, send_sem, recv_sem, out_sem,
 ):
-    i = pl.program_id(0)
-    dk = q_ref.shape[1]
-    dv = v_ref.shape[1]
-
-    @pl.when(i == 0)
-    def _():
-        st[...] = jnp.zeros_like(st)
-        off[...] = jnp.zeros_like(off)
-
-    x = x_ref[...]
-    proj = dot(x, w_ref[...])
-    rank = dot(x, rd_ref[...])
-    dpre = exact(rank, ru_ref[...], ((1,), (0,))) + bias_ref[...]
-    dlog = jax.nn.log_sigmoid(dpre) * (1.0 / GATE_NORM)
-    k_low = proj[:, :dk].astype(BF16)
-    v_low = proj[:, dk : dk + dv].astype(BF16)
-    q_low = proj[:, dk + dv : 2 * dk + dv].astype(BF16)
-    q_ref[...] = q_low
-    k_ref[...] = k_low
-    v_ref[...] = v_low
-    s_ref[...] = proj[:, 2 * dk + dv :]
-    rank_ref[...] = rank
-    dpre_ref[...] = dpre
+    count, d = rows.shape
+    half = count // 2
+    blk = half // 2
+    dk, dv = q.shape[2], v.shape[2]
+    kv = dk + dv
+    where = Places(2 ** len(bits))
+    wires = Wires(send_sem, recv_sem)
+    loads, stores = [], []
+
+    def load(src, dst):
+        copy = pltpu.make_async_copy(src, dst, load_sem.at[len(loads)])
+        loads.append(copy)
+        copy.start()
+        return copy
+
+    def store(src, dst):
+        copy = pltpu.make_async_copy(src, dst, out_sem.at[len(stores)])
+        stores.append(copy)
+        copy.start()
+
+    load_tok = load(tok_h, tok)
+    load_kv = [load(kw_h, w.at[0, :, pl.ds(0, dk)]), load(vw_h, w.at[0, :, pl.ds(dk, dv)])]
+    load_qs = [load(qw_h, w.at[0, :, pl.ds(kv, dk)]), load(sw_h, w.at[0, :, pl.ds(kv + dk, dv)])]
+    load_wo = load(wo_h, wo.at[0])
+
+    where.meet()
+
+    odd = where.has(1)
+    over_x = where.across(1)
+    quarter = d // 4
+
+    def weight_pieces(cols):
+        made = []
+        for i in range(2):
+            near = pl.ds(pl.multiple_of(odd * 2 * quarter + i * quarter, quarter), quarter)
+            made.append(
+                (
+                    wires.copy(w.at[0, near, cols], w.at[1, near, cols], where.by_row),
+                    wires.copy(w.at[1, near, cols], w.at[1, near, cols], over_x),
+                )
+            )
+        return made
+
+    kv_in = weight_pieces(pl.ds(0, kv))
+    qs_in = weight_pieces(pl.ds(kv, kv))
+    near = pl.ds(pl.multiple_of(odd * (dv // 2), dv // 2), dv // 2)
+    wo_in = [
+        wires.copy(wo.at[0, near], wo.at[1, near], where.by_row),
+        wires.copy(wo.at[1, near], wo.at[1, near], over_x),
+    ]
+    cot_row, cot_both = [], []
+    for i in range(2):
+        at = pl.ds(i * blk, blk)
+        cot_row.append(wires.copy(cot_h.at[at], c2_h.at[at], where.by_row))
+        cot_both.append(wires.copy(c2_h.at[at], c3_h.at[at], where.by_core))
+    cot_core = wires.copy(cot_h, c1_h, where.by_core)
+    row_out = []
+    for i in range(2):
+        at = pl.ds(pl.multiple_of(where.core * half + i * blk, blk), blk)
+        row_out.append(wires.copy(rows.at[at], rows.at[at], where.by_core))
+    terms = [wires.copy(tb.at[j], tr.at[j], where.by_core) for j in range(2)]
+    scan = Scan(where, wires, tot_s, tot_m, pre_s, pre_m, sc_out, sc_in, False)
+
+    for copy in load_kv:
+        copy.wait()
+    for piece in kv_in:
+        piece[0].start()
+    load_tok.wait()
+    ngain = ngain_ref[...]
+    for i in range(2):
+        x = tok[pl.ds(i * blk, blk), :].astype(F32)
+        inv = lax.rsqrt(jnp.mean(x * x, axis=-1, keepdims=True) + NORM_EPS)
+        rows[pl.ds(pl.multiple_of(where.core * half + i * blk, blk), blk), :] = (x * inv * ngain).astype(BF16)
+        row_out[i].start()
+    for copy in load_qs:
+        copy.wait()
+    load_wo.wait()
+    for copy in row_out:
+        copy.wait_recv()
+    cot_core.start()
+    store(rows, rows_h)
+
     mask = triangle(True)
     ones = mask.astype(F32)
     scale = dk**-0.5
-    for j in range(BLOCK // CHUNK):
-        rows = slice(j * CHUNK, (j + 1) * CHUNK)
-        cum = exact(ones, dlog[rows], ((1,), (0,)))
-        mid = cum[HALF - 1 : HALF]
-        end = cum[CHUNK - 1 :]
-        qf = q_low[rows].astype(F32) * scale
-        kf = k_low[rows].astype(F32)
-        v = v_low[rows]
-        qd = (qf * jnp.exp(cum - mid)).astype(BF16)
-        kd = (kf * jnp.exp(mid - cum)).astype(BF16)
-        qi = (qf * jnp.exp(cum)).astype(BF16)
-        ke = (kf * jnp.exp(end - cum)).astype(BF16)
-        scores = jnp.where(mask, dot_nt(qd, kd), 0.0).astype(BF16)
-        state = st[...]
-        state_low = state.astype(BF16)
-        offset = off[...]
-        base_ref[rows, :] = dot(scores, v) + dot_nt(qi, state_low)
-        reach_ref[rows, :] = (qf * jnp.exp(cum + offset)).astype(BF16)
-        cum_ref[rows, :] = cum
-        sin_ref[j] = state_low
-        off_ref[j] = offset
-        st[...] = state * jnp.exp(end) + dot_tn(v, ke)
-        off[...] = offset + end
-    state_ref[...] = st[...]
-    mult_ref[...] = jnp.exp(off[...])
-
-
-def forward_head(x, w, rank_down, rank_cols, bias_cols, dk, dv):
-    n, d = x.shape
-    rank = rank_down.shape[1]
+    blocks = count // BLOCK
     per = BLOCK // CHUNK
+
+    def first_step(i, _):
+        h, b = i // blocks, i % blocks
+        at = pl.ds(pl.multiple_of(b * BLOCK, BLOCK), BLOCK)
+        for p in range(2):
+
+            @pl.when(i == blocks - 2 + p)
+            def _():
+                kv_in[p][0].wait_recv()
+                kv_in[p][1].start()
+
+            @pl.when(i == 2 * blocks - 2 + p)
+            def _():
+                qs_in[p][0].wait_recv()
+                qs_in[p][1].start()
+
+        @pl.when(i == blocks - 1)
+        def _():
+            for piece in qs_in:
+                piece[0].start()
+            cot_row[0].start()
+
+        @pl.when(i == blocks)
+        def _():
+            for piece in kv_in:
+                piece[1].wait_recv()
+
+        @pl.when(b == 0)
+        def _():
+            st[...] = jnp.zeros_like(st)
+            off[...] = jnp.zeros_like(off)
+
+        x = rows[at, :]
+
+        @pl.when(i < blocks)
+        def _():
+            rank[at, :] = dot(x, rd_ref[...])
+
+        proj = dot(x, w[h, :, :kv])
+        pre = exact(rank[at, :], ru_ref[h], ((1,), (0,))) + bias_ref[h]
+        dlog = jax.nn.log_sigmoid(pre) * (1.0 / GATE_NORM)
+        k_low = proj[:, :dk].astype(BF16)
+        v_low = proj[:, dk:].astype(BF16)
+        k[h, at, :] = k_low
+        v[h, at, :] = v_low
+        dpre[h, at, :] = pre
+        for j in range(per):
+            part = slice(j * CHUNK, (j + 1) * CHUNK)
+            c = b * per + j
+            ch = exact(ones, dlog[part], ((1,), (0,)))
+            end = ch[CHUNK - 1 :]
+            ke = (k_low[part].astype(F32) * jnp.exp(end - ch)).astype(BF16)
+            state = st[...]
+            offset = off[...]
+            cum[h, pl.ds(pl.multiple_of(c * CHUNK, CHUNK), CHUNK), :] = ch
+            sin[h, c] = state.astype(BF16)
+            off_o[h, c] = offset
+            st[...] = state * jnp.exp(end) + dot_tn(v_low[part], ke)
+            off[...] = offset + end
+
+        @pl.when(b == blocks - 1)
+        def _():
+            tot_s[h] = st[...]
+            mult = restart_ref[...] * jnp.exp(off[...])
+            tot_m[h] = mult
+            mult_o[h] = mult
+
+        return 0
+
+    lax.fori_loop(0, 2 * blocks, first_step, 0)
+    scan.begin()
+    wo_in[0].start()
+    cot_row[1].start()
+    for src, dst in ((k, k_h), (v, v_h), (cum, cum_h), (dpre, dpre_h), (rank, rank_h), (sin, sin_h)):
+        store(src, dst)
+
+    def second_step(i, _):
+        h, b = i // blocks, i % blocks
+        at = pl.ds(pl.multiple_of(b * BLOCK, BLOCK), BLOCK)
+
+        @pl.when(i == blocks)
+        def _():
+            for piece in qs_in:
+                piece[1].wait_recv()
+
+        for n in range(min(len(bits), 3)):
+
+            @pl.when(i == 2 + 3 * n)
+            def _():
+                scan.advance()
+
+        @pl.when(i == 2 * blocks - 1)
+        def _():
+            wo_in[0].wait_recv()
+            wo_in[1].start()
+
+        proj = dot(rows[at, :], w[h, :, kv:])
+        q_low = proj[:, :dk].astype(BF16)
+        q[h, at, :] = q_low
+        sw[h, at, :] = proj[:, dk:]
+        for j in range(per):
+            part = slice(j * CHUNK, (j + 1) * CHUNK)
+            c = b * per + j
+            this = pl.ds(pl.multiple_of(c * CHUNK, CHUNK), CHUNK)
+            ch = cum[h, this, :]
+            mid_row = ch[HALF - 1 : HALF]
+            qf = q_low[part].astype(F32) * scale
+            kf = k[h, this, :].astype(F32)
+            qd = (qf * jnp.exp(ch - mid_row)).astype(BF16)
+            kd = (kf * jnp.exp(mid_row - ch)).astype(BF16)
+            qi = (qf * jnp.exp(ch)).astype(BF16)
+            scores = jnp.where(mask, dot_nt(qd, kd), 0.0).astype(BF16)
+            mx[h, this, :] = dot(scores, v[h, this, :]) + dot_nt(qi, sin[h, c])
+            reach[h, this, :] = (qf * jnp.exp(ch + off_o[h, c])).astype(BF16)
+        return 0
+
+    lax.fori_loop(0, 2 * blocks, second_step, 0)
+    for src, dst in ((q, q_h), (sw, s_h), (reach, reach_h), (w, w_h)):
+        store(src, dst)
+    while scan.advance():
+        pass
+    for h in range(2):
+        enter_o[h] = restart_ref[...] * pre_s[h]
+    wo_in[1].wait_recv()
+    store(wo, wo2_h)
+    gain = ggain_ref[...]
+
+    def gate_step(i, _):
+        b = jnp.where(i < 2, 2 - 2 * where.core + i, 2 * where.core + i - 2)
+        at = pl.ds(pl.multiple_of(b * blk, blk), blk)
+        total = None
+        for h in range(2):
+            mixed = mx[h, at, :] + dot_nt(reach[h, at, :], enter_o[h].astype(BF16))
+            inv = lax.rsqrt(jnp.mean(mixed * mixed, axis=-1, keepdims=True) + GROUP_EPS)
+            s = sw[h, at, :]
+            g = (mixed * inv * gain * (s * jax.nn.sigmoid(s))).astype(BF16)
+            mx[h, at, :] = mixed
+            gated[h, at, :] = g
+            part = dot(g, wo[h])
+            total = part if total is None else total + part
+        for j in range(2):
+
+            @pl.when(i == j)
+            def _():
+                tb[j] = total.astype(BF16)
+                terms[j].start()
+
+            @pl.when(i == 2 + j)
+            def _():
+                mid[pl.ds(j * blk, blk), :] = tok[pl.ds(j * blk, blk), :].astype(F32) + total
+
+        return 0
+
+    lax.fori_loop(0, 4, gate_step, 0)
+    for i in range(2):
+        cot_row[i].wait_recv()
+        cot_both[i].start()
+    for src, dst in ((mx, mx_h), (gated, gated_h)):
+        store(src, dst)
+    for j in range(2):
+        at = pl.ds(j * blk, blk)
+        terms[j].wait_recv()
+        mid[at, :] += tr[j].astype(F32)
+    store(mid, mid_h)
+    cot_core.wait_recv()
+    for copy in cot_both:
+        copy.wait_recv()
+    for copy in stores:
+        copy.wait()
+    wires.drain()
+
+
+def front_phase(tokens, cotangent, kw, vw, qw, sw, wo, rd, ru, bias, ggain, ngain, restart):
+    bits = wide_bits()
+    half, d = tokens.shape
+    count = 2 * half
+    dk, dv, rk = kw.shape[1], vw.shape[1], rd.shape[1]
+    chunks, n_bits = count // CHUNK, len(bits)
+    hbm = pl.BlockSpec(memory_space=pltpu.HBM)
+    vmem = pl.BlockSpec(memory_space=pltpu.VMEM)
+    dma = pltpu.SemaphoreType.DMA
+    v_ = pltpu.VMEM
+    out_shape = [
+        sds((half, d), F32), sds((count, d), BF16), sds((2, count, dk), BF16), sds((2, count, dk), BF16),
+        sds((2, count, dv), BF16), sds((2, count, dv), F32), sds((2, count, dk), F32), sds((2, count, dk), F32),
+        sds((count, rk), F32), sds((2, count, dk), BF16), sds((2, chunks, dv, dk), BF16), sds((2, count, dv), F32),
+        sds((2, count, dv), BF16), sds((2, d, 2 * dk + 2 * dv), BF16), sds((2, dv, d), BF16),
+        sds((half, d), BF16), sds((half, d), BF16), sds((half, d), BF16),
+        sds((2, chunks, 1, dk), F32), sds((2, dv, dk), F32), sds((2, 1, dk), F32),
+    ]
+    scratch = [
+        v_((half, d), BF16), v_((count, d), BF16), v_((2, d, 2 * dk + 2 * dv), BF16), v_((2, dv, d), BF16),
+        v_((2, count, dk), BF16), v_((2, count, dk), BF16), v_((2, count, dv), BF16), v_((2, count, dv), F32),
+        v_((2, count, dk), F32), v_((2, count, dk), F32), v_((count, rk), F32), v_((2, count, dk), BF16),
+        v_((2, chunks, dv, dk), BF16), v_((2, count, dv), F32), v_((2, count, dv), BF16),
+        v_((2, half // 2, d), BF16), v_((2, half // 2, d), BF16), v_((half, d), F32), v_((dv, dk), F32), v_((1, dk), F32),
+        v_((2, dv, dk), F32), v_((2, 1, dk), F32), v_((2, dv, dk), F32), v_((2, 1, dk), F32),
+        v_((n_bits + 1, 2, dv + 16, dk), BF16), v_((n_bits + 1, 2, dv + 16, dk), BF16),
+        dma((8,)), dma((32,)), dma((32,)), dma((20,)),
+    ]
     return pl.pallas_call(
-        forward_head_kernel,
-        name="forward_head",
-        grid=(n // BLOCK,),
-        in_specs=[
-            rows_spec(BLOCK, d), whole(w.shape), whole(rank_down.shape), whole(rank_cols.shape), whole(bias_cols.shape),
-        ],
-        out_specs=[
-            rows_spec(BLOCK, dk), rows_spec(BLOCK, dk), rows_spec(BLOCK, dv), rows_spec(BLOCK, dv),
-            rows_spec(BLOCK, dk), rows_spec(BLOCK, dk), rows_spec(BLOCK, rank), rows_spec(BLOCK, dv), rows_spec(BLOCK, dk),
-            pl.BlockSpec((per, dv, dk), lambda i: (i, 0, 0)), pl.BlockSpec((per, 1, dk), lambda i: (i, 0, 0)),
-            whole((dv, dk)), whole((1, dk)),
-        ],
-        out_shape=[
-            sds((n, dk), BF16), sds((n, dk), BF16), sds((n, dv), BF16), sds((n, dv), F32),
-            sds((n, dk), F32), sds((n, dk), F32), sds((n, rank), F32), sds((n, dv), F32), sds((n, dk), BF16),
-            sds((n // CHUNK, dv, dk), BF16), sds((n // CHUNK, 1, dk), F32),
-            sds((dv, dk), F32), sds((1, dk), F32),
-        ],
-        scratch_shapes=[pltpu.VMEM((dv, dk), F32), pltpu.VMEM((1, dk), F32)],
-        compiler_params=params(),
-        cost_estimate=cost(2 * n * d * (2 * dk + 2 * dv) * 1.5, n * d * 2 + n * 4000, n * dk * 6),
-    )(x, w, rank_down, rank_cols, bias_cols)
-
-
-def gate_out_kernel(b0, b1, r0, r1, s0, s1, e0, e1, gain_ref, w0, w1, m0, m1, g0, g1, out_ref):
-    total = None
-    gain = gain_ref[...]
-    for b, r, s, e, w, m, g in ((b0, r0, s0, e0, w0, m0, g0), (b1, r1, s1, e1, w1, m1, g1)):
-        mixed = b[...] + dot_nt(r[...], e[...])
-        inv = lax.rsqrt(jnp.mean(mixed * mixed, axis=-1, keepdims=True) + GROUP_EPS)
-        sw = s[...]
-        gated = (mixed * inv * gain * (sw * jax.nn.sigmoid(sw))).astype(BF16)
-        m[...] = mixed
-        g[...] = gated
-        part = dot(gated, w[...])
-        total = part if total is None else total + part
-    out_ref[...] = total.astype(BF16)
-
-
-def gate_out(bases, reaches, swishes, enters, gain, weights):
-    n, dv = bases[0].shape
-    dk = reaches[0].shape[1]
-    d = weights[0].shape[1]
-    row = rows_spec(BLOCK, dv)
-    return pl.pallas_call(
-        gate_out_kernel,
-        name="gate_out",
-        grid=(n // BLOCK,),
-        in_specs=[row, row, rows_spec(BLOCK, dk), rows_spec(BLOCK, dk), row, row]
-        + [whole((dv, dk))] * 2 + [whole((1, dv))] + [whole((dv, d))] * 2,
-        out_specs=[row, row, row, row, rows_spec(BLOCK, d)],
-        out_shape=[sds((n, dv), F32)] * 2 + [sds((n, dv), BF16)] * 2 + [sds((n, d), BF16)],
-        compiler_params=params(),
-        cost_estimate=cost(2 * n * dv * (d + dk) * 2, n * (dv * 28 + d * 2), n * dv * 2),
-    )(*bases, *reaches, *swishes, *enters, gain, *weights)
+        functools.partial(front_phase_kernel, bits),
+        name="front_phase",
+        in_specs=[hbm] * 7 + [vmem] * 6,
+        out_specs=[hbm] * 18 + [vmem] * 3,
+        out_shape=out_shape,
+        scratch_shapes=scratch,
+        compiler_params=pltpu.CompilerParams(collective_id=3, has_side_effects=True, vmem_limit_bytes=60 << 20),
+        cost_estimate=cost(12e9, 60e6, 1e6),
+    )(tokens, cotangent, kw, vw, qw, sw, wo, rd, ru, bias, ggain, ngain, restart)
 
 
 def tile_of(step):
@@ -412,169 +763,6 @@
     )(middle, *cots, wg_t, wu_t, wd, gain)
 
 
-class Wires:
-    def __init__(self, send_sem, recv_sem):
-        self.send_sem, self.recv_sem, self.used, self.all = send_sem, recv_sem, 0, []
-
-    def copy(self, src, dst, target):
-        made = pltpu.make_async_remote_copy(
-            src,
-            dst,
-            self.send_sem.at[self.used],
-            self.recv_sem.at[self.used],
-            device_id=target,
-            device_id_type=MESH,
-        )
-        self.used += 1
-        self.all.append(made)
-        return made
-
-    def drain(self):
-        for made in self.all:
-            made.wait_send()
-
-
-class Places:
-    def __init__(self, wide_count):
-        self.wide, self.place = lax.axis_index("wide"), lax.axis_index("narrow")
-        self.core = self.place % 2
-        self.second = self.place // 2
-        self.by_core = (self.wide, self.place + 1 - 2 * self.core)
-        self.by_row = (self.wide, (self.place + 2) % 4)
-        self.bits = []
-        bit = 1
-        while bit < wide_count:
-            self.bits.append(bit)
-            bit *= 2
-
-    def has(self, bit):
-        return (self.wide // bit) % 2
-
-    def across(self, bit):
-        return (self.wide + bit - 2 * bit * self.has(bit), self.place)
-
-    def meet(self):
-        barrier = pltpu.get_barrier_semaphore()
-        others = [self.by_core, self.by_row] + [self.across(bit) for bit in self.bits]
-        for other in others:
-            pl.semaphore_signal(barrier, 1, device_id=other, device_id_type=MESH)
-        pl.semaphore_wait(barrier, len(others))
-
-
-class Scan:
-    def __init__(self, where, wires, tot_s, tot_m, pre_s, pre_m, out, into, backward):
-        self.tot_s, self.tot_m, self.pre_s, self.pre_m = tot_s, tot_m, pre_s, pre_m
-        self.out, self.into = out, into
-        self.steps = []
-        for i, bit in enumerate([0] + where.bits):
-            target = where.across(bit) if bit else where.by_row
-            is_set = where.has(bit) if bit else where.second
-            later = (1 - is_set if backward else is_set) > 0
-            self.steps.append((wires.copy(out.at[i], into.at[i], target), later, bit == 0))
-        pre_s[...] = jnp.zeros_like(pre_s)
-        pre_m[...] = jnp.ones_like(pre_m)
-
-    def begin(self, i=0):
-        self.at = i
-        dv = self.tot_s.shape[1]
-        for h in range(2):
-            self.out[i, h, :dv, :] = self.tot_s[h].astype(BF16)
-            self.out[i, h, dv:, :] = jnp.broadcast_to(self.tot_m[h], (16, self.tot_m.shape[2])).astype(BF16)
-        self.steps[i][0].start()
-
-    def advance(self):
-        self.finish(self.at)
-        if self.at + 1 < len(self.steps):
-            self.begin(self.at + 1)
-            return True
-        return False
-
-    def finish(self, i):
-        copy, later, swapped = self.steps[i]
-        copy.wait_recv()
-        dv = self.tot_s.shape[1]
-        for h in range(2):
-            g = 1 - h if swapped else h
-            oth_s = self.into[i, g, :dv, :].astype(F32)
-            oth_m = self.into[i, g, dv : dv + 1, :].astype(F32)
-            pre_s, pre_m, tot_s, tot_m = self.pre_s[h], self.pre_m[h], self.tot_s[h], self.tot_m[h]
-            self.pre_s[h] = jnp.where(later, oth_s * pre_m + pre_s, pre_s)
-            self.pre_m[h] = jnp.where(later, oth_m * pre_m, pre_m)
-            self.tot_s[h] = jnp.where(later, oth_s * tot_m + tot_s, tot_s * oth_m + oth_s)
-            self.tot_m[h] = tot_m * oth_m
-
-
-class Scatter:
-    def __init__(self, where, wires, source, keep, order, recvs):
-        self.recvs, self.steps = recvs, []
-        left = sorted(where.bits, reverse=True)
-        held, first = source, keep
-        for bit, recv in zip(order, recvs):
-            dim = left.index(bit)
-            mine = where.has(bit)
-            other = held.at[(slice(None),) * dim + (1 - mine,)]
-            self.steps.append((wires.copy(other, recv, where.across(bit)), first if first is not None else held, dim, mine, first is not None))
-            left.pop(dim)
-            held, first = recv, None
-
-    def begin(self, i=0):
-        self.at = i
-        self.steps[i][0].start()
-
-    def advance(self):
-        if self.at + 1 < len(self.steps):
-            self.finish(self.at)
-            self.begin(self.at + 1)
-
-    def result(self):
-        while self.at + 1 < len(self.steps):
-            self.advance()
-        return self.finish(self.at)
-
-    def finish(self, i):
-        copy, held, dim, mine, picked = self.steps[i]
-        copy.wait_recv()
-        recv = self.recvs[i]
-        last = i == len(self.steps) - 1
-        for at in itertools.product(range(2), repeat=len(recv.shape) - 2):
-            source = at if picked else at[:dim] + (mine,) + at[dim:]
-            total = recv[at].astype(F32) + held[source].astype(F32)
-            if last:
-                return total
-            recv[at] = total.astype(BF16)
-        return None
-
-
-class Everywhere:
-    def __init__(self, where, wires, values, recvs):
-        self.values, self.recvs = values, recvs
-        targets = [where.by_core, where.by_row] + [where.across(bit) for bit in where.bits]
-        self.steps = [wires.copy(values.at[i], recvs.at[i], target) for i, target in enumerate(targets)]
-
-    def begin(self, i=0):
-        self.at = i
-        self.steps[i].start()
-
-    def advance(self):
-        if self.at + 1 < len(self.steps):
-            self.finish(self.at)
-            self.begin(self.at + 1)
-
-    def result(self):
-        while self.at + 1 < len(self.steps):
-            self.advance()
-        self.finish(self.at)
-        return self.values[len(self.steps)]
-
-    def finish(self, i):
-        self.steps[i].wait_recv()
-        self.values[i + 1] = self.values[i] + self.recvs[i]
-
-
-def bit_index(w, bits):
-    return tuple((w // bit) % 2 for bit in sorted(bits, reverse=True))
-
-
 def back_phase_kernel(
     bits,
     gm_h, mx_h, s_h, r_h, gt_h, rows_h, q_h, k_h, v_h, cum_h, dpre_h, rank_h, sin_h, w_h, wo_h, g_h, gmid_h, tok_h,
@@ -598,19 +786,16 @@
         return copy
 
     orders = (bits, bits[1:] + bits[:1], bits)
-    first = [load(gm_h, gm)]
-    for h in range(2):
-        first += [load(wo_h[h], wo.at[h]), load(mx_h[h], mx.at[h]), load(s_h[h], sw.at[h]), load(r_h[h], reach.at[h])]
-    second = [load(gt_h[h], gated.at[h]) for h in range(2)] + [load(rows_h, rows)]
+    first = [load(gm_h, gm), load(wo_h, wo), load(mx_h, mx), load(s_h, sw), load(r_h, reach)]
+    second = [load(gt_h, gated), load(rows_h, rows)]
     third = []
     for i in range(3):
         left = sorted(bits, reverse=True)
         dim = left.index(orders[i][0])
         third.append(load(g_h[i].at[(slice(None),) * dim + (where.has(orders[i][0]),)], keep[i]))
     fourth = [load(rank_h, rank)]
-    for h in range(2):
-        for src, dst in ((q_h, q), (k_h, k), (v_h, v), (cum_h, cum), (dpre_h, dpre), (sin_h, sin), (w_h, w)):
-            fourth.append(load(src[h], dst.at[h]))
+    for src, dst in ((q_h, q), (k_h, k), (v_h, v), (cum_h, cum), (dpre_h, dpre), (sin_h, sin), (w_h, w)):
+        fourth.append(load(src, dst))
     fifth = [load(gmid_h, gmid), load(tok_h, tok)]
 
     where.meet()
@@ -865,7 +1050,7 @@
     bits = wide_bits()
     count, d = rows.shape
     half = count // 2
-    dk, dv, rk = q[0].shape[1], v[0].shape[1], rank.shape[1]
+    dk, dv, rk = q.shape[2], v.shape[2], rank.shape[1]
     ff = grads[0].shape[-1]
     each = d // 2 ** len(bits)
     n_bits, chunks = len(bits), count // CHUNK
@@ -942,111 +1127,40 @@
     return bits
 
 
-def scan_states(mult, state, backward):
-    place = {"narrow": lax.axis_index("narrow"), "wide": lax.axis_index("wide")}
-    heads, dv, dk = state.shape
-    pre_m, pre_s = jnp.ones_like(mult), jnp.zeros_like(state)
-    tot_m, tot_s = mult, state
-    for axis, bit in [("narrow", 2)] + [("wide", b) for b in wide_bits()]:
-        packed = jnp.concatenate(
-            [tot_s, jnp.broadcast_to(tot_m, (heads, 16, dk))], axis=1
-        ).astype(BF16)
-        other = hop(packed, axis, bit).astype(F32)
-        if axis == "narrow":
-            other = other[::-1]
-        oth_s, oth_m = other[:, :dv], other[:, dv : dv + 1]
-        is_set = (place[axis] & bit) != 0
-        mine_later = jnp.logical_not(is_set) if backward else is_set
-        new_s = oth_s * pre_m + pre_s
-        new_m = oth_m * pre_m
-        sum_later = oth_s * tot_m + tot_s
-        sum_first = tot_s * oth_m + oth_s
-        pre_s = jnp.where(mine_later, new_s, pre_s)
-        pre_m = jnp.where(mine_later, new_m, pre_m)
-        tot_s = jnp.where(mine_later, sum_later, sum_first)
-        tot_m = tot_m * oth_m
-    return pre_s
-
-
 def shards(
     tokens, cotangent, flags, norm_gain, query_weight, key_weight, value_weight, swish_weight, rank_down, rank_up,
     decay_bias, group_gain, output_weight, mlp_gain, mlp_gate, mlp_up, mlp_down,
 ):
-    own_rows = tokens.shape[0]
     place = lax.axis_index("narrow")
-    core = place & 1
-    second = (place & 2) != 0
-    wide_odd = (lax.axis_index("wide") & 1) != 0
-    dk = query_weight.shape[1]
-    dv = value_weight.shape[1]
-    d = tokens.shape[1]
-
-    def in_order(mine, other):
-        return jnp.where(
-            core == 0, jnp.concatenate([mine, other]), jnp.concatenate([other, mine])
-        )
-
-    def from_row_partner(value):
-        half = value.shape[0] // 2
-        piece = lax.dynamic_slice_in_dim(value, jnp.where(wide_odd, half, 0), half, 0)
-        first = hop(piece, "narrow", 2)
-        relayed = hop(first, "wide", 1)
-        return jnp.where(
-            wide_odd, jnp.concatenate([relayed, first]), jnp.concatenate([first, relayed])
-        )
-
-    def head_cols(index):
-        ru = lax.dynamic_slice_in_dim(rank_up, index * dk, dk, 1).astype(F32)
-        bias = lax.dynamic_slice_in_dim(decay_bias, index * dk, dk, 0).astype(F32)
-        return ru, bias.reshape(1, dk)
-
-    restart = 1.0 - flags[0].astype(F32)
-    restart = jnp.where(second, 1.0, restart)
-    norm_gain_f = norm_gain.astype(F32)
-    mlp_gain_f = mlp_gain.astype(F32)
+    dk, dv, d = query_weight.shape[1], value_weight.shape[1], tokens.shape[1]
+    restart = jnp.where((place & 2) != 0, 1.0, 1.0 - flags[0].astype(F32))
+    restart = jnp.full((1, dk), restart, F32)
+    norm_gain_f = norm_gain.astype(F32).reshape(1, d)
+    mlp_gain_f = mlp_gain.astype(F32).reshape(1, d)
     gain_row = group_gain.astype(F32).reshape(1, dv)
 
-    inputs = tokens.astype(F32)
-    inv_one = lax.rsqrt(jnp.mean(inputs * inputs, axis=-1, keepdims=True) + NORM_EPS)
-    normed = (inputs * inv_one * norm_gain_f).astype(BF16)
-    normed_two = hop(normed, "narrow", 1)
-    rows_all = in_order(normed, normed_two)
-
-    w_own = jnp.concatenate([key_weight, value_weight, query_weight, swish_weight], axis=1)
-    w_other = from_row_partner(w_own)
-    out_other = from_row_partner(output_weight)
-    cot_late, w_other, out_other = lax.optimization_barrier((cotangent, w_other, out_other))
-    cot_y = hop(cot_late, "narrow", 2)
-    cot_c = hop(cotangent, "narrow", 1)
-    cot_d = hop(cot_y, "narrow", 1)
-
-    ru_own, bias_own = head_cols(place)
-    ru_oth, bias_oth = head_cols(place ^ 2)
-    weights_out = (output_weight, out_other)
-    one = forward_head(rows_all, w_own, rank_down, ru_own, bias_own, dk, dv)
-    two = forward_head(rows_all, w_other, rank_down, ru_oth, bias_oth, dk, dv)
-    (q, k, v, s, cum, dpre, rank_pre, base, reach, sin, off, state, mult) = zip(one, two)
-    rank_pre = rank_pre[0]
-    mults = restart * jnp.stack(mult)
-    enter = restart * scan_states(mults, jnp.stack(state), False)
-    enter_low = enter.astype(BF16)
-    mixed0, mixed1, gated0, gated1, term = gate_out(
-        base, reach, s, (enter_low[0], enter_low[1]), gain_row, weights_out
+    def both_heads(value):
+        return jnp.stack([lax.dynamic_slice_in_dim(value, head * dk, dk, 1) for head in (place, place ^ 2)]).astype(F32)
+
+    ru = both_heads(rank_up)
+    bias = both_heads(decay_bias.reshape(1, -1))
+    (
+        middle, rows_all, q, k, v, s, cum, dpre, rank_pre, reach, sin, mixed, gated, w, weights_out, cot_c, cot_y, cot_d,
+        off, enter, mults,
+    ) = front_phase(
+        tokens, cotangent, key_weight, value_weight, query_weight, swish_weight, output_weight, rank_down, ru, bias,
+        gain_row, norm_gain_f, restart,
     )
-    own_term = lax.dynamic_slice_in_dim(term, core * own_rows, own_rows, 0)
-    send_term = lax.dynamic_slice_in_dim(term, (1 - core) * own_rows, own_rows, 0)
-    middle = inputs + (own_term.astype(F32) + hop(send_term, "narrow", 1).astype(F32))
     grad_middle, gm_all, mlp_gain_part, gate_g, up_g, down_g, near, far = mlp_phase(
-        middle, (cotangent, cot_c, cot_y, cot_d), mlp_gate.T, mlp_up.T, mlp_down, mlp_gain_f.reshape(1, d)
+        middle, (cotangent, cot_c, cot_y, cot_d), mlp_gate.T, mlp_up.T, mlp_down, mlp_gain_f
     )
     result = (middle + (near.astype(F32) + hop(far, "narrow", 2).astype(F32))).astype(BF16)
     bits = wide_bits()
     split = (2,) * len(bits) + (d // 2 ** len(bits), -1)
     input_grad, gate_t, up_t, down_t, out_t, k_g, v_g, q_g, s_g, rdown_t, rup_g, bias_g, mgain_g, group_g, ngain = back_phase(
-        gm_all, (mixed0, mixed1), s, reach, (gated0, gated1), rows_all, q, k, v, cum, dpre, rank_pre, sin,
-        (w_own, w_other), weights_out, tuple(g.reshape(split) for g in (gate_g, up_g, down_g)), grad_middle, tokens,
-        jnp.stack(off), enter, mults, jnp.stack([ru_own, ru_oth]), rank_down, gain_row, norm_gain_f.reshape(1, d),
-        mlp_gain_part, jnp.full((1, dk), restart, F32),
+        gm_all, mixed, s, reach, gated, rows_all, q, k, v, cum, dpre, rank_pre, sin,
+        w, weights_out, tuple(g.reshape(split) for g in (gate_g, up_g, down_g)), grad_middle, tokens,
+        off, enter, mults, ru, rank_down, gain_row, norm_gain_f, mlp_gain_part, restart,
     )
     return (
         result,

time: 360 us -> 305 us (0.85)
  waiting for transfers between devices: 42 us -> 0.01 us
  Pallas kernels: 240 us -> 279 us
  local copies, waits for them, and re-layouts: 31.6 us -> 14.2 us
  starting transfers between devices: 17.7 us -> 1.1 us
  other arithmetic: 23.7 us -> 8.92 us
    ppermute x14 -> x1, waiting for transfers between devices: 42 us -> 0.01 us  [hop(): lax.ppermute(value, axis, [(i, i ^ bit) for i in range(lax.axis_size(axis...]
    pallas_call x3 -> x1, Pallas kernels: 32.5 us -> 70.1 us  [front_phase(): pl.pallas_call(functools.partial(front_phase_kernel, bits), name='front_p...]
    ppermute x14 -> x1, starting transfers between devices: 17.7 us -> 1.1 us  [hop(): lax.ppermute(value, axis, [(i, i ^ bit) for i in range(lax.axis_size(axis...]
    unnamed x128 -> x48, local copies, waits for them, and re-layouts: 26.2 us -> 12.2 us
    select_n x4 -> x0, other arithmetic: 9.31 us -> none  [the longest x2 5.65 us: from_row_partner(): jnp.where(wide_odd, jnp.concatenate([relayed, first]), jnp.concatenate([f...]
    add x1 -> x0, other arithmetic: 3.97 us -> none  [shards(): inputs + (own_term.astype(F32) + hop(send_term, 'narrow', 1).astype(F32))]
    dynamic_slice x3 -> x0, local copies, waits for them, and re-layouts: 3.94 us -> none  [the longest x1 2.73 us: shards(): lax.dynamic_slice_in_dim(term, (1 - core) * own_rows, own_rows, 0)]
  transfers between devices with their start and end apart: 14 -> 1, of which waited for: 7 -> 0; matrix products, arithmetic and copies ran while one was open for 6% -> 0% of each run, Pallas kernels for 43% -> 45%
where the time goes in v1:
time: 305 us
  Pallas kernels  279 us (91%)
  local copies, waits for them, and re-layouts  14.2 us (5%)
  other arithmetic  8.92 us (3%)
    pallas_call x1, Pallas kernels, back_phase(): pl.pallas_call(kernel, name='back_phase', in_specs=[hbm] * (n_in - n_vmem...  138 us
    pallas_call x1, Pallas kernels, mlp_phase(): pl.pallas_call(mlp_phase_kernel, name='mlp_phase', in_specs=[hbm] * 8 + [...  70.8 us
    pallas_call x1, Pallas kernels, front_phase(): pl.pallas_call(functools.partial(front_phase_kernel, bits), name='front_p...  70.1 us
    unnamed x48, local copies, waits for them, and re-layouts  12.2 us
  transfers between devices with their start and end apart: 1, of which 0 were waited for; matrix products, arithmetic and copies ran while one was open for 0% of the time, Pallas kernels for 45%

profile of v1, /device:TPU:0, one launch (start us, length us, event | category | flops | bytes accessed | tf_op | source)
XLA Modules:
  0.0 305.0 jit_solution(7345690036353091551)
XLA Ops:
  0.7 1.6 copy.33.rd_ref.refs_24_
  2.3 0.7 dynamic-slice_bitcast_fusion.1
  3.0 0.8 dynamic-slice_bitcast_fusion.3
  3.8 1.2 reshape.109
  5.0 1.3 reshape.111
  6.9 1.3 reshape.113
  8.2 0.6 maximum_convert_fusion.ru_ref.refs_23_
  8.8 0.6 maximum_convert_fusion.1.bias_ref
  9.4 0.5 broadcast_in_dim.3.restart_ref.refs_28_
  9.9 70.1 %front_phase.1 = (f32[640,1024]{1,0:T(8,128)}, bf16[1280,1024]{1,0:T(8,128)(2,1)}, bf16[2,1280,128]{2,1,0:T(8,128)(2,1)}, bf16[2,1280,128]{2,1,0:T(8,128)(2,1)},...) custom-call(bf16[640,1024]{1,0:T(8,128)(2,1)} %refs_19_.1, ...), custom_call_target="tpu_custom_call" | custom-call | flops 12000000000 | bytes 60000000 | tf_op jit(solution)/shard_map/front_phase/pallas_call | solution.py:526
  80.0 70.8 %mlp_phase.1 = (f32[640,1024]{1,0:T(8,128)}, bf16[1280,1024]{1,0:T(8,128)(2,1)}, f32[1,1024]{1,0:T(1,128)}, bf16[1024,704]{1,0:T(8,128)(2,1)}, bf16[1024,704]{1,...) custom-call(f32[640,1024]{1,0:T(8,128)} %get-tuple-element.60.mid_h, ...), custom_call_target="tpu_custom_call" | custom-call | flops 33218887680 | bytes 60000000 | tf_op jit(solution)/shard_map/mlp_phase/pallas_call | solution.py:744
  150.8 1.1 collective-permute-start
  151.9 0.0 copy-start.1
  151.9 138.5 %back_phase.1 = (f32[640,1024]{1,0:T(8,128)}, f32[704,128]{1,0:T(8,128)}, f32[704,128]{1,0:T(8,128)}, f32[704,128]{1,0:T(8,128)}, f32[256,128]{1,0:T(8,128)}, /*...) custom-call(bf16[1280,1024]{1,0:T(8,128)(2,1)} %get-tuple-element.66, ...), custom_call_target="tpu_custom_call" | custom-call | flops 40000000000 | bytes 60000000 | tf_op jit(solution)/shard_map/back_phase/pallas_call | solution.py:1106
  290.4 0.0 collective-permute-done
  290.4 0.0 copy-done.1
  290.4 0.0 copy-start
  290.4 4.0 %add_convert_fusion = bf16[640,1024]{1,0:T(8,128)(2,1)} fusion(f32[640,1024]{1,0:T(8,128)} %get-tuple-element.60.mid_h, bf16[640,1024]{1,0:T(8,128)(2,1)} %collective-permute-done, bf16[640,1024]{1,0:T(8,128)(2,1)S(1)} %copy-done.1), kind=kLoop, calls=%fused_computation | loop fusion | flops 3276800 | bytes 6553600 | tf_op jit(solution)/shard_map/convert_element_type | solution.py:1157
  294.4 0.0 copy-done
  294.4 0.0 copy-start.13
  294.4 0.0 copy-start.10
  294.4 0.0 copy-start.9
  294.4 0.0 copy-start.7
  294.4 0.0 copy-start.6
  294.4 0.0 copy-start.8
  294.4 0.0 copy-start.11
  294.5 0.0 copy-start.14
  294.5 0.0 copy-start.15
  294.5 0.0 copy-start.5
  294.5 0.0 copy-start.12
  294.5 1.5 copy.51
  296.0 0.0 copy-done.13
  296.0 0.0 copy-start.4
  296.0 0.0 copy-start.3
  296.0 0.0 copy-start.2
  296.0 0.6 copy.52
  296.6 0.0 copy-done.10
  296.6 0.6 copy.53
  297.2 0.0 copy-done.9
  297.2 0.6 copy.54
  297.9 0.0 copy-done.7
  297.9 0.7 copy.55
  298.5 0.0 copy-done.6
  298.5 0.7 copy.56
  299.2 0.0 copy-done.8
  299.2 0.6 copy.57
  299.8 0.0 copy-done.11
  299.8 0.6 copy.58
  300.4 0.0 copy-done.14
  300.4 0.6 copy.59
  301.0 0.0 copy-done.15
  301.0 0.6 copy.60
  301.6 0.0 copy-done.5
  301.6 0.7 copy.61
  302.2 0.0 copy-done.12
  302.2 0.6 copy.62
  302.8 0.0 copy-done.4
  302.8 0.7 copy.63
  303.6 0.0 copy-done.3
  303.6 0.7 copy.64
  304.3 0.0 copy-done.2
  304.3 0.7 copy.65
Async XLA Ops:
  150.8 139.6 %collective-permute-start = (bf16[640,1024]{1,0:T(8,128)(2,1)}, bf16[640,1024]{1,0:T(8,128)(2,1)}, u32[]{:S(2)}, u32[]{:S(2)}) collective-permute-start(bf16[640,1024]{1,0:T(8,128)(2,1)} %get-tuple-element.65), channel_id=1, source_target_pairs={{0,2},{1,3},{2,0},{3,1},{4,6},{5,7},{6,4},{7,5},{8,10},{9,11},{10,... | collective-permute-start | bytes 3932168 | tf_op jit(solution)/shard_map/ppermute | solution.py:1119
  151.9 138.5 %copy-start.1 = (bf16[640,1024]{1,0:T(8,128)(2,1)S(1)}, bf16[640,1024]{1,0:T(8,128)(2,1)}, u32[]{:S(2)}) copy-start(bf16[640,1024]{1,0:T(8,128)(2,1)} %get-tuple-element.64) | copy-start | bytes 3932164
  290.4 4.0 %copy-start = (f32[640,1024]{1,0:T(8,128)S(1)}, f32[640,1024]{1,0:T(8,128)}, u32[]{:S(2)}) copy-start(f32[640,1024]{1,0:T(8,128)} %get-tuple-element.125) | copy-start | bytes 7864324
  294.4 1.6 copy-start.13
  294.4 2.2 copy-start.10
  294.4 2.8 copy-start.9
  294.4 3.4 %copy-start.7 = (f32[128,256]{1,0:T(8,128)S(1)}, f32[128,256]{1,0:T(8,128)}, u32[]{:S(2)}) copy-start(f32[128,256]{1,0:T(8,128)} %get-tuple-element.129) | copy-start | bytes 393220
  294.4 4.1 %copy-start.6 = (f32[128,256]{1,0:T(8,128)S(1)}, f32[128,256]{1,0:T(8,128)}, u32[]{:S(2)}) copy-start(f32[128,256]{1,0:T(8,128)} %get-tuple-element.130) | copy-start | bytes 393220
  294.4 4.7 %copy-start.8 = (f32[16,1024]{1,0:T(8,128)S(1)}, f32[16,1024]{1,0:T(8,128)}, u32[]{:S(2)}) copy-start(f32[16,1024]{1,0:T(8,128)} %get-tuple-element.95) | copy-start | bytes 196612
  294.4 5.4 %copy-start.11 = (f32[16,512]{1,0:T(8,128)S(1)}, f32[16,512]{1,0:T(8,128)}, u32[]{:S(2)}) copy-start(f32[16,512]{1,0:T(8,128)} %get-tuple-element.132) | copy-start | bytes 98308
  294.5 6.0 %copy-start.14 = (f32[1,512]{1,0:T(1,128)S(1)}, f32[1,512]{1,0:T(1,128)}, u32[]{:S(2)}) copy-start(f32[1,512]{1,0:T(1,128)} %get-tuple-element.97) | copy-start | bytes 6148
  294.5 6.5 %copy-start.15 = (f32[1,256]{1,0:T(1,128)S(1)}, f32[1,256]{1,0:T(1,128)}, u32[]{:S(2)}) copy-start(f32[1,256]{1,0:T(1,128)} %get-tuple-element.98) | copy-start | bytes 3076
  294.5 7.1 %copy-start.5 = (f32[256,128]{1,0:T(8,128)S(1)}, f32[256,128]{1,0:T(8,128)}, u32[]{:S(2)}) copy-start(f32[256,128]{1,0:T(8,128)} %get-tuple-element.135) | copy-start | bytes 393220
  294.5 7.8 %copy-start.12 = (f32[1,1024]{1,0:T(1,128)S(1)}, f32[1,1024]{1,0:T(1,128)}, u32[]{:S(2)}) copy-start(f32[1,1024]{1,0:T(1,128)} %get-tuple-element.100) | copy-start | bytes 12292
  296.0 6.8 %copy-start.4 = (f32[704,128]{1,0:T(8,128)S(1)}, f32[704,128]{1,0:T(8,128)}, u32[]{:S(2)}) copy-start(f32[704,128]{1,0:T(8,128)} %get-tuple-element.101) | copy-start | bytes 1081348
  296.0 7.6 %copy-start.3 = (f32[704,128]{1,0:T(8,128)S(1)}, f32[704,128]{1,0:T(8,128)}, u32[]{:S(2)}) copy-start(f32[704,128]{1,0:T(8,128)} %get-tuple-element.102) | copy-start | bytes 1081348
  296.0 8.3 %copy-start.2 = (f32[704,128]{1,0:T(8,128)S(1)}, f32[704,128]{1,0:T(8,128)}, u32[]{:S(2)}) copy-start(f32[704,128]{1,0:T(8,128)} %get-tuple-element.139) | copy-start | bytes 1081348

commit v2 on v1

--- a/solution.py
+++ b/solution.py
@@ -158,30 +158,35 @@
 
 class Scatter:
     def __init__(self, where, wires, source, keep, order, recvs):
-        self.recvs, self.steps = recvs, []
-        left = sorted(where.bits, reverse=True)
+        self.recvs, self.steps, self.at = recvs, [], 0
+        left = sorted(order, reverse=True)
         held, first = source, keep
         for bit, recv in zip(order, recvs):
             dim = left.index(bit)
             mine = where.has(bit)
             other = held.at[(slice(None),) * dim + (1 - mine,)]
-            self.steps.append((wires.copy(other, recv, where.across(bit)), first if first is not None else held, dim, mine, first is not None))
+            copy = wires.copy(other, recv, where.across(bit))
+            self.steps.append((copy, held if first is None else first, dim, mine, first is not None))
             left.pop(dim)
             held, first = recv, None
 
-    def begin(self, i=0):
-        self.at = i
-        self.steps[i][0].start()
+    def go(self):
+        self.steps[self.at][0].start()
+
+    def land(self):
+        total = self.finish(self.at)
+        self.at += 1
+        return total
 
     def advance(self):
         if self.at + 1 < len(self.steps):
-            self.finish(self.at)
-            self.begin(self.at + 1)
+            self.land()
+            self.go()
 
     def result(self):
         while self.at + 1 < len(self.steps):
             self.advance()
-        return self.finish(self.at)
+        return self.land()
 
     def finish(self, i):
         copy, held, dim, mine, picked = self.steps[i]
@@ -223,13 +228,63 @@
         self.values[i + 1] = self.values[i] + self.recvs[i]
 
 
+class Shared:
+    def __init__(self, where, wires, parts, first, values, recvs, out):
+        self.core, self.parts, self.first = where.core, parts, first
+        self.values, self.recvs, self.out, self.at = values, recvs, out, 0
+        targets = [where.by_row] + [where.across(bit) for bit in where.bits]
+        self.steps = [wires.copy(parts.at[1 - where.core], first, where.by_core)]
+        self.steps += [wires.copy(values.at[i], recvs.at[i], target) for i, target in enumerate(targets)]
+        self.steps.append(wires.copy(out.at[where.core], out.at[where.core], where.by_core))
+
+    def begin(self):
+        self.steps[0].start()
+
+    def advance(self):
+        i, last = self.at, len(self.steps) - 1
+        if i == last:
+            return
+        self.steps[i].wait_recv()
+        if i == 0:
+            total = self.parts[self.core] + self.first[...]
+        else:
+            total = self.values[i - 1] + self.recvs[i - 1]
+        if i + 1 == last:
+            self.out[self.core] = total
+        else:
+            self.values[i] = total
+        self.at = i + 1
+        self.steps[i + 1].start()
+
+    def result(self):
+        while self.at + 1 < len(self.steps):
+            self.advance()
+        self.steps[-1].wait_recv()
+        return self.out
+
+
 def bit_index(w, bits):
     return tuple((w // bit) % 2 for bit in sorted(bits, reverse=True))
 
 
+def put_rows(ref, lead, j, size, bits, lanes, value):
+    each = ref.shape[-2]
+    for p in range(size // each):
+        at = lead + bit_index(j * (size // each) + p, bits) + (slice(None), lanes)
+        ref[at] = value[p * each : (p + 1) * each]
+
+
+def lanes_at(start, size):
+    return pl.ds(pl.multiple_of(start, size), size)
+
+
+def row_places(d, dv, qk):
+    return (0, d, 2 * d, 2 * d + dv, 2 * d + dv + qk)
+
+
 def front_phase_kernel(
     bits,
-    tok_h, cot_h, kw_h, vw_h, qw_h, sw_h, wo_h, rd_ref, ru_ref, bias_ref, ggain_ref, ngain_ref, restart_ref,
+    tok_h, cot_h, kw_h, vw_h, qw_h, sw_h, wo_h, rd_ref, ru_ref, row_ref,
     mid_h, rows_h, q_h, k_h, v_h, s_h, cum_h, dpre_h, rank_h, reach_h, sin_h, mx_h, gated_h, w_h, wo2_h, c1_h, c2_h, c3_h,
     off_o, enter_o, mult_o,
     tok, rows, w, wo, q, k, v, sw, cum, dpre, rank, reach, sin, mx, gated, tb, tr, mid, st, off,
@@ -262,6 +317,10 @@
     load_wo = load(wo_h, wo.at[0])
 
     where.meet()
+    at_row = row_places(d, dv, 4 * dk)
+    ngain = row_ref[:, at_row[0] : at_row[1]]
+    gain = row_ref[:, at_row[2] : at_row[3]]
+    restart = row_ref[:, at_row[4] : at_row[4] + dk]
 
     odd = where.has(1)
     over_x = where.across(1)
@@ -304,7 +363,6 @@
     for piece in kv_in:
         piece[0].start()
     load_tok.wait()
-    ngain = ngain_ref[...]
     for i in range(2):
         x = tok[pl.ds(i * blk, blk), :].astype(F32)
         inv = lax.rsqrt(jnp.mean(x * x, axis=-1, keepdims=True) + NORM_EPS)
@@ -359,10 +417,13 @@
 
         @pl.when(i < blocks)
         def _():
-            rank[at, :] = dot(x, rd_ref[...])
+            rank[at, :] = dot_nt(x, rd_ref[...])
 
         proj = dot(x, w[h, :, :kv])
-        pre = exact(rank[at, :], ru_ref[h], ((1,), (0,))) + bias_ref[h]
+        head = (where.place + 2 * h) % 4
+        ru = ru_ref[:, lanes_at(head * dk, dk)].astype(F32)
+        bias = row_ref[:, lanes_at(at_row[3] + head * dk, dk)]
+        pre = exact(rank[at, :], ru, ((1,), (0,))) + bias
         dlog = jax.nn.log_sigmoid(pre) * (1.0 / GATE_NORM)
         k_low = proj[:, :dk].astype(BF16)
         v_low = proj[:, dk:].astype(BF16)
@@ -386,7 +447,7 @@
         @pl.when(b == blocks - 1)
         def _():
             tot_s[h] = st[...]
-            mult = restart_ref[...] * jnp.exp(off[...])
+            mult = restart * jnp.exp(off[...])
             tot_m[h] = mult
             mult_o[h] = mult
 
@@ -445,10 +506,9 @@
     while scan.advance():
         pass
     for h in range(2):
-        enter_o[h] = restart_ref[...] * pre_s[h]
+        enter_o[h] = restart * pre_s[h]
     wo_in[1].wait_recv()
     store(wo, wo2_h)
-    gain = ggain_ref[...]
 
     def gate_step(i, _):
         b = jnp.where(i < 2, 2 - 2 * where.core + i, 2 * where.core + i - 2)
@@ -495,11 +555,11 @@
     wires.drain()
 
 
-def front_phase(tokens, cotangent, kw, vw, qw, sw, wo, rd, ru, bias, ggain, ngain, restart):
+def front_phase(tokens, cotangent, kw, vw, qw, sw, wo, rd, ru, row):
     bits = wide_bits()
     half, d = tokens.shape
     count = 2 * half
-    dk, dv, rk = kw.shape[1], vw.shape[1], rd.shape[1]
+    dk, dv, rk = kw.shape[1], vw.shape[1], rd.shape[0]
     chunks, n_bits = count // CHUNK, len(bits)
     hbm = pl.BlockSpec(memory_space=pltpu.HBM)
     vmem = pl.BlockSpec(memory_space=pltpu.VMEM)
@@ -526,13 +586,13 @@
     return pl.pallas_call(
         functools.partial(front_phase_kernel, bits),
         name="front_phase",
-        in_specs=[hbm] * 7 + [vmem] * 6,
+        in_specs=[hbm] * 7 + [vmem] * 3,
         out_specs=[hbm] * 18 + [vmem] * 3,
         out_shape=out_shape,
         scratch_shapes=scratch,
         compiler_params=pltpu.CompilerParams(collective_id=3, has_side_effects=True, vmem_limit_bytes=60 << 20),
         cost_estimate=cost(12e9, 60e6, 1e6),
-    )(tokens, cotangent, kw, vw, qw, sw, wo, rd, ru, bias, ggain, ngain, restart)
+    )(tokens, cotangent, kw, vw, qw, sw, wo, rd, ru, row)
 
 
 def tile_of(step):
@@ -540,19 +600,22 @@
 
 
 def mlp_phase_kernel(
-    mid_h, c0_h, c1_h, c2_h, c3_h, wg_h, wu_h, wd_h, gain_ref,
+    bits,
+    mid_h, c0_h, c1_h, c2_h, c3_h, wg_h, wu_h, wd_h, row_ref,
     gmid_h, gm_h, part_ref, gg_h, gu_h, gd_h, near_h, far_h,
-    mid, xs, cs, wg, wu, wd, hs, ggs, gus, gn, rc, rd, ac, ry, dn, dnr, gr_st, gmb,
-    load_sem, send_sem, recv_sem, gr_sem, out_sem,
+    mid, xs, cs, wg, wu, wd, hs, ggs, gus, gn, rc, rd, ac, ry, dn, dnr, gmb, sum_g, sum_u, sum_d, got_g, got_u,
+    load_sem, send_sem, recv_sem, out_sem,
 ):
-    tile = xs.shape[1]
+    tile = xs.shape[0] // 8
     rows = 2 * tile
-    d = xs.shape[2]
-    ff = hs.shape[2]
-    wide, place = lax.axis_index("wide"), lax.axis_index("narrow")
-    core = place % 2
-    by_core = (wide, place + 1 - 2 * core)
-    by_row = (wide, (place + 2) % 4)
+    d = xs.shape[1]
+
+    def rows_of(t):
+        return lanes_at(t * tile, tile)
+
+    where = Places(2 ** len(bits))
+    wires = Wires(send_sem, recv_sem)
+    by_core, by_row = where.by_core, where.by_row
 
     loads = [pltpu.make_async_copy(mid_h, mid, load_sem.at[0])]
     for i, (src, dst) in enumerate(((wg_h, wg), (wu_h, wu), (wd_h, wd))):
@@ -560,35 +623,52 @@
     for i, src in enumerate((c0_h, c1_h, c2_h, c3_h)):
         for j in range(2):
             loads.append(
-                pltpu.make_async_copy(src.at[pl.ds(j * tile, tile)], cs.at[2 * i + j], load_sem.at[4 + 2 * i + j])
+                pltpu.make_async_copy(src.at[pl.ds(j * tile, tile)], cs.at[rows_of(2 * i + j)], load_sem.at[4 + 2 * i + j])
             )
     for load in loads:
         load.start()
-
-    barrier = pltpu.get_barrier_semaphore()
-    for other in (by_core, by_row):
-        pl.semaphore_signal(barrier, 1, device_id=other, device_id_type=MESH)
-    pl.semaphore_wait(barrier, 2)
-
-    def remote(src, dst, index, target):
-        return pltpu.make_async_remote_copy(
-            src, dst, send_sem.at[index], recv_sem.at[index], device_id=target, device_id_type=MESH
-        )
-
-    x_row = [remote(xs.at[j], xs.at[4 + j], j, by_row) for j in range(2)]
-    x_core = [remote(xs.at[j], xs.at[2 + j], 2 + j, by_core) for j in range(2)]
-    x_both = [remote(xs.at[4 + j], xs.at[6 + j], 4 + j, by_core) for j in range(2)]
-    g_near = [remote(gn.at[2 + j], rc.at[j], 6 + j, by_core) for j in range(2)]
-    g_far = [remote(gn.at[6 + j], rd.at[j], 8 + j, by_core) for j in range(2)]
-    g_row = [remote(ac.at[j], ry.at[j], 10 + j, by_row) for j in range(2)]
-    d_in = [remote(dn.at[(2, 3, 6, 7)[j]], dnr.at[j], 14 + j, by_core) for j in range(4)]
-    gain = gain_ref[...]
+    stores = []
+
+    def store(src, dst):
+        copy = pltpu.make_async_copy(src, dst, out_sem.at[len(stores)])
+        stores.append(copy)
+        copy.start()
+
+    where.meet()
+    x_row = [wires.copy(xs.at[rows_of(j)], xs.at[rows_of(4 + j)], by_row) for j in range(2)]
+    x_core = [wires.copy(xs.at[rows_of(j)], xs.at[rows_of(2 + j)], by_core) for j in range(2)]
+    x_both = [wires.copy(xs.at[rows_of(4 + j)], xs.at[rows_of(6 + j)], by_core) for j in range(2)]
+    g_near = [wires.copy(gn.at[2 + j], rc.at[j], by_core) for j in range(2)]
+    g_far = [wires.copy(gn.at[6 + j], rd.at[j], by_core) for j in range(2)]
+    g_row = [wires.copy(ac.at[j], ry.at[j], by_row) for j in range(2)]
+    d_in = [wires.copy(dn.at[(2, 3, 6, 7)[j]], dnr.at[j], by_core) for j in range(4)]
+    left = sorted(bits, reverse=True)
+
+    def first_hop(total, got, bit):
+        dim, mine = left.index(bit), where.has(bit)
+        mids = (slice(None),) * (dim - 1)
+        copies = [
+            wires.copy(total.at[(top,) + mids + (1 - mine,)], got.at[top], where.across(bit)) for top in range(2)
+        ]
+
+        def finish():
+            for copy in copies:
+                copy.wait_recv()
+            for at in itertools.product(range(2), repeat=len(bits) - 1):
+                own = at[:dim] + (mine,) + at[dim:]
+                got[at] = (got[at].astype(F32) + total[own].astype(F32)).astype(BF16)
+
+        return copies, finish
+
+    hop_g, end_g = first_hop(sum_g, got_g, bits[0])
+    hop_u, end_u = first_hop(sum_u, got_u, bits[1])
+    gain = row_ref[:, d : 2 * d]
 
     loads[0].wait()
     for j in range(2):
         m = mid[pl.ds(j * tile, tile), :]
         inv = lax.rsqrt(jnp.mean(m * m, axis=-1, keepdims=True) + NORM_EPS)
-        xs[j] = (m * inv * gain).astype(BF16)
+        xs[rows_of(j), :] = (m * inv * gain).astype(BF16)
         x_row[j].start()
         x_core[j].start()
     for load in loads[1:]:
@@ -596,6 +676,7 @@
 
     def step(s, _):
         t = tile_of(s)
+        at = rows_of(t)
 
         @pl.when(s == 2)
         def _():
@@ -616,18 +697,18 @@
             def _():
                 x_both[j].wait_recv()
 
-        x = xs[t]
+        x = xs[at, :]
         gate = dot_nt(x, wg[...])
         up = dot_nt(x, wu[...])
-        gh = dot_nt(cs[t], wd[...])
+        gh = dot_nt(cs[at, :], wd[...])
         sig = jax.nn.sigmoid(gate)
         act = gate * sig
         hidden = (act * up).astype(BF16)
         g_up = (gh * act).astype(BF16)
         g_gate = (gh * up * sig * (1.0 + gate * (1.0 - sig))).astype(BF16)
-        hs[t] = hidden
-        ggs[t] = g_gate
-        gus[t] = g_up
+        hs[at, :] = hidden
+        ggs[at, :] = g_gate
+        gus[at, :] = g_up
         gn[t] = (dot(g_gate, wg[...]) + dot(g_up, wu[...])).astype(BF16)
 
         for j in range(2):
@@ -656,50 +737,27 @@
     for copy in d_in:
         copy.start()
 
-    blk = gr_st.shape[2]
-    count = d // blk
-
-    def gr_copies(slot, j):
-        at = pl.ds(pl.multiple_of(j * blk, blk), blk)
-        return [
-            pltpu.make_async_copy(gr_st.at[slot, i], dst.at[at], gr_sem.at[slot, i])
-            for i, dst in enumerate((gg_h, gu_h, gd_h))
-        ]
-
-    def weights(j, _):
-        slot = j % 2
-        cols = pl.ds(pl.multiple_of(j * blk, blk), blk)
-
-        @pl.when(j >= 2)
-        def _():
-            for copy in gr_copies(slot, j - 2):
-                copy.wait()
-
-        for i, lefts, rights in ((0, xs, ggs), (1, xs, gus), (2, cs, hs)):
-            acc = dot_tn(lefts[0, :, cols], rights[0])
-            for t in range(1, 8):
-                acc = acc + dot_tn(lefts[t, :, cols], rights[t])
-            gr_st[slot, i] = acc.astype(BF16)
-        for copy in gr_copies(slot, j):
-            copy.start()
-        return 0
-
-    lax.fori_loop(0, count, weights, 0)
-    for j in (count - 2, count - 1):
-        for copy in gr_copies(j % 2, j):
-            copy.wait()
-    sums = []
-    for j in range(2):
-        d_in[j].wait_recv()
-        d_in[2 + j].wait_recv()
-        for at, extra, out in ((j, j, near_h), (4 + j, 2 + j, far_h)):
-            dn[at] = (dn[at].astype(F32) + dnr[extra].astype(F32)).astype(BF16)
-            sums.append(pltpu.make_async_copy(dn.at[at], out.at[pl.ds(j * tile, tile)], out_sem.at[3 + len(sums)]))
-            sums[-1].start()
+    size = 256
+    count = d // size
+
+    def weight_grad(lefts, rights, total, copies):
+        def step(j, _):
+            cols = lanes_at(j * size, size)
+            acc = dot_tn(lefts[:, cols], rights[...])
+            put_rows(total, (), j, size, bits, slice(None), acc.astype(BF16))
+            for top, copy in enumerate(copies):
+
+                @pl.when(j == (top + 1) * count // 2 - 1)
+                def _():
+                    copy.start()
+
+            return 0
+
+        lax.fori_loop(0, count, step, 0)
 
     part = jnp.zeros((1, d), F32)
-    gm_out = []
-    for j in range(2):
+
+    def final(j, part):
         at = pl.ds(j * tile, tile)
         g_near[j].wait_recv()
         g_row[j].wait_recv()
@@ -709,67 +767,83 @@
         unit = m * inv
         weighted = grad * gain
         part = part + jnp.sum(grad * unit, axis=0, keepdims=True)
-        gmid = cs[j].astype(F32) + inv * (weighted - unit * jnp.mean(weighted * unit, axis=-1, keepdims=True))
+        gmid = cs[rows_of(j), :].astype(F32) + inv * (weighted - unit * jnp.mean(weighted * unit, axis=-1, keepdims=True))
         mid[at, :] = gmid
         gmb[j] = gmid.astype(BF16)
-        there = gm_h.at[pl.ds(pl.multiple_of(core * rows + j * tile, tile), tile)]
-        copies = [
-            pltpu.make_async_copy(gmb.at[j], there, out_sem.at[1 + j]),
-            remote(gmb.at[j], there, 12 + j, by_core),
-        ]
-        for copy in copies:
-            copy.start()
-        gm_out += copies
-    part_ref[...] = part
-    last = pltpu.make_async_copy(mid, gmid_h, out_sem.at[0])
-    last.start()
+        there = gm_h.at[lanes_at(where.core * rows + j * tile, tile)]
+        store(gmb.at[j], there)
+        store(mid.at[at], gmid_h.at[at])
+        gm_out[j].start()
+        return part
+
+    gm_out = []
+    for j in range(2):
+        there = gm_h.at[lanes_at(where.core * rows + j * tile, tile)]
+        gm_out.append(wires.copy(gmb.at[j], there, by_core))
+
+    weight_grad(xs, ggs, sum_g, hop_g)
+    weight_grad(xs, gus, sum_u, hop_u)
+    part = final(0, part)
+    weight_grad(cs, hs, sum_d, [])
+    store(sum_d, gd_h)
+    for j in range(2):
+        d_in[j].wait_recv()
+        d_in[2 + j].wait_recv()
+        for at, extra, out in ((j, j, near_h), (4 + j, 2 + j, far_h)):
+            dn[at] = (dn[at].astype(F32) + dnr[extra].astype(F32)).astype(BF16)
+            store(dn.at[at], out.at[pl.ds(j * tile, tile)])
+    end_g()
+    store(got_g, gg_h)
+    part_ref[...] = final(1, part)
+    end_u()
+    store(got_u, gu_h)
     for copy in gm_out:
+        copy.wait_recv()
+    for copy in stores:
         copy.wait()
-    last.wait()
-    for copy in sums:
-        copy.wait()
-    for group in (d_in, x_row, x_core, x_both, g_near, g_far, g_row):
-        for copy in group:
-            copy.wait_send()
-
-
-def mlp_phase(middle, cots, wg_t, wu_t, wd, gain):
+    wires.drain()
+
+
+def mlp_phase(middle, cots, wg_t, wu_t, wd, row):
+    bits = wide_bits()
     rows, d = middle.shape
     ff = wd.shape[0]
     tile = rows // 2
-    blk = 128
     hbm = pl.BlockSpec(memory_space=pltpu.HBM)
     vmem = pl.BlockSpec(memory_space=pltpu.VMEM)
     dma = pltpu.SemaphoreType.DMA
+    v_ = pltpu.VMEM
+    block = (d // 2 ** len(bits), ff)
+    full, part = (2,) * len(bits) + block, (2,) * (len(bits) - 1) + block
     return pl.pallas_call(
-        mlp_phase_kernel,
+        functools.partial(mlp_phase_kernel, bits),
         name="mlp_phase",
         in_specs=[hbm] * 8 + [vmem],
         out_specs=[hbm, hbm, vmem] + [hbm] * 5,
         out_shape=[sds((rows, d), F32), sds((2 * rows, d), BF16), sds((1, d), F32)]
-        + [sds((d, ff), BF16)] * 3 + [sds((rows, d), BF16)] * 2,
+        + [sds(part, BF16), sds(part, BF16), sds(full, BF16)] + [sds((rows, d), BF16)] * 2,
         scratch_shapes=[
-            pltpu.VMEM((rows, d), F32), pltpu.VMEM((8, tile, d), BF16), pltpu.VMEM((8, tile, d), BF16),
-            pltpu.VMEM((ff, d), BF16), pltpu.VMEM((ff, d), BF16), pltpu.VMEM((ff, d), BF16),
-            pltpu.VMEM((8, tile, ff), BF16), pltpu.VMEM((8, tile, ff), BF16), pltpu.VMEM((8, tile, ff), BF16),
-            pltpu.VMEM((8, tile, d), BF16), pltpu.VMEM((2, tile, d), BF16), pltpu.VMEM((2, tile, d), BF16),
-            pltpu.VMEM((2, tile, d), BF16), pltpu.VMEM((2, tile, d), BF16),
-            pltpu.VMEM((8, tile, d), BF16), pltpu.VMEM((4, tile, d), BF16),
-            pltpu.VMEM((2, 3, blk, ff), BF16), pltpu.VMEM((2, tile, d), BF16),
-            dma((12,)), dma((18,)), dma((18,)), dma((2, 3)), dma((7,)),
+            v_((rows, d), F32), v_((8 * tile, d), BF16), v_((8 * tile, d), BF16),
+            v_((ff, d), BF16), v_((ff, d), BF16), v_((ff, d), BF16),
+            v_((8 * tile, ff), BF16), v_((8 * tile, ff), BF16), v_((8 * tile, ff), BF16),
+            v_((8, tile, d), BF16), v_((2, tile, d), BF16), v_((2, tile, d), BF16),
+            v_((2, tile, d), BF16), v_((2, tile, d), BF16), v_((8, tile, d), BF16), v_((4, tile, d), BF16),
+            v_((2, tile, d), BF16), v_(full, BF16), v_(full, BF16), v_(full, BF16), v_(part, BF16), v_(part, BF16),
+            dma((12,)), dma((24,)), dma((24,)), dma((12,)),
         ],
-        compiler_params=pltpu.CompilerParams(collective_id=1, has_side_effects=True, vmem_limit_bytes=62 << 20),
+        compiler_params=pltpu.CompilerParams(collective_id=1, has_side_effects=True, vmem_limit_bytes=63 << 20),
         cost_estimate=cost(18 * 4 * rows * d * ff, 60e6, 4 * rows * ff),
-    )(middle, *cots, wg_t, wu_t, wd, gain)
+    )(middle, *cots, wg_t, wu_t, wd, row)
 
 
 def back_phase_kernel(
     bits,
-    gm_h, mx_h, s_h, r_h, gt_h, rows_h, q_h, k_h, v_h, cum_h, dpre_h, rank_h, sin_h, w_h, wo_h, g_h, gmid_h, tok_h,
-    off_ref, enter_ref, mult_ref, ru_ref, rd_ref, ggain_ref, ngain_ref, mpart_ref, restart_ref,
-    in_h, gate_o, up_o, down_o, wout_o, k_o, v_o, q_o, s_o, rdown_o, rup_o, bias_o, mgain_o, group_o, ngain_o,
-    gm, mx, sw, reach, gated, rows, q, k, v, cum, dpre, rank, sin, w, wo, keep, mrecv, gmid, tok,
-    gx, al, grank, ds, lb_m, pre_s, pre_m, sc_out, sc_in, osv, osy, osr, kv, kvy, kvr, tb, tr, sm, smr, ng, ngr,
+    gm_h, mx_h, s_h, r_h, gt_h, rows_h, q_h, k_h, v_h, cum_h, dpre_h, rank_h, sin_h, w_h, wo_h, g_h, gmid_h, tok_h, far_h,
+    off_ref, enter_ref, mult_ref, ru_ref, rd_ref, row_ref, mpart_ref,
+    in_h, fr_h, gate_o, up_o, down_o, wout_o, k_o, v_o, q_o, s_o, rdown_o, rup_o, bias_o, mgain_o, group_o, ngain_o,
+    gm, mx, sw, reach, gated, rows, q, k, v, cum, dpre, rank, sin, w, wo, held, mrecv, gmid, tok,
+    gx, al, grank, ds, lb_m, pre_s, pre_m, sc_out, sc_in, osv, osy, osr, kva, kvay, kvar, kvb, kvbr, kvbo, tb, tr,
+    sm, smf, smv, smr, smo, ng, ngr,
     load_sem, send_sem, recv_sem, out_sem,
 ):
     count, d = rows.shape
@@ -785,38 +859,51 @@
         copy.start()
         return copy
 
-    orders = (bits, bits[1:] + bits[:1], bits)
+    orders = (bits[1:], bits[:1] + bits[2:], bits)
+    third = [load(g_h[0], held[0]), load(g_h[1], held[1])]
     first = [load(gm_h, gm), load(wo_h, wo), load(mx_h, mx), load(s_h, sw), load(r_h, reach)]
     second = [load(gt_h, gated), load(rows_h, rows)]
-    third = []
-    for i in range(3):
-        left = sorted(bits, reverse=True)
-        dim = left.index(orders[i][0])
-        third.append(load(g_h[i].at[(slice(None),) * dim + (where.has(orders[i][0]),)], keep[i]))
+    dim = sorted(bits, reverse=True).index(bits[0])
+    keep = load(g_h[2].at[(slice(None),) * dim + (where.has(bits[0]),)], held[2])
     fourth = [load(rank_h, rank)]
     for src, dst in ((q_h, q), (k_h, k), (v_h, v), (cum_h, cum), (dpre_h, dpre), (sin_h, sin), (w_h, w)):
         fourth.append(load(src, dst))
     fifth = [load(gmid_h, gmid), load(tok_h, tok)]
 
     where.meet()
-    mlp = [Scatter(where, wires, g_h[i], keep[i], orders[i], mrecv[i]) for i in range(3)]
+    mlp = [
+        Scatter(where, wires, held[0], None, orders[0], mrecv[0]),
+        Scatter(where, wires, held[1], None, orders[1], mrecv[1]),
+        Scatter(where, wires, g_h[2], held[2], orders[2], mrecv[2]),
+    ]
     scan = Scan(where, wires, ds, lb_m, pre_s, pre_m, sc_out, sc_in, True)
     os_y = wires.copy(osv.at[1], osy, where.by_row)
-    os_s = Scatter(where, wires, osv.at[0], None, bits[1:] + bits[:1], osr)
-    kv_y = wires.copy(kv.at[1], kvy, where.by_row)
-    kv_s = Scatter(where, wires, kv.at[0], None, bits, kvr)
+    os_s = Scatter(where, wires, osv.at[0], None, bits, osr)
+    kva_y = wires.copy(kva.at[1], kvay, where.by_row)
+    kva_s = Scatter(where, wires, kva.at[0], None, bits, kvar)
+    kvb_s = [Scatter(where, wires, kvb.at[h], None, bits, kvbr[h]) for h in range(2)]
+    kvb_y = wires.copy(kvbo.at[0], kvbo.at[1], where.by_row)
     tots = [wires.copy(tb.at[j], tr.at[j], where.by_core) for j in range(2)]
-    every = Everywhere(where, wires, sm, smr)
+    far = []
+    for j in range(2):
+        at = pl.ds(j * (half // 2), half // 2)
+        far.append(wires.copy(far_h.at[at], fr_h.at[at], where.by_row))
+    every = Shared(where, wires, sm, smf, smv, smr, smo)
     every_n = Everywhere(where, wires, ng, ngr)
     n_bits = len(bits)
-    for part in mlp:
-        part.begin()
+    at_row = row_places(d, dv, 4 * dk)
+    ngain = row_ref[:, at_row[0] : at_row[1]]
+    gain = row_ref[:, at_row[2] : at_row[3]]
+    restart = row_ref[:, at_row[4] : at_row[4] + dk]
+    far[0].start()
+    for copy in third:
+        copy.wait()
+    mlp[1].go()
+    mlp[0].go()
 
     blk = half // 2
-    gain = ggain_ref[...]
     ds[...] = jnp.zeros_like(ds)
-    sm[0] = jnp.zeros_like(sm[0])
-    ng[0] = jnp.zeros_like(ng[0])
+    sm[...] = jnp.zeros_like(sm)
     for copy in first:
         copy.wait()
 
@@ -841,42 +928,39 @@
 
     group_part = lax.fori_loop(0, 4, gate_step, jnp.zeros((1, dv), F32))
     for h in range(2):
-        ds[h] = ds[h] * restart_ref[...]
+        ds[h] = ds[h] * restart
         lb_m[h] = mult_ref[h]
     scan.begin()
 
     size = 256
-    per = size // osv.shape[-2]
-
-    def put(ref, h, j, lanes, value):
-        rows_each = ref.shape[-2]
-        for p in range(per):
-            ref[(h,) + bit_index(j * per + p, bits) + (slice(None), lanes)] = value[p * rows_each : (p + 1) * rows_each]
 
     def out_step(j, _):
         cols = pl.ds(pl.multiple_of(j * size, size), size)
         for h in (1, 0):
-            put(osv, h, j, slice(0, dv), dot_tn(gm[:, cols], gated[h]).astype(BF16))
+            value = dot_tn(gm[:, cols], gated[h]).astype(BF16)
+            put_rows(osv, (h,), j, size, bits, slice(0, dv), value)
         return 0
 
     def swish_step(j, _):
         cols = pl.ds(pl.multiple_of(j * size, size), size)
         for h in (1, 0):
-            put(osv, h, j, slice(dv, 2 * dv), dot_tn(rows[:, cols], al[h, :, 2 * dk + dv :]).astype(BF16))
+            value = dot_tn(rows[:, cols], al[h, :, 2 * dk + dv :]).astype(BF16)
+            put_rows(osv, (h,), j, size, bits, slice(dv, 2 * dv), value)
         return 0
 
     for copy in second:
         copy.wait()
     lax.fori_loop(0, d // size, out_step, 0)
+    lax.fori_loop(0, d // size, swish_step, 0)
     scan.advance()
-    lax.fori_loop(0, d // size, swish_step, 0)
     os_y.start()
-    for copy in third:
-        copy.wait()
+    scan.advance()
+    keep.wait()
+    mlp[2].go()
     while scan.advance():
-        if scan.at == n_bits:
-            mlp[1].advance()
-            mlp[0].advance()
+        pass
+    mlp[0].advance()
+    mlp[1].advance()
     for copy in fourth:
         copy.wait()
 
@@ -887,8 +971,23 @@
     scale = dk**-0.5
     rk = rank.shape[1]
 
+    def add_row(ref, extra):
+        for at in itertools.product(range(2), repeat=n_bits):
+            ref[(0,) + at] = (ref[(0,) + at].astype(F32) + extra[at].astype(F32)).astype(BF16)
+
     def back_step(step, carry):
         c = chunks - 1 - step
+
+        @pl.when(step == chunks // 2)
+        def _():
+            mlp[2].advance()
+
+        @pl.when(step == chunks - 3)
+        def _():
+            os_y.wait_recv()
+            add_row(osv, osy)
+            os_s.go()
+
         at = pl.ds(pl.multiple_of(c * CHUNK, CHUNK), CHUNK)
         grs, new = None, []
         for h in range(2):
@@ -905,6 +1004,7 @@
             qi = (qf * e_qi).astype(BF16)
             ke = (kf * e_ke).astype(BF16)
             go = gx[h, at, :]
+            ru = ru_ref[:, lanes_at(((where.place + 2 * h) % 4) * dk, dk)].astype(F32)
             state = sin[h, c].astype(F32) + enter_ref[h] * jnp.exp(off_ref[h, c])
             state_low = state.astype(BF16)
             dstate = ds[h]
@@ -926,7 +1026,7 @@
             al[h, at, :dk] = d_k.astype(BF16)
             al[h, at, dk : dk + dv] = d_v.astype(BF16)
             al[h, at, dk + dv : 2 * dk + dv] = d_q.astype(BF16)
-            gr = exact(g_pre, ru_ref[h], ((1,), (1,)))
+            gr = exact(g_pre, ru, ((1,), (1,)))
             grs = gr if grs is None else grs + gr
             new.append(carry[2 * h] + exact(rank[at, :], g_pre, ((0,), (0,))))
             new.append(carry[2 * h + 1] + jnp.sum(g_pre, axis=0, keepdims=True))
@@ -936,32 +1036,27 @@
 
     zero = (jnp.zeros((rk, dk), F32), jnp.zeros((1, dk), F32))
     rup0, gb0, rup1, gb1 = lax.fori_loop(0, chunks, back_step, zero + zero)
-    for i in (1, 0, 2):
-        mlp[i].advance()
-
-    def kvq_step(h):
+    def kvq_step(ref, h, low):
         def step(j, _):
-            cols = pl.ds(pl.multiple_of(j * size, size), size)
-            put(kv, h, j, slice(None), dot_tn(rows[:, cols], al[h, :, : 2 * dk + dv]).astype(BF16))
+            cols = lanes_at(j * size, size)
+            value = dot_tn(rows[:, cols], al[h, :, low : low + size]).astype(BF16)
+            put_rows(ref, (h,), j, size, bits, slice(None), value)
             return 0
 
         lax.fori_loop(0, d // size, step, 0)
 
-    kvq_step(1)
-    kv_y.start()
-
-    def add_row(ref, extra):
-        for at in itertools.product(range(2), repeat=n_bits):
-            ref[(0,) + at] = (ref[(0,) + at].astype(F32) + extra[at].astype(F32)).astype(BF16)
-
-    os_y.wait_recv()
-    add_row(osv, osy)
-    os_s.begin()
+    kvq_step(kva, 1, 0)
+    kva_y.start()
+    for h in range(2):
+        kvq_step(kvb, h, size)
+        kvb_s[h].go()
+    mlp[2].advance()
+    os_s.advance()
 
     def total_step(i, _):
         b = jnp.where(i < 2, 2 - 2 * where.core + i, 2 * where.core + i - 2)
         at = pl.ds(pl.multiple_of(b * blk, blk), blk)
-        total = dot_nt(al[0, at, :], w[0]) + dot_nt(al[1, at, :], w[1]) + dot_nt(grank[at, :], rd_ref[...])
+        total = dot_nt(al[0, at, :], w[0]) + dot_nt(al[1, at, :], w[1]) + dot(grank[at, :], rd_ref[...])
         for j in range(2):
 
             @pl.when(i == j)
@@ -977,22 +1072,23 @@
 
     lax.fori_loop(0, 4, total_step, 0)
 
-    sm[0, 0:rk, :] = dot_tn(grank[...], rows[...])
-    at0 = pl.ds(pl.multiple_of(where.place * dk, dk), dk)
-    at1 = pl.ds(pl.multiple_of(((where.place + 2) % 4) * dk, dk), dk)
-    sm[0, rk : 2 * rk, at0] = rup0
-    sm[0, rk : 2 * rk, at1] = rup1
-    sm[0, 2 * rk : 2 * rk + 1, at0] = gb0
-    sm[0, 2 * rk : 2 * rk + 1, at1] = gb1
-    sm[0, 2 * rk + 1 : 2 * rk + 2, :] = mpart_ref[...]
-    sm[0, 2 * rk + 2 : 2 * rk + 3, :dv] = group_part
+    qk = 4 * dk
+    sm[0] = dot_tn(grank[...], rows[...])
+    at0 = where.place * dk
+    at1 = ((where.place + 2) % 4) * dk
+    sm[1, :, lanes_at(at0, dk)] = rup0
+    sm[1, :, lanes_at(at1, dk)] = rup1
+    sm[1, 0:1, lanes_at(qk + at0, dk)] = gb0
+    sm[1, 0:1, lanes_at(qk + at1, dk)] = gb1
+    sm[1, 1:2, qk : qk + dv] = group_part
+    for i in range(d // qk):
+        sm[1, 2 + i : 3 + i, qk : 2 * qk] = mpart_ref[:, i * qk : (i + 1) * qk]
     every.begin()
-    kvq_step(0)
+    kvq_step(kva, 0, 0)
     every.advance()
 
     for copy in fifth:
         copy.wait()
-    ngain = ngain_ref[...]
     part = jnp.zeros((1, d), F32)
     for j in range(2):
         at = pl.ds(j * blk, blk)
@@ -1006,46 +1102,63 @@
         gmid[at, :] = gmid[at, :] + inv * (weighted - unit * jnp.mean(weighted * unit, axis=-1, keepdims=True))
     done = pltpu.make_async_copy(gmid, in_h, out_sem.at[0])
     done.start()
-    ng[0, 0:1, :] = part
+    for i in range(8):
+        ng[0, i : i + 1, :] = part[:, i * (d // 8) : (i + 1) * (d // 8)]
     every_n.begin()
 
-    outs = (gate_o, up_o, down_o)
-    kv_y.wait_recv()
-    add_row(kv, kvy)
-    kv_s.begin()
-    for i in (1, 0):
-        outs[i][...] = jnp.transpose(mlp[i].result())
-    mlp[2].advance()
+    kva_y.wait_recv()
+    far[1].start()
+    add_row(kva, kvay)
+    kva_s.go()
+    for part in kvb_s:
+        part.advance()
+    os_s.advance()
     every.advance()
     every_n.advance()
-    for _ in range(n_bits - 1):
-        os_s.advance()
+    for i, out in ((0, gate_o), (1, up_o)):
+        out[...] = jnp.transpose(mlp[i].result())
+    for i in range(n_bits - 1):
+        kva_s.advance()
+        if i < n_bits - 2:
+            for part in kvb_s:
+                part.advance()
+        every.advance()
         every_n.advance()
-        kv_s.advance()
-        every.advance()
-    outs[2][...] = jnp.transpose(mlp[2].result())
+    kvbo[0] = kvb_s[1].result().astype(BF16)
+    kvb_y.start()
+    down_o[...] = jnp.transpose(mlp[2].result())
     total = os_s.result()
     wout_o[...] = jnp.transpose(total[:, :dv])
     s_o[...] = total[:, dv:]
+    every.advance()
     every_n.advance()
-    total = kv_s.result()
-    k_o[...] = total[:, :dk]
-    v_o[...] = total[:, dk : dk + dv]
-    q_o[...] = total[:, dk + dv :]
+    first_half = kva_s.result()
+    last_half = kvb_s[0].result()
+    kvb_y.wait_recv()
+    last_half = last_half + kvbo[1].astype(F32)
+    k_o[...] = first_half[:, :dk]
+    v_o[:, : size - dk] = first_half[:, dk:]
+    v_o[:, size - dk :] = last_half[:, : dk + dv - size]
+    q_o[...] = last_half[:, dk + dv - size :]
     small = every.result()
-    rdown_o[...] = small[:rk]
-    rup_o[...] = small[rk : 2 * rk, : rup_o.shape[1]]
-    bias_o[...] = small[2 * rk : 2 * rk + 1, : bias_o.shape[1]]
-    mgain_o[...] = small[2 * rk + 1 : 2 * rk + 2]
-    group_o[...] = small[2 * rk + 2 : 2 * rk + 3, :dv]
-    ngain_o[...] = every_n.result()[:1]
+    rdown_o[...] = small[0]
+    rup_o[...] = small[1, :, :qk]
+    bias_o[...] = small[1, 0:1, qk : 2 * qk]
+    group_o[...] = small[1, 1:2, qk : qk + dv]
+    for i in range(d // qk):
+        mgain_o[:, i * qk : (i + 1) * qk] = small[1, 2 + i : 3 + i, qk : 2 * qk]
+    whole_n = every_n.result()
+    for i in range(8):
+        ngain_o[:, i * (d // 8) : (i + 1) * (d // 8)] = whole_n[i : i + 1, :]
+    for copy in far:
+        copy.wait_recv()
     done.wait()
     wires.drain()
 
 
 def back_phase(
-    gm, mx, s, reach, gated, rows, q, k, v, cum, dpre, rank, sin, w, wo, grads, gmid, tokens,
-    off, enter, mult, ru, rd, ggain, ngain, mpart, restart,
+    gm, mx, s, reach, gated, rows, q, k, v, cum, dpre, rank, sin, w, wo, grads, gmid, tokens, far,
+    off, enter, mult, ru, rd, row, mpart,
 ):
     bits = wide_bits()
     count, d = rows.shape
@@ -1067,34 +1180,34 @@
 
     pair, three = [hbm] * 2, [hbm] * 3
     kvq = 2 * dk + dv
-    small = 2 * rk + 8
     scratch = [
         v_((count, d), BF16), v_((2, count, dv), F32), v_((2, count, dv), F32), v_((2, count, dk), BF16),
         v_((2, count, dv), BF16), v_((count, d), BF16), v_((2, count, dk), BF16), v_((2, count, dk), BF16),
         v_((2, count, dv), BF16), v_((2, count, dk), F32), v_((2, count, dk), F32), v_((count, rk), F32),
         v_((2, chunks, dv, dk), BF16), v_((2, d, kvq + dv), BF16), v_((2, dv, d), BF16),
-        [v_(shape(n_bits - 1, ff), BF16)] * 3, [falls(ff)] * 3, v_((half, d), F32), v_((half, d), BF16),
+        [v_(shape(n_bits - 1, ff), BF16)] * 3, [falls(ff)[1:], falls(ff)[1:], falls(ff)], v_((half, d), F32), v_((half, d), BF16),
         v_((2, count, dv), BF16), v_((2, count, kvq + dv), BF16), v_((count, rk), BF16),
         v_((2, dv, dk), F32), v_((2, 1, dk), F32), v_((2, dv, dk), F32), v_((2, 1, dk), F32),
         v_((n_bits + 1, 2, dv + 16, dk), BF16), v_((n_bits + 1, 2, dv + 16, dk), BF16),
         v_((2,) + shape(n_bits, 2 * dv), BF16), v_(shape(n_bits, 2 * dv), BF16), falls(2 * dv),
-        v_((2,) + shape(n_bits, kvq), BF16), v_(shape(n_bits, kvq), BF16), falls(kvq),
+        v_((2,) + shape(n_bits, 256), BF16), v_(shape(n_bits, 256), BF16), falls(256),
+        v_((2,) + shape(n_bits, 256), BF16), [falls(256), falls(256)], v_((2, each, 256), BF16),
         v_((4, half // 2, d), BF16), v_((2, half // 2, d), BF16),
-        v_((n_bits + 3, small, d), F32), v_((n_bits + 2, small, d), F32),
-        v_((n_bits + 3, 8, d), F32), v_((n_bits + 2, 8, d), F32),
-        dma((48,)), dma((64,)), dma((64,)), dma((1,)),
+        v_((2, rk, d), F32), v_((rk, d), F32), v_((n_bits + 1, rk, d), F32), v_((n_bits + 1, rk, d), F32), v_((2, rk, d), F32),
+        v_((n_bits + 3, 8, d // 8), F32), v_((n_bits + 2, 8, d // 8), F32),
+        dma((24,)), dma((80,)), dma((80,)), dma((1,)),
     ]
     out_shape = [
-        sds((half, d), F32), sds((ff, each), F32), sds((ff, each), F32), sds((ff, each), F32), sds((dv, each), F32),
+        sds((half, d), F32), sds((half, d), BF16), sds((ff, each), F32), sds((ff, each), F32), sds((ff, each), F32), sds((dv, each), F32),
         sds((each, dk), F32), sds((each, dv), F32), sds((each, dk), F32), sds((each, dv), F32),
         sds((rk, d), F32), sds((rk, 4 * dk), F32), sds((1, 4 * dk), F32), sds((1, d), F32), sds((1, dv), F32), sds((1, d), F32),
     ]
     operands = (
-        gm, mx, s, reach, gated, rows, q, k, v, cum, dpre, rank, sin, w, wo, grads, gmid, tokens,
-        off, enter, mult, ru, rd, ggain, ngain, mpart, restart,
+        gm, mx, s, reach, gated, rows, q, k, v, cum, dpre, rank, sin, w, wo, grads, gmid, tokens, far,
+        off, enter, mult, ru, rd, row, mpart,
     )
     flat, tree = jax.tree.flatten(operands)
-    n_vmem = len(jax.tree.leaves(operands[18:]))
+    n_vmem = len(jax.tree.leaves(operands[19:]))
     flat_scratch, scratch_tree = jax.tree.flatten(scratch, is_leaf=lambda x: not isinstance(x, list))
     n_in, n_out = len(flat), len(out_shape)
 
@@ -1107,7 +1220,7 @@
         kernel,
         name="back_phase",
         in_specs=[hbm] * (n_in - n_vmem) + [vmem] * n_vmem,
-        out_specs=[hbm] + [vmem] * (n_out - 1),
+        out_specs=[hbm, hbm] + [vmem] * (n_out - 2),
         out_shape=out_shape,
         scratch_shapes=flat_scratch,
         compiler_params=pltpu.CompilerParams(collective_id=2, has_side_effects=True, vmem_limit_bytes=62 << 20),
@@ -1115,8 +1228,31 @@
     )(*flat)
 
 
-def hop(value, axis, bit):
-    return lax.ppermute(value, axis, [(i, i ^ bit) for i in range(lax.axis_size(axis))])
+def finish_kernel(count, mid_ref, near_ref, far_ref, grad_ref, *refs):
+    res_ref, in_ref = refs[count : count + 2]
+    res_ref[...] = (mid_ref[...] + (near_ref[...].astype(F32) + far_ref[...].astype(F32))).astype(BF16)
+    in_ref[...] = grad_ref[...]
+
+    @pl.when(pl.program_id(0) == 0)
+    def _():
+        for src, dst in zip(refs[:count], refs[count + 2 :]):
+            dst[...] = src[...]
+
+
+def finish(middle, near, far, grad, smalls):
+    rows, d = middle.shape
+    blk = rows // 4
+    row = rows_spec(blk, d)
+    wholes = [pl.BlockSpec(v.shape, lambda i: (0, 0)) for v in smalls]
+    return pl.pallas_call(
+        functools.partial(finish_kernel, len(smalls)),
+        name="finish",
+        grid=(4,),
+        in_specs=[row] * 4 + wholes,
+        out_specs=[row] * 2 + wholes,
+        out_shape=[sds((rows, d), BF16), sds((rows, d), F32)] + [sds(v.shape, v.dtype) for v in smalls],
+        compiler_params=params(62),
+    )(middle, near, far, grad, *smalls)
 
 
 def wide_bits():
@@ -1134,34 +1270,25 @@
     place = lax.axis_index("narrow")
     dk, dv, d = query_weight.shape[1], value_weight.shape[1], tokens.shape[1]
     restart = jnp.where((place & 2) != 0, 1.0, 1.0 - flags[0].astype(F32))
-    restart = jnp.full((1, dk), restart, F32)
-    norm_gain_f = norm_gain.astype(F32).reshape(1, d)
-    mlp_gain_f = mlp_gain.astype(F32).reshape(1, d)
-    gain_row = group_gain.astype(F32).reshape(1, dv)
-
-    def both_heads(value):
-        return jnp.stack([lax.dynamic_slice_in_dim(value, head * dk, dk, 1) for head in (place, place ^ 2)]).astype(F32)
-
-    ru = both_heads(rank_up)
-    bias = both_heads(decay_bias.reshape(1, -1))
+    parts = [part.astype(F32) for part in (norm_gain, mlp_gain, group_gain, decay_bias)]
+    row = jnp.concatenate(parts + [jnp.full((dk,), restart, F32)]).reshape(1, -1)
+    rd = rank_down.T
     (
         middle, rows_all, q, k, v, s, cum, dpre, rank_pre, reach, sin, mixed, gated, w, weights_out, cot_c, cot_y, cot_d,
         off, enter, mults,
     ) = front_phase(
-        tokens, cotangent, key_weight, value_weight, query_weight, swish_weight, output_weight, rank_down, ru, bias,
-        gain_row, norm_gain_f, restart,
+        tokens, cotangent, key_weight, value_weight, query_weight, swish_weight, output_weight, rd, rank_up, row
     )
     grad_middle, gm_all, mlp_gain_part, gate_g, up_g, down_g, near, far = mlp_phase(
-        middle, (cotangent, cot_c, cot_y, cot_d), mlp_gate.T, mlp_up.T, mlp_down, mlp_gain_f
+        middle, (cotangent, cot_c, cot_y, cot_d), mlp_gate.T, mlp_up.T, mlp_down, row
     )
-    result = (middle + (near.astype(F32) + hop(far, "narrow", 2).astype(F32))).astype(BF16)
-    bits = wide_bits()
-    split = (2,) * len(bits) + (d // 2 ** len(bits), -1)
-    input_grad, gate_t, up_t, down_t, out_t, k_g, v_g, q_g, s_g, rdown_t, rup_g, bias_g, mgain_g, group_g, ngain = back_phase(
+    input_grad, far_sum, *smalls = back_phase(
         gm_all, mixed, s, reach, gated, rows_all, q, k, v, cum, dpre, rank_pre, sin,
-        w, weights_out, tuple(g.reshape(split) for g in (gate_g, up_g, down_g)), grad_middle, tokens,
-        off, enter, mults, ru, rank_down, gain_row, norm_gain_f, mlp_gain_part, restart,
+        w, weights_out, (gate_g, up_g, down_g), grad_middle, tokens, far, off, enter, mults, rank_up, rd, row,
+        mlp_gain_part,
     )
+    result, input_grad, *smalls = finish(middle, near, far_sum, input_grad, smalls)
+    gate_t, up_t, down_t, out_t, k_g, v_g, q_g, s_g, rdown_t, rup_g, bias_g, mgain_g, group_g, ngain = smalls
     return (
         result,
         input_grad,

time: 305 us -> 259 us (0.85)
  Pallas kernels: 279 us -> 254 us
  local copies, waits for them, and re-layouts: 14.2 us -> 0.62 us
  other arithmetic: 8.92 us -> 2.71 us
    pallas_call x1, Pallas kernels: 138 us -> 106 us  [back_phase(): pl.pallas_call(kernel, name='back_phase', in_specs=[hbm] * (n_in - n_vmem...]
    unnamed x48 -> x0, local copies, waits for them, and re-layouts: 12.2 us -> none
    pallas_call x1 -> x2, Pallas kernels: 70.8 us -> 78.5 us  [the longest x1 71.6 us: mlp_phase(): pl.pallas_call(functools.partial(mlp_phase_kernel, bits), name='mlp_phase...]
    convert_element_type x3 -> x0, other arithmetic: 5.15 us -> none  [the longest x1 3.98 us: shards(): (middle + (near.astype(F32) + hop(far, 'narrow', 2).astype(F32))).astype(...]
    reshape x3 -> x0, other arithmetic: 3.77 us -> none  [the longest x1 1.28 us: shards(): mlp_gain_f = mlp_gain.astype(F32).reshape(1, d)]
  transfers between devices with their start and end apart: 1 -> 0, of which waited for: 0 -> 0; matrix products, arithmetic and copies ran while one was open for 0% -> 0% of each run, Pallas kernels for 45% -> 0%
where the time goes in v2:
time: 259 us
  Pallas kernels  254 us (98%)
  other arithmetic  2.71 us (1%)
    pallas_call x1, Pallas kernels, back_phase(): pl.pallas_call(kernel, name='back_phase', in_specs=[hbm] * (n_in - n_vmem...  106 us
    pallas_call x1, Pallas kernels, mlp_phase(): pl.pallas_call(functools.partial(mlp_phase_kernel, bits), name='mlp_phase...  71.6 us
    pallas_call x1, Pallas kernels, front_phase(): pl.pallas_call(functools.partial(front_phase_kernel, bits), name='front_p...  69.8 us
    pallas_call x1, Pallas kernels, finish(): pl.pallas_call(functools.partial(finish_kernel, len(smalls)), name='finis...  6.89 us

profile of v2, /device:TPU:0, one launch (start us, length us, event | category | flops | bytes accessed | tf_op | source)
XLA Modules:
  0.0 259.0 jit_solution(9661141817943941310)
XLA Ops:
  0.6 0.7 constant_dynamic-update-slice_fusion.4
  1.3 0.7 constant_dynamic-update-slice_fusion.3
  2.0 0.7 constant_dynamic-update-slice_fusion.2
  2.7 0.7 constant_dynamic-update-slice_fusion.1
  4.0 0.6 reshape.38.row_ref.refs_26_
  4.6 69.8 %front_phase.1 = (f32[640,1024]{1,0:T(8,128)}, bf16[1280,1024]{1,0:T(8,128)(2,1)}, bf16[2,1280,128]{2,1,0:T(8,128)(2,1)}, bf16[2,1280,128]{2,1,0:T(8,128)(2,1)},...) custom-call(bf16[640,1024]{1,0:T(8,128)(2,1)} %refs_19_.1, ...), custom_call_target="tpu_custom_call" | custom-call | flops 12000000000 | bytes 60000000 | tf_op jit(solution)/shard_map/front_phase/pallas_call | solution.py:586
  74.4 71.6 %mlp_phase.1 = (f32[640,1024]{1,0:T(8,128)}, bf16[1280,1024]{1,0:T(8,128)(2,1)}, f32[1,1024]{1,0:T(1,128)}, bf16[2,2,128,704]{3,2,1,0:T(8,128)(2,1)}, bf16[2,2,1...) custom-call(f32[640,1024]{1,0:T(8,128)} %get-tuple-element.77.mid_h., ...), custom_call_target="tpu_custom_call" | custom-call | flops 33218887680 | bytes 60000000 | tf_op jit(solution)/shard_map/mlp_phase/pallas_call | solution.py:818
  146.1 105.8 %back_phase.1 = (f32[640,1024]{1,0:T(8,128)}, bf16[640,1024]{1,0:T(8,128)(2,1)}, f32[704,128]{1,0:T(8,128)}, f32[704,128]{1,0:T(8,128)}, f32[704,128]{1,0:T(8,12...) custom-call(bf16[1280,1024]{1,0:T(8,128)(2,1)} %get-tuple-element.82, ...), custom_call_target="tpu_custom_call" | custom-call | flops 40000000000 | bytes 60000000 | tf_op jit(solution)/shard_map/back_phase/pallas_call | solution.py:1219
  251.9 6.9 %finish.1 = (bf16[640,1024]{1,0:T(8,128)(2,1)}, f32[640,1024]{1,0:T(8,128)}, f32[704,128]{1,0:T(8,128)}, f32[704,128]{1,0:T(8,128)}, f32[704,128]{1,0:T(8,128)},...) custom-call(f32[640,1024]{1,0:T(8,128)} %get-tuple-element.77.mid_h., ...), custom_call_target="tpu_custom_call" | custom-call | tf_op jit(solution)/shard_map/finish/pallas_call | solution.py:1247
  (1 shorter events, 0.0 us)

commit v3 on v2

--- a/solution.py
+++ b/solution.py
@@ -116,44 +116,48 @@
 class Scan:
     def __init__(self, where, wires, tot_s, tot_m, pre_s, pre_m, out, into, backward):
         self.tot_s, self.tot_m, self.pre_s, self.pre_m = tot_s, tot_m, pre_s, pre_m
-        self.out, self.into = out, into
+        self.out, self.into, self.at, self.order = out, into, 0, (0, 1)
         self.steps = []
         for i, bit in enumerate([0] + where.bits):
             target = where.across(bit) if bit else where.by_row
             is_set = where.has(bit) if bit else where.second
             later = (1 - is_set if backward else is_set) > 0
-            self.steps.append((wires.copy(out.at[i], into.at[i], target), later, bit == 0))
+            copies = [wires.copy(out.at[i, h], into.at[i, h], target) for h in range(2)]
+            self.steps.append((copies, later, bit == 0))
         pre_s[...] = jnp.zeros_like(pre_s)
         pre_m[...] = jnp.ones_like(pre_m)
 
-    def begin(self, i=0):
-        self.at = i
+    def send(self, i, h):
         dv = self.tot_s.shape[1]
+        self.out[i, h, :dv, :] = self.tot_s[h].astype(BF16)
+        self.out[i, h, dv:, :] = jnp.broadcast_to(self.tot_m[h], (16, self.tot_m.shape[2])).astype(BF16)
+        self.steps[i][0][h].start()
+
+    def begin(self):
         for h in range(2):
-            self.out[i, h, :dv, :] = self.tot_s[h].astype(BF16)
-            self.out[i, h, dv:, :] = jnp.broadcast_to(self.tot_m[h], (16, self.tot_m.shape[2])).astype(BF16)
-        self.steps[i][0].start()
+            self.send(0, h)
 
     def advance(self):
-        self.finish(self.at)
-        if self.at + 1 < len(self.steps):
-            self.begin(self.at + 1)
-            return True
-        return False
-
-    def finish(self, i):
-        copy, later, swapped = self.steps[i]
-        copy.wait_recv()
+        i, more = self.at, self.at + 1 < len(self.steps)
+        copies, later, swapped = self.steps[i]
         dv = self.tot_s.shape[1]
-        for h in range(2):
-            g = 1 - h if swapped else h
+        heads = []
+        for g in self.order:
+            h = 1 - g if swapped else g
+            heads.append(h)
+            copies[g].wait_recv()
             oth_s = self.into[i, g, :dv, :].astype(F32)
             oth_m = self.into[i, g, dv : dv + 1, :].astype(F32)
             pre_s, pre_m, tot_s, tot_m = self.pre_s[h], self.pre_m[h], self.tot_s[h], self.tot_m[h]
+            if more:
+                self.tot_s[h] = jnp.where(later, oth_s * tot_m + tot_s, tot_s * oth_m + oth_s)
+                self.tot_m[h] = tot_m * oth_m
+                self.send(i + 1, h)
             self.pre_s[h] = jnp.where(later, oth_s * pre_m + pre_s, pre_s)
             self.pre_m[h] = jnp.where(later, oth_m * pre_m, pre_m)
-            self.tot_s[h] = jnp.where(later, oth_s * tot_m + tot_s, tot_s * oth_m + oth_s)
-            self.tot_m[h] = tot_m * oth_m
+        self.order = tuple(heads)
+        self.at = i + 1
+        return more
 
 
 class Scatter:
@@ -581,7 +585,7 @@
         v_((2, half // 2, d), BF16), v_((2, half // 2, d), BF16), v_((half, d), F32), v_((dv, dk), F32), v_((1, dk), F32),
         v_((2, dv, dk), F32), v_((2, 1, dk), F32), v_((2, dv, dk), F32), v_((2, 1, dk), F32),
         v_((n_bits + 1, 2, dv + 16, dk), BF16), v_((n_bits + 1, 2, dv + 16, dk), BF16),
-        dma((8,)), dma((32,)), dma((32,)), dma((20,)),
+        dma((8,)), dma((48,)), dma((48,)), dma((20,)),
     ]
     return pl.pallas_call(
         functools.partial(front_phase_kernel, bits),
@@ -885,8 +889,8 @@
     kvb_y = wires.copy(kvbo.at[0], kvbo.at[1], where.by_row)
     tots = [wires.copy(tb.at[j], tr.at[j], where.by_core) for j in range(2)]
     far = []
-    for j in range(2):
-        at = pl.ds(j * (half // 2), half // 2)
+    for j in range(4):
+        at = pl.ds(j * (half // 4), half // 4)
         far.append(wires.copy(far_h.at[at], fr_h.at[at], where.by_row))
     every = Shared(where, wires, sm, smf, smv, smr, smo)
     every_n = Everywhere(where, wires, ng, ngr)
@@ -987,6 +991,7 @@
             os_y.wait_recv()
             add_row(osv, osy)
             os_s.go()
+            far[1].start()
 
         at = pl.ds(pl.multiple_of(c * CHUNK, CHUNK), CHUNK)
         grs, new = None, []
@@ -1036,42 +1041,6 @@
 
     zero = (jnp.zeros((rk, dk), F32), jnp.zeros((1, dk), F32))
     rup0, gb0, rup1, gb1 = lax.fori_loop(0, chunks, back_step, zero + zero)
-    def kvq_step(ref, h, low):
-        def step(j, _):
-            cols = lanes_at(j * size, size)
-            value = dot_tn(rows[:, cols], al[h, :, low : low + size]).astype(BF16)
-            put_rows(ref, (h,), j, size, bits, slice(None), value)
-            return 0
-
-        lax.fori_loop(0, d // size, step, 0)
-
-    kvq_step(kva, 1, 0)
-    kva_y.start()
-    for h in range(2):
-        kvq_step(kvb, h, size)
-        kvb_s[h].go()
-    mlp[2].advance()
-    os_s.advance()
-
-    def total_step(i, _):
-        b = jnp.where(i < 2, 2 - 2 * where.core + i, 2 * where.core + i - 2)
-        at = pl.ds(pl.multiple_of(b * blk, blk), blk)
-        total = dot_nt(al[0, at, :], w[0]) + dot_nt(al[1, at, :], w[1]) + dot(grank[at, :], rd_ref[...])
-        for j in range(2):
-
-            @pl.when(i == j)
-            def _():
-                tb[j] = total.astype(BF16)
-                tots[j].start()
-
-            @pl.when(i == 2 + j)
-            def _():
-                tb[2 + j] = total.astype(BF16)
-
-        return 0
-
-    lax.fori_loop(0, 4, total_step, 0)
-
     qk = 4 * dk
     sm[0] = dot_tn(grank[...], rows[...])
     at0 = where.place * dk
@@ -1084,6 +1053,43 @@
     for i in range(d // qk):
         sm[1, 2 + i : 3 + i, qk : 2 * qk] = mpart_ref[:, i * qk : (i + 1) * qk]
     every.begin()
+    def kvq_step(ref, h, low):
+        def step(j, _):
+            cols = lanes_at(j * size, size)
+            value = dot_tn(rows[:, cols], al[h, :, low : low + size]).astype(BF16)
+            put_rows(ref, (h,), j, size, bits, slice(None), value)
+            return 0
+
+        lax.fori_loop(0, d // size, step, 0)
+
+    kvq_step(kva, 1, 0)
+    kva_y.start()
+    for h in range(2):
+        kvq_step(kvb, h, size)
+        kvb_s[h].go()
+    mlp[2].advance()
+    os_s.advance()
+
+    def total_step(i, _):
+        b = jnp.where(i < 2, 2 - 2 * where.core + i, 2 * where.core + i - 2)
+        at = pl.ds(pl.multiple_of(b * blk, blk), blk)
+        total = dot_nt(al[0, at, :], w[0]) + dot_nt(al[1, at, :], w[1]) + dot(grank[at, :], rd_ref[...])
+        for j in range(2):
+
+            @pl.when(i == j)
+            def _():
+                tb[j] = total.astype(BF16)
+                tots[j].start()
+
+            @pl.when(i == 2 + j)
+            def _():
+                tb[2 + j] = total.astype(BF16)
+
+        return 0
+
+    every.advance()
+    lax.fori_loop(0, 4, total_step, 0)
+
     kvq_step(kva, 0, 0)
     every.advance()
 
@@ -1107,7 +1113,8 @@
     every_n.begin()
 
     kva_y.wait_recv()
-    far[1].start()
+    far[2].start()
+    far[3].start()
     add_row(kva, kvay)
     kva_s.go()
     for part in kvb_s:
@@ -1195,7 +1202,7 @@
         v_((4, half // 2, d), BF16), v_((2, half // 2, d), BF16),
         v_((2, rk, d), F32), v_((rk, d), F32), v_((n_bits + 1, rk, d), F32), v_((n_bits + 1, rk, d), F32), v_((2, rk, d), F32),
         v_((n_bits + 3, 8, d // 8), F32), v_((n_bits + 2, 8, d // 8), F32),
-        dma((24,)), dma((80,)), dma((80,)), dma((1,)),
+        dma((24,)), dma((96,)), dma((96,)), dma((1,)),
     ]
     out_shape = [
         sds((half, d), F32), sds((half, d), BF16), sds((ff, each), F32), sds((ff, each), F32), sds((ff, each), F32), sds((dv, each), F32),

time: 259 us -> 248 us (0.958)
  Pallas kernels: 254 us -> 243 us
    pallas_call x1, Pallas kernels: 106 us -> 95.9 us  [back_phase(): pl.pallas_call(kernel, name='back_phase', in_specs=[hbm] * (n_in - n_vmem...]
where the time goes in v3:
time: 248 us
  Pallas kernels  243 us (98%)
  other arithmetic  2.71 us (1%)
    pallas_call x1, Pallas kernels, back_phase(): pl.pallas_call(kernel, name='back_phase', in_specs=[hbm] * (n_in - n_vmem...  95.9 us
    pallas_call x1, Pallas kernels, mlp_phase(): pl.pallas_call(functools.partial(mlp_phase_kernel, bits), name='mlp_phase...  71.6 us
    pallas_call x1, Pallas kernels, front_phase(): pl.pallas_call(functools.partial(front_phase_kernel, bits), name='front_p...  68.5 us
    pallas_call x1, Pallas kernels, finish(): pl.pallas_call(functools.partial(finish_kernel, len(smalls)), name='finis...  6.89 us

profile of v3, /device:TPU:0, one launch (start us, length us, event | category | flops | bytes accessed | tf_op | source)
XLA Modules:
  0.0 247.7 jit_solution(7235160539977189860)
XLA Ops:
  0.6 0.7 constant_dynamic-update-slice_fusion.4
  1.3 0.7 constant_dynamic-update-slice_fusion.3
  2.0 0.7 constant_dynamic-update-slice_fusion.2
  2.7 0.7 constant_dynamic-update-slice_fusion.1
  4.0 0.6 reshape.38.row_ref.refs_26_
  4.6 68.5 %front_phase.1 = (f32[640,1024]{1,0:T(8,128)}, bf16[1280,1024]{1,0:T(8,128)(2,1)}, bf16[2,1280,128]{2,1,0:T(8,128)(2,1)}, bf16[2,1280,128]{2,1,0:T(8,128)(2,1)},...) custom-call(bf16[640,1024]{1,0:T(8,128)(2,1)} %refs_19_.1, ...), custom_call_target="tpu_custom_call" | custom-call | flops 12000000000 | bytes 60000000 | tf_op jit(solution)/shard_map/front_phase/pallas_call | solution.py:590
  73.1 71.6 %mlp_phase.1 = (f32[640,1024]{1,0:T(8,128)}, bf16[1280,1024]{1,0:T(8,128)(2,1)}, f32[1,1024]{1,0:T(1,128)}, bf16[2,2,128,704]{3,2,1,0:T(8,128)(2,1)}, bf16[2,2,1...) custom-call(f32[640,1024]{1,0:T(8,128)} %get-tuple-element.77.mid_h., ...), custom_call_target="tpu_custom_call" | custom-call | flops 33218887680 | bytes 60000000 | tf_op jit(solution)/shard_map/mlp_phase/pallas_call | solution.py:822
  144.7 95.9 %back_phase.1 = (f32[640,1024]{1,0:T(8,128)}, bf16[640,1024]{1,0:T(8,128)(2,1)}, f32[704,128]{1,0:T(8,128)}, f32[704,128]{1,0:T(8,128)}, f32[704,128]{1,0:T(8,12...) custom-call(bf16[1280,1024]{1,0:T(8,128)(2,1)} %get-tuple-element.82, ...), custom_call_target="tpu_custom_call" | custom-call | flops 40000000000 | bytes 60000000 | tf_op jit(solution)/shard_map/back_phase/pallas_call | solution.py:1226
  240.6 6.9 %finish.1 = (bf16[640,1024]{1,0:T(8,128)(2,1)}, f32[640,1024]{1,0:T(8,128)}, f32[704,128]{1,0:T(8,128)}, f32[704,128]{1,0:T(8,128)}, f32[704,128]{1,0:T(8,128)},...) custom-call(f32[640,1024]{1,0:T(8,128)} %get-tuple-element.77.mid_h., ...), custom_call_target="tpu_custom_call" | custom-call | tf_op jit(solution)/shard_map/finish/pallas_call | solution.py:1254
  (1 shorter events, 0.0 us)

commit v4 on v3

--- a/solution.py
+++ b/solution.py
@@ -326,29 +326,50 @@
     gain = row_ref[:, at_row[2] : at_row[3]]
     restart = row_ref[:, at_row[4] : at_row[4] + dk]
 
-    odd = where.has(1)
-    over_x = where.across(1)
-    quarter = d // 4
-
-    def weight_pieces(cols):
-        made = []
-        for i in range(2):
-            near = pl.ds(pl.multiple_of(odd * 2 * quarter + i * quarter, quarter), quarter)
-            made.append(
-                (
-                    wires.copy(w.at[0, near, cols], w.at[1, near, cols], where.by_row),
-                    wires.copy(w.at[1, near, cols], w.at[1, near, cols], over_x),
-                )
-            )
-        return made
-
-    kv_in = weight_pieces(pl.ds(0, kv))
-    qs_in = weight_pieces(pl.ds(kv, kv))
-    near = pl.ds(pl.multiple_of(odd * (dv // 2), dv // 2), dv // 2)
-    wo_in = [
-        wires.copy(wo.at[0, near], wo.at[1, near], where.by_row),
-        wires.copy(wo.at[1, near], wo.at[1, near], over_x),
-    ]
+    first_bit, second_bit = where.bits[0], where.bits[1]
+    over_a, over_b = where.across(first_bit), where.across(second_bit)
+    spot_a, spot_b = where.has(first_bit), where.has(second_bit)
+
+    class Quarters:
+        def __init__(self, ref, cols):
+            quarter = ref.shape[1] // 4
+
+            def part(of_a, of_b, low, size):
+                at = pl.ds(pl.multiple_of((of_a + 2 * of_b) * quarter + low, size), size)
+                return (at,) if cols is None else (at, cols)
+
+            mine = part(spot_a, spot_b, 0, quarter)
+            from_a = part(1 - spot_a, spot_b, 0, quarter // 2)
+            from_b = part(spot_a, 1 - spot_b, quarter // 2, quarter // 2)
+            got = ref.at[(1,) + mine]
+            self.row = wires.copy(ref.at[(0,) + mine], got, where.by_row)
+            self.near = [wires.copy(got, got, over_a), wires.copy(got, got, over_b)]
+            self.far = [
+                wires.copy(ref.at[(1,) + from_a], ref.at[(1,) + from_a], over_b),
+                wires.copy(ref.at[(1,) + from_b], ref.at[(1,) + from_b], over_a),
+            ]
+
+        def start(self):
+            self.row.start()
+
+        def relay(self):
+            self.row.wait_recv()
+            for copy in self.near:
+                copy.start()
+
+        def forward(self):
+            for copy in self.near:
+                copy.wait_recv()
+            for copy in self.far:
+                copy.start()
+
+        def done(self):
+            for copy in self.far:
+                copy.wait_recv()
+
+    kv_in = Quarters(w, pl.ds(0, kv))
+    qs_in = Quarters(w, pl.ds(kv, kv))
+    wo_in = Quarters(wo, None)
     cot_row, cot_both = [], []
     for i in range(2):
         at = pl.ds(i * blk, blk)
@@ -364,8 +385,7 @@
 
     for copy in load_kv:
         copy.wait()
-    for piece in kv_in:
-        piece[0].start()
+    kv_in.start()
     load_tok.wait()
     for i in range(2):
         x = tok[pl.ds(i * blk, blk), :].astype(F32)
@@ -374,7 +394,9 @@
         row_out[i].start()
     for copy in load_qs:
         copy.wait()
+    qs_in.start()
     load_wo.wait()
+    wo_in.start()
     for copy in row_out:
         copy.wait_recv()
     cot_core.start()
@@ -386,31 +408,18 @@
     blocks = count // BLOCK
     per = BLOCK // CHUNK
 
-    def first_step(i, _):
-        h, b = i // blocks, i % blocks
+    def first_step(h, i, _):
+        b = i
         at = pl.ds(pl.multiple_of(b * BLOCK, BLOCK), BLOCK)
-        for p in range(2):
-
-            @pl.when(i == blocks - 2 + p)
+        if h == 0:
+
+            @pl.when(i == 2)
             def _():
-                kv_in[p][0].wait_recv()
-                kv_in[p][1].start()
-
-            @pl.when(i == 2 * blocks - 2 + p)
+                kv_in.relay()
+
+            @pl.when(i == blocks - 1)
             def _():
-                qs_in[p][0].wait_recv()
-                qs_in[p][1].start()
-
-        @pl.when(i == blocks - 1)
-        def _():
-            for piece in qs_in:
-                piece[0].start()
-            cot_row[0].start()
-
-        @pl.when(i == blocks)
-        def _():
-            for piece in kv_in:
-                piece[1].wait_recv()
+                qs_in.relay()
 
         @pl.when(b == 0)
         def _():
@@ -419,8 +428,7 @@
 
         x = rows[at, :]
 
-        @pl.when(i < blocks)
-        def _():
+        if h == 0:
             rank[at, :] = dot_nt(x, rd_ref[...])
 
         proj = dot(x, w[h, :, :kv])
@@ -457,33 +465,9 @@
 
         return 0
 
-    lax.fori_loop(0, 2 * blocks, first_step, 0)
-    scan.begin()
-    wo_in[0].start()
-    cot_row[1].start()
-    for src, dst in ((k, k_h), (v, v_h), (cum, cum_h), (dpre, dpre_h), (rank, rank_h), (sin, sin_h)):
-        store(src, dst)
-
-    def second_step(i, _):
-        h, b = i // blocks, i % blocks
+    def second_step(h, i, _):
+        b = i
         at = pl.ds(pl.multiple_of(b * BLOCK, BLOCK), BLOCK)
-
-        @pl.when(i == blocks)
-        def _():
-            for piece in qs_in:
-                piece[1].wait_recv()
-
-        for n in range(min(len(bits), 3)):
-
-            @pl.when(i == 2 + 3 * n)
-            def _():
-                scan.advance()
-
-        @pl.when(i == 2 * blocks - 1)
-        def _():
-            wo_in[0].wait_recv()
-            wo_in[1].start()
-
         proj = dot(rows[at, :], w[h, :, kv:])
         q_low = proj[:, :dk].astype(BF16)
         q[h, at, :] = q_low
@@ -504,14 +488,28 @@
             reach[h, this, :] = (qf * jnp.exp(ch + off_o[h, c])).astype(BF16)
         return 0
 
-    lax.fori_loop(0, 2 * blocks, second_step, 0)
+    lax.fori_loop(0, blocks, functools.partial(first_step, 0), 0)
+    kv_in.forward()
+    cot_row[0].start()
+    lax.fori_loop(0, blocks, functools.partial(second_step, 0), 0)
+    kv_in.done()
+    qs_in.forward()
+    wo_in.relay()
+    lax.fori_loop(0, blocks, functools.partial(first_step, 1), 0)
+    scan.begin()
+    cot_row[1].start()
+    for src, dst in ((k, k_h), (v, v_h), (cum, cum_h), (dpre, dpre_h), (rank, rank_h), (sin, sin_h)):
+        store(src, dst)
+    qs_in.done()
+    wo_in.forward()
+    lax.fori_loop(0, blocks, functools.partial(second_step, 1), 0)
     for src, dst in ((q, q_h), (sw, s_h), (reach, reach_h), (w, w_h)):
         store(src, dst)
     while scan.advance():
         pass
     for h in range(2):
         enter_o[h] = restart * pre_s[h]
-    wo_in[1].wait_recv()
+    wo_in.done()
     store(wo, wo2_h)
 
     def gate_step(i, _):

time: 248 us -> 243 us (0.980)
  Pallas kernels: 243 us -> 237 us
    pallas_call x1, Pallas kernels: 68.5 us -> 57.5 us  [front_phase(): pl.pallas_call(functools.partial(front_phase_kernel, bits), name='front_p...]
    pallas_call x1, Pallas kernels: 95.9 us -> 101 us  [back_phase(): pl.pallas_call(kernel, name='back_phase', in_specs=[hbm] * (n_in - n_vmem...]
where the time goes in v4:
time: 243 us; the launch traced here: 242 us
  Pallas kernels  237 us (98%)
  other arithmetic  2.71 us (1%)
    pallas_call x1, Pallas kernels, back_phase(): pl.pallas_call(kernel, name='back_phase', in_specs=[hbm] * (n_in - n_vmem...  101 us
    pallas_call x1, Pallas kernels, mlp_phase(): pl.pallas_call(functools.partial(mlp_phase_kernel, bits), name='mlp_phase...  72.5 us
    pallas_call x1, Pallas kernels, front_phase(): pl.pallas_call(functools.partial(front_phase_kernel, bits), name='front_p...  57.5 us
    pallas_call x1, Pallas kernels, finish(): pl.pallas_call(functools.partial(finish_kernel, len(smalls)), name='finis...  6.89 us

profile of v4, /device:TPU:0, one launch (start us, length us, event | category | flops | bytes accessed | tf_op | source)
XLA Modules:
  0.0 242.3 jit_solution(4728698574418104195)
XLA Ops:
  0.6 0.7 constant_dynamic-update-slice_fusion.4
  1.3 0.7 constant_dynamic-update-slice_fusion.3
  2.0 0.7 constant_dynamic-update-slice_fusion.2
  2.7 0.7 constant_dynamic-update-slice_fusion.1
  4.0 0.6 reshape.38.row_ref.refs_26_
  4.6 57.5 %front_phase.1 = (f32[640,1024]{1,0:T(8,128)}, bf16[1280,1024]{1,0:T(8,128)(2,1)}, bf16[2,1280,128]{2,1,0:T(8,128)(2,1)}, bf16[2,1280,128]{2,1,0:T(8,128)(2,1)},...) custom-call(bf16[640,1024]{1,0:T(8,128)(2,1)} %refs_19_.1, ...), custom_call_target="tpu_custom_call" | custom-call | flops 12000000000 | bytes 60000000 | tf_op jit(solution)/shard_map/front_phase/pallas_call | solution.py:588
  62.1 72.5 %mlp_phase.1 = (f32[640,1024]{1,0:T(8,128)}, bf16[1280,1024]{1,0:T(8,128)(2,1)}, f32[1,1024]{1,0:T(1,128)}, bf16[2,2,128,704]{3,2,1,0:T(8,128)(2,1)}, bf16[2,2,1...) custom-call(f32[640,1024]{1,0:T(8,128)} %get-tuple-element.77.mid_h., ...), custom_call_target="tpu_custom_call" | custom-call | flops 33218887680 | bytes 60000000 | tf_op jit(solution)/shard_map/mlp_phase/pallas_call | solution.py:820
  134.6 100.6 %back_phase.1 = (f32[640,1024]{1,0:T(8,128)}, bf16[640,1024]{1,0:T(8,128)(2,1)}, f32[704,128]{1,0:T(8,128)}, f32[704,128]{1,0:T(8,128)}, f32[704,128]{1,0:T(8,12...) custom-call(bf16[1280,1024]{1,0:T(8,128)(2,1)} %get-tuple-element.82, ...), custom_call_target="tpu_custom_call" | custom-call | flops 40000000000 | bytes 60000000 | tf_op jit(solution)/shard_map/back_phase/pallas_call | solution.py:1224
  235.2 6.9 %finish.1 = (bf16[640,1024]{1,0:T(8,128)(2,1)}, f32[640,1024]{1,0:T(8,128)}, f32[704,128]{1,0:T(8,128)}, f32[704,128]{1,0:T(8,128)}, f32[704,128]{1,0:T(8,128)},...) custom-call(f32[640,1024]{1,0:T(8,128)} %get-tuple-element.77.mid_h., ...), custom_call_target="tpu_custom_call" | custom-call | tf_op jit(solution)/shard_map/finish/pallas_call | solution.py:1252
  (1 shorter events, 0.0 us)

commit v5 on v4

--- a/solution.py
+++ b/solution.py
@@ -673,7 +673,7 @@
         xs[rows_of(j), :] = (m * inv * gain).astype(BF16)
         x_row[j].start()
         x_core[j].start()
-    for load in loads[1:]:
+    for load in loads[1:6]:
         load.wait()
 
     def step(s, _):
@@ -682,6 +682,8 @@
 
         @pl.when(s == 2)
         def _():
+            for load in loads[6:]:
+                load.wait()
             x_core[0].wait_recv()
 
         @pl.when(s == 3)
@@ -1246,13 +1248,13 @@
 
 def finish(middle, near, far, grad, smalls):
     rows, d = middle.shape
-    blk = rows // 4
+    blk = rows // 2
     row = rows_spec(blk, d)
     wholes = [pl.BlockSpec(v.shape, lambda i: (0, 0)) for v in smalls]
     return pl.pallas_call(
         functools.partial(finish_kernel, len(smalls)),
         name="finish",
-        grid=(4,),
+        grid=(2,),
         in_specs=[row] * 4 + wholes,
         out_specs=[row] * 2 + wholes,
         out_shape=[sds((rows, d), BF16), sds((rows, d), F32)] + [sds(v.shape, v.dtype) for v in smalls],
@@ -1276,7 +1278,12 @@
     dk, dv, d = query_weight.shape[1], value_weight.shape[1], tokens.shape[1]
     restart = jnp.where((place & 2) != 0, 1.0, 1.0 - flags[0].astype(F32))
     parts = [part.astype(F32) for part in (norm_gain, mlp_gain, group_gain, decay_bias)]
-    row = jnp.concatenate(parts + [jnp.full((dk,), restart, F32)]).reshape(1, -1)
+    parts.append(jnp.full((dk,), restart, F32))
+    total, at = sum(part.size for part in parts), 0
+    row = jnp.zeros((1, total), F32)
+    for part in parts:
+        row = row + jnp.pad(part.reshape(1, -1), ((0, 0), (at, total - at - part.size)))
+        at += part.size
     rd = rank_down.T
     (
         middle, rows_all, q, k, v, s, cum, dpre, rank_pre, reach, sin, mixed, gated, w, weights_out, cot_c, cot_y, cot_d,

time: 243 us -> 240 us (0.988)
  Pallas kernels: 237 us -> 232 us
    pallas_call x1, Pallas kernels: 101 us -> 96.8 us  [back_phase(): pl.pallas_call(kernel, name='back_phase', in_specs=[hbm] * (n_in - n_vmem...]
    unnamed x4 -> x0, other arithmetic: 2.71 us -> none
where the time goes in v5:
time: 240 us; the launch traced here: 237 us
  Pallas kernels  232 us (97%)
  local copies, waits for them, and re-layouts  2.72 us (1%)
    pallas_call x1, Pallas kernels, back_phase(): pl.pallas_call(kernel, name='back_phase', in_specs=[hbm] * (n_in - n_vmem...  96.8 us
    pallas_call x1, Pallas kernels, mlp_phase(): pl.pallas_call(functools.partial(mlp_phase_kernel, bits), name='mlp_phase...  71.9 us
    pallas_call x1, Pallas kernels, front_phase(): pl.pallas_call(functools.partial(front_phase_kernel, bits), name='front_p...  57.5 us
    pallas_call x1, Pallas kernels, finish(): pl.pallas_call(functools.partial(finish_kernel, len(smalls)), name='finis...  5.99 us

profile of v5, /device:TPU:0, one launch (start us, length us, event | category | flops | bytes accessed | tf_op | source)
XLA Modules:
  0.0 237.0 jit_solution(12099165123901591236)
XLA Ops:
  1.3 0.7 reshape.58
  2.0 0.7 reshape.57
  2.7 0.7 reshape.56
  3.4 0.7 reshape.55
  4.0 0.6 reshape_add_fusion.row_ref.refs_26_
  4.7 57.5 %front_phase.1 = (f32[640,1024]{1,0:T(8,128)}, bf16[1280,1024]{1,0:T(8,128)(2,1)}, bf16[2,1280,128]{2,1,0:T(8,128)(2,1)}, bf16[2,1280,128]{2,1,0:T(8,128)(2,1)},...) custom-call(bf16[640,1024]{1,0:T(8,128)(2,1)} %refs_19_.1, ...), custom_call_target="tpu_custom_call" | custom-call | flops 12000000000 | bytes 60000000 | tf_op jit(solution)/shard_map/front_phase/pallas_call | solution.py:588
  62.1 71.9 %mlp_phase.1 = (f32[640,1024]{1,0:T(8,128)}, bf16[1280,1024]{1,0:T(8,128)(2,1)}, f32[1,1024]{1,0:T(1,128)}, bf16[2,2,128,704]{3,2,1,0:T(8,128)(2,1)}, bf16[2,2,1...) custom-call(f32[640,1024]{1,0:T(8,128)} %get-tuple-element.77.mid_h., ...), custom_call_target="tpu_custom_call" | custom-call | flops 33218887680 | bytes 60000000 | tf_op jit(solution)/shard_map/mlp_phase/pallas_call | solution.py:822
  134.1 96.8 %back_phase.1 = (f32[640,1024]{1,0:T(8,128)}, bf16[640,1024]{1,0:T(8,128)(2,1)}, f32[704,128]{1,0:T(8,128)}, f32[704,128]{1,0:T(8,128)}, f32[704,128]{1,0:T(8,12...) custom-call(bf16[1280,1024]{1,0:T(8,128)(2,1)} %get-tuple-element.82, ...), custom_call_target="tpu_custom_call" | custom-call | flops 40000000000 | bytes 60000000 | tf_op jit(solution)/shard_map/back_phase/pallas_call | solution.py:1226
  230.8 6.0 %finish.1 = (bf16[640,1024]{1,0:T(8,128)(2,1)}, f32[640,1024]{1,0:T(8,128)}, f32[704,128]{1,0:T(8,128)}, f32[704,128]{1,0:T(8,128)}, f32[704,128]{1,0:T(8,128)},...) custom-call(f32[640,1024]{1,0:T(8,128)} %get-tuple-element.77.mid_h., ...), custom_call_target="tpu_custom_call" | custom-call | tf_op jit(solution)/shard_map/finish/pallas_call | solution.py:1254
  (2 shorter events, 0.0 us)
